TPU v7x, 512 devices: a whole 4x4x16 slice. The times are simulated.
512 devices in a mesh: grp: 16 (over x, y), mlp: 32 (over z, core).
Axes of the slice: x: 4, y: 4, z: 16, core: 2. Of those that a mesh axis runs over, the one named last changes fastest.
Arguments:
- queries: bfloat16 [65536, 4096], P(('grp', 'mlp')), may hold values from -8 to 8
- keys: bfloat16 [65536, 4096], P(('grp', 'mlp')), may hold values from -8 to 8
- values: bfloat16 [65536, 4096], P(('grp', 'mlp')), may hold values from -6 to 6
- gamma: bfloat16 [4096], P('mlp'), may hold values from 0.25 to 2
- w_merge: bfloat16 [4096, 4096], P('grp', 'mlp'), may hold values from -0.09375 to 0.09375
- grids: int32 [256, 2], P('grp'), may hold values from 8 to 16, as said below
- positions: int32 [16384], replicated, may hold values from 0 to 16383, as said below
Outputs:
- prompt_embeds: bfloat16 [16384, 4096], P('grp', 'mlp')
Inputs may be any that keep to these rules, and one draw needn't show every extreme that they name: `grids`: every grid side is even and at least 8; each group has an image of 16 x 16, and a group's images fill at most 4096 slots. positions is a permutation. From one group's 1024 slots at most 128 go to one block of 1024 consecutive prompt positions, and exactly 128 go to some block.
All inputs are finite; a program needn't handle non-finite values.
Results may differ from a plain program's by a relative error of at most 0.015.
Values may be sent and summed in bfloat16 or wider, within the bound.
No kernel may reach another device: no remote copies, remote signals or barrier semaphores. Data moves between devices by JAX's collectives and lax.ppermute only.
A program may use at most 64 MiB of HBM per device.

v0:
```python
import jax
import jax.numpy as jnp
from jax import lax
from jax.sharding import PartitionSpec as P

HD = 128
GRID = 16


def token_layout(grid, gtok):
    heights = grid[:, 0]
    widths = grid[:, 1]
    areas = heights * widths
    ends = jnp.cumsum(areas)
    starts = ends - areas
    count = grid.shape[0]
    slots = jnp.arange(gtok, dtype=jnp.int32)
    image = jnp.sum((slots[:, None] >= ends[None, :]).astype(jnp.int32), axis=1)
    starts_ext = jnp.concatenate([starts, ends[-1:]])
    widths_ext = jnp.concatenate([widths, jnp.full((1,), 2, jnp.int32)])
    onehot = (image[:, None] == jnp.arange(count + 1, dtype=jnp.int32)[None, :]).astype(jnp.int32)
    first = jnp.sum(onehot * starts_ext[None, :], axis=1)
    width = jnp.sum(onehot * widths_ext[None, :], axis=1)
    local = slots - first
    return (image, local // width, local % width)


def pool_layout(grid, gpool):
    heights = grid[:, 0]
    widths = grid[:, 1]
    areas = heights * widths
    ends = jnp.cumsum(areas)
    starts = ends - areas
    count = grid.shape[0]
    slots = jnp.arange(gpool, dtype=jnp.int32)
    image = jnp.sum((slots[:, None] >= (ends // 4)[None, :]).astype(jnp.int32), axis=1)
    starts_ext = jnp.concatenate([starts, ends[-1:]])
    widths_ext = jnp.concatenate([widths, jnp.full((1,), 2, jnp.int32)])
    onehot = (image[:, None] == jnp.arange(count + 1, dtype=jnp.int32)[None, :]).astype(jnp.int32)
    first = jnp.sum(onehot * starts_ext[None, :], axis=1)
    width = jnp.sum(onehot * widths_ext[None, :], axis=1)
    local = slots - first // 4
    half = width // 2
    anchor = first + 2 * (local // half) * width + 2 * (local % half)
    sources = jnp.stack([anchor, anchor + 1, anchor + width, anchor + width + 1], axis=1)
    sources = jnp.clip(sources, 0, 4 * gpool - 1)
    return (sources, image < count)


def rotate(block, row, col):
    quarter = block.shape[2] // 4
    freq = 100.0 ** (-jnp.arange(quarter, dtype=jnp.float32) / quarter)
    ang_row = row.astype(jnp.float32)[:, None, None] * freq[None, None, :]
    ang_col = col.astype(jnp.float32)[:, None, None] * freq[None, None, :]
    full = block.astype(jnp.float32)
    first = full[..., :quarter]
    second = full[..., quarter : 2 * quarter]
    third = full[..., 2 * quarter : 3 * quarter]
    fourth = full[..., 3 * quarter :]
    out = jnp.concatenate(
        [
            first * jnp.cos(ang_row) - second * jnp.sin(ang_row),
            second * jnp.cos(ang_row) + first * jnp.sin(ang_row),
            third * jnp.cos(ang_col) - fourth * jnp.sin(ang_col),
            fourth * jnp.cos(ang_col) + third * jnp.sin(ang_col),
        ],
        axis=-1,
    )
    return out.astype(jnp.bfloat16)


def attend(rot_q, rot_k, vals, image, qrows, margin):
    gtok = rot_q.shape[0]
    scale = rot_q.shape[2] ** (-0.5)
    pad_k = jnp.pad(rot_k, ((margin, margin), (0, 0), (0, 0)))
    pad_v = jnp.pad(vals, ((margin, margin), (0, 0), (0, 0)))
    pad_id = jnp.pad(image, (margin, margin), constant_values=-1)

    def block(index):
        start = index * qrows
        q_blk = lax.dynamic_slice_in_dim(rot_q, start, qrows, 0)
        k_blk = lax.dynamic_slice_in_dim(pad_k, start, qrows + 2 * margin, 0)
        v_blk = lax.dynamic_slice_in_dim(pad_v, start, qrows + 2 * margin, 0)
        q_ids = lax.dynamic_slice_in_dim(image, start, qrows, 0)
        k_ids = lax.dynamic_slice_in_dim(pad_id, start, qrows + 2 * margin, 0)
        scores = (
            jnp.einsum("qhd,khd->hqk", q_blk, k_blk, preferred_element_type=jnp.float32) * scale
        )
        keep = q_ids[:, None] == k_ids[None, :]
        scores = jnp.where(keep[None, :, :], scores, -1e30)
        top = jnp.max(scores, axis=-1, keepdims=True)
        expo = jnp.exp(scores - top)
        probs = (expo / jnp.sum(expo, axis=-1, keepdims=True)).astype(jnp.bfloat16)
        return jnp.einsum("hqk,khd->qhd", probs, v_blk, preferred_element_type=jnp.float32)

    outs = lax.map(block, jnp.arange(gtok // qrows, dtype=jnp.int32))
    return outs.reshape(gtok, rot_q.shape[1], rot_q.shape[2])


def body(queries, keys, values, gamma, w_merge, grids, positions):
    head_q, head_k, head_v = (
        lax.all_to_all(queries, "mlp", split_axis=1, concat_axis=0, tiled=True),
        lax.all_to_all(keys, "mlp", split_axis=1, concat_axis=0, tiled=True),
        lax.all_to_all(values, "mlp", split_axis=1, concat_axis=0, tiled=True),
    )
    gtok = head_q.shape[0]
    width_dev = head_q.shape[1]
    heads_dev = width_dev // HD
    gpool = gtok // 4
    image, row, col = token_layout(grids, gtok)
    rot_q = rotate(head_q.reshape(gtok, heads_dev, HD), row, col)
    rot_k = rotate(head_k.reshape(gtok, heads_dev, HD), row, col)
    attn = attend(
        rot_q, rot_k, head_v.reshape(gtok, heads_dev, HD), image, min(512, gtok), GRID * GRID
    )
    gains = gamma.astype(jnp.float32).reshape(heads_dev, HD)
    branch = (attn * gains[None, :, :]).astype(jnp.bfloat16).reshape(gtok, width_dev)
    sources, valid = pool_layout(grids, gpool)
    picked = jnp.take(branch, sources, axis=0).astype(jnp.float32)
    pooled = jnp.where(valid[:, None], 0.25 * jnp.sum(picked, axis=1), 0.0).astype(jnp.bfloat16)
    full_columns = lax.all_gather(w_merge, "grp", axis=0, tiled=True)
    merged = jnp.dot(
        lax.all_gather(pooled, "mlp", axis=1, tiled=True),
        full_columns,
        preferred_element_type=jnp.float32,
    ).astype(jnp.bfloat16)
    group = lax.axis_index("grp")
    prompt = positions.shape[0]
    source_of = (
        jnp.zeros((prompt,), jnp.int32).at[positions].set(jnp.arange(prompt, dtype=jnp.int32))
    )
    mine = lax.dynamic_slice_in_dim(source_of, group * gpool, gpool, 0)
    everything = lax.all_gather(merged, "grp", axis=0, tiled=True)
    placed = jnp.take(everything, mine, axis=0)
    return placed


def solution(mesh):
    return jax.shard_map(
        body,
        mesh=mesh,
        in_specs=(
            P(("grp", "mlp"), None),
            P(("grp", "mlp"), None),
            P(("grp", "mlp"), None),
            P("mlp"),
            P("grp", "mlp"),
            P("grp", None),
            P(),
        ),
        out_specs=P("grp", "mlp"),
        check_vma=False,
    )
```

profile of v0, /device:TPU:1, one launch (start us, length us, event | category | flops | bytes accessed | tf_op | source)
XLA Modules:
  0.0 445.1 jit_solution(18084548913521165497)
XLA Ops:
  6.5 2.4 copy.48
  8.9 16.7 %all-to-all-start.1 = ((bf16[128,32,128]{0,2,1:T(8,128)(2,1)}), bf16[128,32,128]{0,2,1:T(8,128)(2,1)S(1)}, u32[]{:S(2)}, u32[]{:S(2)}) async-start(bf16[128,32,128]{0,2,1:T(8,128)(2,1)} %bitcast.15), calls=%async_computation.1 | async-start | bytes 2097152 | tf_op jit(solution)/shard_map/all_to_all | solution.py:102
  27.0 54.4 %all-to-all-done.1 = bf16[128,32,128]{0,2,1:T(8,128)(2,1)S(1)} async-done(((bf16[128,32,128]{0,2,1:T(8,128)(2,1)}), bf16[128,32,128]{0,2,1:T(8,128)(2,1)S(1)}, u32[]{:S(2)}, u32[]{:S(2)}) %all-to-all-start.1) | async-done | bytes 1048608 | tf_op jit(solution)/shard_map/all_to_all | solution.py:102
  81.4 4.1 all-to-all-start.2
  86.9 54.4 %all-to-all-done.2 = bf16[128,32,128]{0,2,1:T(8,128)(2,1)S(1)} async-done(((bf16[128,32,128]{0,2,1:T(8,128)(2,1)}), bf16[128,32,128]{0,2,1:T(8,128)(2,1)S(1)}, u32[]{:S(2)}, u32[]{:S(2)}) %all-to-all-start.2) | async-done | bytes 1048608 | tf_op jit(solution)/shard_map/all_to_all | solution.py:103
  141.3 5.3 %all-to-all-start = ((bf16[128,32,128]{0,2,1:T(8,128)(2,1)}), bf16[128,32,128]{0,2,1:T(8,128)(2,1)}, u32[]{:S(2)}, u32[]{:S(2)}) async-start(bf16[128,32,128]{0,2,1:T(8,128)(2,1)} %bitcast.12), calls=%async_computation | async-start | bytes 2097152 | tf_op jit(solution)/shard_map/all_to_all | solution.py:104
  151.9 2.5 copy.49
  154.4 1.7 reshape.802
  156.4 2.6 copy.51
  158.9 2.7 reshape.803
  161.6 40.8 %all-to-all-done = bf16[128,32,128]{0,2,1:T(8,128)(2,1)} async-done(((bf16[128,32,128]{0,2,1:T(8,128)(2,1)}), bf16[128,32,128]{0,2,1:T(8,128)(2,1)}, u32[]{:S(2)}, u32[]{:S(2)}) %all-to-all-start) | async-done | bytes 1048608 | tf_op jit(solution)/shard_map/all_to_all | solution.py:104
  206.1 4.5 %fusion.31 = (bf16[4096,1,32]{0,2,1:T(8,128)(2,1)S(1)}, bf16[4096,1,32]{0,2,1:T(8,128)(2,1)S(1)}, bf16[4096,1,32]{0,2,1:T(8,128)(2,1)S(1)}, bf16[4096,1,32]{0,2,...) fusion(f32[4096,1,128]{0,2,1:T(8,128)S(1)} %reshape.802, ...), kind=kLoop, calls=%fused_computation.53 | loop fusion | flops 4456448 | bytes 6324352 | tf_op jit(solution)/shard_map/convert.8
  212.8 42.0 %while.10 = (s32[]{:T(128)}, f32[8,512,1,128]{3,1,0,2:T(8,128)S(1)}, s32[8]{0:T(128)S(1)}, bf16[4608,1,128]{2,0,1:T(8,128)(2,1)}, s32[4096]{0:T(1024)S(1)}, /*in...) while((s32[]{:T(128)}, ...), condition=%wide.region_11.12_spmd, body=%wide.region_8.11_spmd.sunk | while | flops 273153024 | bytes 8286440 | solution.py:96
  216.2 1.6 convolution_bitcast_fusion.2
  232.0 1.6 convolution_bitcast_fusion.2
  237.3 1.6 convolution_bitcast_fusion.2
  253.0 1.6 convolution_bitcast_fusion.2
  255.0 12.1 %gather_fusion = bf16[4096,128]{1,0:T(8,128)(2,1)S(1)} fusion(bf16[4096,128]{1,0:T(8,128)(2,1)S(1)} %fusion.10, s32[4096]{0:T(1024)S(1)} %broadcast_clamp_fusion), kind=kCustom, calls=%fused_computation | custom fusion | bytes 2113536 | tf_op jit(solution)/shard_map/jit(_take)/gather | solution.py:119
  267.1 5.8 %convert_reduce_fusion = f32[1024,128]{1,0:T(8,128)S(1)} fusion(bf16[1024,4,128]{2,1,0:T(4,128)(2,1)S(1)} %bitcast.71, pred[1024,4]{1,0:T(8,128)(4,1)S(1)} %copy.45), kind=kLoop, calls=%fused_computation.24 | loop fusion | flops 1441792 | bytes 1576960 | tf_op jit(solution)/shard_map/reduce_sum | solution.py:120
  274.2 88.9 %all-gather.4.cloned.1.call-done = bf16[1024,4096]{1,0:T(8,128)(2,1)} async-done(((bf16[1024,128]{1,0:T(8,128)(2,1)}), bf16[1024,4096]{1,0:T(8,128)(2,1)}) %all-gather.4.cloned.1.call-update) | async-done | bytes 8388624 | tf_op jit(solution)/shard_map/all_gather | solution.py:123
  363.1 6.6 %convolution_convert_fusion = bf16[1024,128]{1,0:T(8,128)(2,1)} fusion(bf16[1024,4096]{1,0:T(8,128)(2,1)} %all-gather.4.cloned.1.call-done, bf16[4096,128]{1,0:T(8,128)(2,1)} %all-gather.6.cloned.1.call-done), kind=kOutput, calls=%fused_computation.25 | convolution fusion | flops 1073872896 | bytes 9699328 | tf_op jit(solution)/shard_map/dot_general | solution.py:122
  369.8 60.3 %scatter_custom_fusion = s32[16384]{0:T(1024)S(1)} fusion(s32[16384]{0:T(1024)S(1)} %compare_select_fusion, s32[16384]{0:T(1024)S(1)} %iota.40, s32[]{:T(128)} %constant.124.clone.1), kind=kCustom, calls=%fused_computation.84 | custom fusion | bytes 65540 | tf_op jit(solution)/shard_map/scatter | solution.py:130
  430.2 1.8 all-gather.8.cloned.1.call-done
  432.0 5.6 %gather_fusion.1 = bf16[1024,128]{1,0:T(8,128)(2,1)S(1)} fusion(bf16[16384,128]{1,0:T(8,128)(2,1)} %all-gather.8.cloned.1.call-done, s32[1024]{0:T(1024)S(1)} %fusion.52), kind=kCustom, calls=%fused_computation.1 | custom fusion | bytes 528384 | tf_op jit(solution)/shard_map/jit(_take)/gather | solution.py:134
  (123 shorter events, 46.8 us)
Async XLA Ops:
  6.5 19.1 %copy-start.2 = (bf16[128,4096]{1,0:T(8,128)(2,1)S(1)}, bf16[128,4096]{1,0:T(8,128)(2,1)}, u32[]{:S(2)}) copy-start(bf16[128,4096]{1,0:T(8,128)(2,1)} %param.10) | copy-start | bytes 3145732
  8.9 72.5 %all-to-all-start.1 = ((bf16[128,32,128]{0,2,1:T(8,128)(2,1)}), bf16[128,32,128]{0,2,1:T(8,128)(2,1)S(1)}, u32[]{:S(2)}, u32[]{:S(2)}) async-start(bf16[128,32,128]{0,2,1:T(8,128)(2,1)} %bitcast.15), calls=%async_computation.1 | async-start | bytes 2097152 | tf_op jit(solution)/shard_map/all_to_all | solution.py:102
  27.0 58.5 %copy-start.3 = (bf16[128,4096]{1,0:T(8,128)(2,1)S(1)}, bf16[128,4096]{1,0:T(8,128)(2,1)}, u32[]{:S(2)}) copy-start(bf16[128,4096]{1,0:T(8,128)(2,1)} %param.11) | copy-start | bytes 3145732
  81.4 59.9 %all-to-all-start.2 = ((bf16[128,32,128]{0,2,1:T(8,128)(2,1)}), bf16[128,32,128]{0,2,1:T(8,128)(2,1)S(1)}, u32[]{:S(2)}, u32[]{:S(2)}) async-start(bf16[128,32,128]{0,2,1:T(8,128)(2,1)} %bitcast.17), calls=%async_computation.2 | async-start | bytes 2097152 | tf_op jit(solution)/shard_map/all_to_all | solution.py:103
  85.5 62.1 %copy-start.5 = (s32[16,2]{0,1:T(2,128)S(1)}, s32[16,2]{0,1:T(2,128)}, u32[]{:S(2)}) copy-start(s32[16,2]{0,1:T(2,128)} %param.14) | copy-start | bytes 388
  85.5 62.8 %copy-start.6 = (bf16[128]{0:T(256)(128)(2,1)S(1)}, bf16[128]{0:T(256)(128)(2,1)}, u32[]{:S(2)}) copy-start(bf16[128]{0:T(256)(128)(2,1)} %param.12) | copy-start | bytes 772
  141.3 61.2 %all-to-all-start = ((bf16[128,32,128]{0,2,1:T(8,128)(2,1)}), bf16[128,32,128]{0,2,1:T(8,128)(2,1)}, u32[]{:S(2)}, u32[]{:S(2)}) async-start(bf16[128,32,128]{0,2,1:T(8,128)(2,1)} %bitcast.12), calls=%async_computation | async-start | bytes 2097152 | tf_op jit(solution)/shard_map/all_to_all | solution.py:104
  146.6 127.6 %all-gather.6.cloned.1.call-start = ((), (), s32[]{:S(2)}) async-start(), calls=%async_computation.4 | async-start | bytes 1114112 | tf_op jit(solution)/shard_map/all_gather | solution.py:121
  147.3 215.8 %all-gather.4.cloned.1.call-start = ((), (), s32[]{:S(2)}) async-start(), calls=%async_computation.3 | async-start | bytes 8650752 | tf_op jit(solution)/shard_map/all_gather | solution.py:123
  204.1 2.0 copy-start
  210.6 2.2 copy-start.1
  273.9 95.9 %copy-start.4 = (s32[16384]{0:T(1024)S(1)}, s32[16384]{0:T(1024)}, u32[]{:S(2)}) copy-start(s32[16384]{0:T(1024)} %param.15) | copy-start | bytes 196612
  273.9 158.1 %all-gather.8.cloned.1.call-start = ((), (), s32[]{:S(2)}) async-start(), calls=%async_computation.5 | async-start | bytes 4456448 | tf_op jit(solution)/shard_map/all_gather | solution.py:133
Sparse Core Ops, SparseCore 0:
  150.4 57.3 all-gather.5
  274.0 89.0 all-gather.3
  369.9 62.0 all-gather.7
where the time goes:
time: 446 us; the launch traced here: 445 us
  waiting for transfers between devices  241 us (54%)
  local copies, waits for them, and re-layouts  105 us (24%)
  matrix products  32.6 us (7%)
  starting transfers between devices  26.6 us (6%)
  other arithmetic  21.6 us (5%)
  between operations  13.4 us (3%)
  loops' own time  4.91 us (1%)
    all_gather x1, waiting for transfers between devices, body(): lax.all_gather(pooled, 'mlp', axis=1, tiled=True)  88.9 us
    scatter x1, local copies, waits for them, and re-layouts, body(): jnp.zeros((prompt,), jnp.int32).at[positions]  60.3 us
    all_to_all x1, waiting for transfers between devices, body(): lax.all_to_all(keys, 'mlp', split_axis=1, concat_axis=0, tiled=True)  54.4 us
    all_to_all x1, waiting for transfers between devices, body(): lax.all_to_all(queries, 'mlp', split_axis=1, concat_axis=0, tiled=True)  54.4 us
    all_to_all x1, waiting for transfers between devices, body(): lax.all_to_all(values, 'mlp', split_axis=1, concat_axis=0, tiled=True)  40.8 us
    all_to_all x1, starting transfers between devices, body(): lax.all_to_all(queries, 'mlp', split_axis=1, concat_axis=0, tiled=True)  16.7 us
    dot_general x8, matrix products, block(): jnp.einsum('hqk,khd->qhd', probs, v_blk, preferred_element_type=jnp.float32)  13.1 us
    dot_general x8, matrix products, block(): jnp.einsum('qhd,khd->hqk', q_blk, k_blk, preferred_element_type=jnp.float32)  12.8 us
  transfers between devices with their start and end apart: 6, of which 5 were waited for; matrix products, arithmetic and copies ran while one was open for 32% of the time, Pallas kernels for 0%

commit v1 on v0

v1 whole, which is shorter than its diff:
```python
import functools
import math

import jax
import jax.numpy as jnp
from jax import lax
from jax.experimental import pallas as pl
from jax.experimental.pallas import tpu as pltpu
from jax.sharding import PartitionSpec as P

HD = 128
HALF = 2048
IMGS = 16
BLK = 128
CHIPS = 16
NB = 4
ROWS = 64
CAP = 128
GROUPS = 16
GPOOL = 1024
NEG = -1e30
F32 = jnp.float32
BF16 = jnp.bfloat16
I32 = jnp.int32


def at(z, c):
    return (z % CHIPS) * 2 + c


SAME = [(at(z, 0), at(z - 1, 0)) for z in range(CHIPS)] + [(at(z, 1), at(z + 1, 1)) for z in range(CHIPS)]
OPP = [(at(z, 1), at(z - 1, 0)) for z in range(CHIPS)] + [(at(z, 0), at(z + 1, 1)) for z in range(CHIPS)]
RING = [(at(z, 0), at(z + 1, 0)) for z in range(CHIPS)] + [(at(z, 1), at(z - 1, 1)) for z in range(CHIPS)]
PART = [(at(z, c), at(z, 1 - c)) for z in range(CHIPS) for c in range(2)]


def vmem():
    return pl.BlockSpec(memory_space=pltpu.VMEM)


def smem():
    return pl.BlockSpec(memory_space=pltpu.SMEM)


def params(mib):
    return pltpu.CompilerParams(vmem_limit_bytes=mib << 20)


def images_of(tok, grid_ref):
    image = jnp.where(tok < 0, -1, 0)
    first = jnp.zeros_like(tok)
    width = jnp.full_like(tok, grid_ref[0, 1])
    end = jnp.full_like(tok, grid_ref[0, 0] * grid_ref[0, 1])
    upto = jnp.int32(0)
    for n in range(IMGS):
        upto = upto + grid_ref[n, 0] * grid_ref[n, 1]
        past = tok >= upto
        image = jnp.where(past, n + 1, image)
        first = jnp.where(past, upto, first)
        if n + 1 < IMGS:
            width = jnp.where(past, grid_ref[n + 1, 1], width)
            end = jnp.where(past, upto + grid_ref[n + 1, 0] * grid_ref[n + 1, 1], end)
        else:
            width = jnp.where(past, 2, width)
    return image, first, width, end


def divide(a, b):
    return jnp.floor((a.astype(F32) + 0.5) / b.astype(F32)).astype(I32)


def rope_kernel(scal_ref, grid_ref, q_ref, k_ref, v_ref, own_ref, oth_ref):
    core = scal_ref[1]
    base = scal_ref[0] * BLK
    tok = base + lax.broadcasted_iota(I32, (BLK, HD), 0)
    lane = lax.broadcasted_iota(I32, (BLK, HD), 1)
    _, first, width, _ = images_of(tok, grid_ref)
    local = tok - first
    row = divide(local, width)
    col = local - row * width
    k = (lane % 32).astype(F32)
    freq = jnp.exp(k * (-math.log(100.0) / 32.0))
    ang = jnp.where(lane < 64, row, col).astype(F32) * freq
    cos = jnp.cos(ang)
    low = (lane % 64) < 32
    sin = jnp.where(low, -jnp.sin(ang), jnp.sin(ang))
    for out_ref, half in ((own_ref, core), (oth_ref, 1 - core)):

        def head(h, carry, out_ref=out_ref, half=half):
            src = pl.multiple_of(half * HALF + h * HD, HD)
            dst = pl.multiple_of(h * HD, HD)
            for i, ref in ((0, q_ref), (1, k_ref)):
                x = ref[:, pl.ds(src, HD)].astype(F32)
                swap = jnp.where(low, pltpu.roll(x, 96, 1), pltpu.roll(x, 32, 1))
                out_ref[i, :, pl.ds(dst, HD)] = (x * cos + swap * sin).astype(BF16)
            out_ref[2, :, pl.ds(dst, HD)] = v_ref[:, pl.ds(src, HD)]
            return carry

        lax.fori_loop(0, HALF // HD, head, 0)


def attend_kernel(scal_ref, grid_ref, a_ref, b_ref, c_ref, d_ref, gamma_ref, mid_ref, edge_ref, bias_ref, pool_ref):
    chip = scal_ref[0] // 2
    core = scal_ref[1]
    lo = chip * 2 * BLK
    hi = lo + 2 * BLK

    @pl.when(pl.program_id(0) == 0)
    def _():
        lane = lax.broadcasted_iota(I32, (8, NB * BLK), 1)
        place = lane // BLK
        ktok = lo + lane % BLK + BLK * jnp.where(core == 0, place, 1 - place)
        kimg, kfirst, kwidth, kend = images_of(ktok, grid_ref)
        for i in range(NB):
            qtok = lo + BLK * jnp.where(core == 0, i, 1 - i) + lax.broadcasted_iota(I32, (BLK, HD), 0)
            qimg, _, _, _ = images_of(qtok, grid_ref)
            for j in range(NB):
                same = qimg == kimg[:1, j * BLK : (j + 1) * BLK]
                bias_ref[i * BLK : (i + 1) * BLK, j * BLK : (j + 1) * BLK] = jnp.where(same, 0.0, NEG)
        local = ktok - kfirst
        prow = divide(jnp.maximum(local, 0), kwidth)
        pcol = local - prow * kwidth
        target = kfirst // 4 + (prow // 2) * (kwidth // 2) + pcol // 2
        begins = (kfirst >= lo) & (kfirst < hi)
        ends = (kend > lo) & (kend <= hi)
        owned = jnp.where(core == 0, begins.astype(I32), ends.astype(I32)) > 0
        valid = owned & (kimg >= 0) & (kimg < IMGS)
        target = jnp.where(valid, target, -1)[:1]
        r = lax.broadcasted_iota(I32, (2 * ROWS, NB * BLK), 0)
        far = jnp.where(core == 0, ROWS, -ROWS)
        mine = chip * ROWS + jnp.where(r < ROWS, r, r - ROWS + far)
        pool_ref[...] = jnp.where((target == mine) & (target >= 0), 1.0, 0.0).astype(BF16)

    refs = (a_ref, b_ref, c_ref, d_ref)
    keys = jnp.concatenate([ref[1] for ref in refs], axis=0)
    vals = jnp.concatenate([ref[2] for ref in refs], axis=0)
    gamma = gamma_ref[...].astype(F32)
    scale = HD ** -0.5
    branch = []
    for i in range(NB):
        s = lax.dot_general(refs[i][0], keys, (((1,), (1,)), ((), ())), preferred_element_type=F32)
        s = s * scale + bias_ref[i * BLK : (i + 1) * BLK, :]
        e = jnp.exp(s - jnp.max(s, axis=1, keepdims=True))
        total = jnp.sum(e, axis=1, keepdims=True)
        o = jnp.dot(e.astype(BF16), vals, preferred_element_type=F32)
        branch.append((o * (gamma / total)).astype(BF16))
    pooled = 0.25 * jnp.dot(pool_ref[...], jnp.concatenate(branch, axis=0), preferred_element_type=F32)
    pooled = pooled.astype(BF16)
    mid_ref[...] = pooled[:ROWS]
    edge_ref[...] = pooled[ROWS:]


def project_kernel(scal_ref, *refs):
    core = scal_ref[1]
    w_ref = refs[-3]
    mine_ref, send_ref = refs[-2:]
    n = (len(refs) - 3) // 2
    own = jnp.concatenate([refs[2 * i][...] for i in range(n)], axis=0)
    oth = jnp.concatenate([refs[2 * i + 1][...] for i in range(n)], axis=0)
    for side, out_ref in ((0, mine_ref), (1, send_ref)):
        total = jnp.dot(own, w_ref[side, core], preferred_element_type=F32)
        total += jnp.dot(oth, w_ref[side, 1 - core], preferred_element_type=F32)
        out_ref[...] = total.astype(BF16)


def index_kernel(scal_ref, pos_ref, to_ref, from_ref):
    group = scal_ref[2]
    i = lax.broadcasted_iota(I32, (GPOOL, GPOOL), 0)
    j = lax.broadcasted_iota(I32, (GPOOL, GPOOL), 1)
    before = jnp.where(i < j, 1.0, 0.0).astype(BF16)
    own = pos_ref[pl.ds(group, 1), :] // GPOOL
    hot = (own == lax.broadcasted_iota(I32, (GROUPS, GPOOL), 0)).astype(F32)
    count = jnp.dot(hot.astype(BF16), before, preferred_element_type=F32)
    rank = jnp.sum(hot * count, axis=0, keepdims=True)
    to_ref[...] = own * CAP + rank.astype(I32)
    pos = pos_ref[...]
    here = pos // GPOOL == group
    rank = jnp.dot(here.astype(F32).astype(BF16), before, preferred_element_type=F32).astype(I32)
    rank = jnp.where(here, rank, -1)
    local = pos % GPOOL + 1
    high = (local // 32).astype(F32)
    low = (local % 32).astype(F32)
    r = lax.broadcasted_iota(I32, (CAP, GPOOL), 0)
    for g in range(GROUPS):
        pick = (rank[g : g + 1] == r).astype(F32).astype(BF16)
        pair = jnp.concatenate([high[g : g + 1], low[g : g + 1], jnp.zeros((6, GPOOL), F32)], axis=0)
        got = lax.dot_general(pair.astype(BF16), pick, (((1,), (1,)), ((), ())), preferred_element_type=F32)
        value = got[0:1] * 32.0 + got[1:2] - 1.0
        from_ref[:, g * CAP : (g + 1) * CAP] = value.astype(I32)


def send_kernel(scal_ref, to_ref, mine_ref, got_ref, out_ref, all_ref):
    chip = scal_ref[0] // 2
    core = scal_ref[1]
    full = CHIPS // 2 - 1
    half = ROWS // 2
    step = jnp.where(core == 0, CHIPS - 1, 1)

    def put(ref, src, n, row):
        all_ref[pl.ds(pl.multiple_of(row, half), n), :] = ref[src : src + n, :]

    put(mine_ref, 0, ROWS, chip * ROWS)
    for k in range(1, full + 1):
        put(mine_ref, k * ROWS, ROWS, ((chip + k * step) % CHIPS) * ROWS)
        put(got_ref, (k - 1) * ROWS, ROWS, ((chip + k * (CHIPS - step)) % CHIPS) * ROWS)
    last = ((chip + CHIPS // 2) % CHIPS) * ROWS
    put(mine_ref, (full + 1) * ROWS, half, last + core * half)
    put(got_ref, full * ROWS, half, last + (1 - core) * half)
    rows = 256
    for i in range(GROUPS * CAP // rows):
        r = i * rows + lax.broadcasted_iota(I32, (rows, GPOOL), 0)
        pick = jnp.where(to_ref[...] == r, 1.0, 0.0).astype(BF16)
        out_ref[i * rows : (i + 1) * rows, :] = jnp.dot(pick, all_ref[...], preferred_element_type=F32).astype(BF16)


def place_kernel(from_ref, got_ref, out_ref):
    rows = 256
    for i in range(GPOOL // rows):
        r = i * rows + lax.broadcasted_iota(I32, (rows, GROUPS * CAP), 0)
        pick = jnp.where(from_ref[...] == r, 1.0, 0.0).astype(BF16)
        out_ref[i * rows : (i + 1) * rows, :] = jnp.dot(pick, got_ref[...], preferred_element_type=F32).astype(BF16)


def body(queries, keys, values, gamma, w_merge, grids, positions):
    me = lax.axis_index("mlp")
    core = me % 2
    scal = jnp.stack([me, core, lax.axis_index("grp"), me]).astype(I32)
    shape = jax.ShapeDtypeStruct

    own, oth = pl.pallas_call(
        rope_kernel,
        out_shape=[shape((3, BLK, HALF), BF16)] * 2,
        in_specs=[smem(), smem(), vmem(), vmem(), vmem()],
        out_specs=[vmem(), vmem()],
        compiler_params=params(24),
        name="rope",
    )(scal, grids, queries, keys, values)
    up = lax.ppermute(own, "mlp", SAME)
    across = lax.ppermute(oth, "mlp", OPP)
    beside = lax.ppermute(oth, "mlp", PART)

    gains = lax.all_to_all(
        jnp.broadcast_to(gamma[None, :], (2 * CHIPS, HD)), "mlp", split_axis=0, concat_axis=0, tiled=True
    )
    gains = lax.dynamic_slice_in_dim(gains, core * CHIPS, CHIPS, 0).reshape(1, HALF)

    cols = lax.all_gather(w_merge, "grp", axis=0, tiled=True)
    cols = jnp.stack([cols, lax.ppermute(cols, "mlp", PART)]).reshape(2, 2, HALF, HD)

    to, frm = pl.pallas_call(
        index_kernel,
        out_shape=[shape((1, GPOOL), I32), shape((1, GROUPS * CAP), I32)],
        in_specs=[smem(), vmem()],
        out_specs=[vmem(), vmem()],
        compiler_params=params(24),
        name="index",
    )(scal, positions.reshape(GROUPS, GPOOL))

    part = pl.BlockSpec((3, BLK, HD), lambda h: (0, 0, h))
    mid, edge = pl.pallas_call(
        attend_kernel,
        grid=(CHIPS,),
        out_shape=[shape((ROWS, HALF), BF16)] * 2,
        in_specs=[smem(), smem(), part, part, part, part, pl.BlockSpec((1, HD), lambda h: (0, h))],
        out_specs=[pl.BlockSpec((ROWS, HD), lambda h: (0, h))] * 2,
        scratch_shapes=[pltpu.VMEM((NB * BLK, NB * BLK), F32), pltpu.VMEM((2 * ROWS, NB * BLK), BF16)],
        compiler_params=params(24),
        name="attend",
    )(scal, grids, own, beside, up, across, gains)

    h_own = mid + lax.ppermute(edge, "mlp", RING)
    h_oth = lax.ppermute(mid, "mlp", PART) + lax.ppermute(edge, "mlp", OPP)
    shards = [h_own, h_oth]
    a, b = h_own, h_oth
    for _ in range(CHIPS // 2 - 1):
        a = lax.ppermute(a, "mlp", RING)
        b = lax.ppermute(b, "mlp", RING)
        shards += [a, b]
    a = lax.ppermute(lax.dynamic_slice_in_dim(a, core * 32, 32, 0), "mlp", RING)
    b = lax.ppermute(lax.dynamic_slice_in_dim(b, core * 32, 32, 0), "mlp", RING)
    shards += [a, b]

    rows = ROWS * (CHIPS // 2) + ROWS // 2
    mine, send = pl.pallas_call(
        project_kernel,
        out_shape=[shape((rows, HD), BF16)] * 2,
        in_specs=[smem()] + [vmem()] * (len(shards) + 1),
        out_specs=[vmem(), vmem()],
        compiler_params=params(32),
        name="project",
    )(scal, *shards, cols)
    got = lax.ppermute(send[ROWS:], "mlp", PART)
    out = pl.pallas_call(
        send_kernel,
        out_shape=shape((GROUPS * CAP, HD), BF16),
        in_specs=[smem(), vmem(), vmem(), vmem()],
        out_specs=vmem(),
        scratch_shapes=[pltpu.VMEM((GPOOL, HD), BF16)],
        compiler_params=params(24),
        name="pack",
    )(scal, to, mine, got)
    out = lax.all_to_all(out, "grp", split_axis=0, concat_axis=0, tiled=True)
    return pl.pallas_call(
        place_kernel,
        out_shape=shape((GPOOL, HD), BF16),
        in_specs=[vmem(), vmem()],
        out_specs=vmem(),
        compiler_params=params(24),
        name="place",
    )(frm, out)


def solution(mesh):
    return jax.shard_map(
        body,
        mesh=mesh,
        in_specs=(
            P(("grp", "mlp"), None),
            P(("grp", "mlp"), None),
            P(("grp", "mlp"), None),
            P("mlp"),
            P("grp", "mlp"),
            P("grp", None),
            P(),
        ),
        out_specs=P("grp", "mlp"),
        check_vma=False,
    )
```

time: 446 us -> 224 us (0.50)
  waiting for transfers between devices: 241 us -> 38.2 us
  local copies, waits for them, and re-layouts: 105 us -> 6.66 us
  starting transfers between devices: 26.6 us -> 105 us
  Pallas kernels: 0 us -> 40.7 us
  matrix products: 32.6 us -> 0 us
  other arithmetic: 21.6 us -> 1.99 us
  blocking collectives: 0 us -> 16.7 us
  loops' own time: 4.91 us -> 0 us
    all_to_all x3 -> x1, waiting for transfers between devices: 150 us -> 29.7 us  [body(): lax.all_to_all(jnp.broadcast_to(gamma[None, :], (2 * CHIPS, HD)), 'mlp',...]
    ppermute x0 -> x24, starting transfers between devices: none -> 98 us  [the longest x7 28.9 us: body(): a = lax.ppermute(a, 'mlp', RING)]
    all_gather x3 -> x1, waiting for transfers between devices: 90.7 us -> 0.02 us  [body(): cols = lax.all_gather(w_merge, 'grp', axis=0, tiled=True)]
    scatter x1 -> x0, local copies, waits for them, and re-layouts: 60.3 us -> none  [body(): jnp.zeros((prompt,), jnp.int32).at[positions]]
    pallas_call x0 -> x6, Pallas kernels: none -> 40.7 us  [the longest x1 25.1 us: body(): pl.pallas_call(attend_kernel, grid=(CHIPS,), out_shape=[shape((ROWS, HALF...]
    dot_general x17 -> x0, matrix products: 32.6 us -> none  [the longest x8 13.1 us: block(): jnp.einsum('hqk,khd->qhd', probs, v_blk, preferred_element_type=jnp.float32)]
    all_to_all x3 -> x1, starting transfers between devices: 26.1 us -> 6.99 us  [body(): lax.all_to_all(jnp.broadcast_to(gamma[None, :], (2 * CHIPS, HD)), 'mlp',...]
    gather x2 -> x0, local copies, waits for them, and re-layouts: 17.7 us -> none  [the longest x1 12.1 us: body(): picked = jnp.take(branch, sources, axis=0).astype(jnp.float32)]
  transfers between devices with their start and end apart: 6 -> 26, of which waited for: 5 -> 9; matrix products, arithmetic and copies ran while one was open for 32% -> 2% of each run, Pallas kernels for 0% -> 12%
where the time goes in v1:
time: 224 us; the launch traced here: 223 us
  starting transfers between devices  105 us (47%)
  Pallas kernels  40.7 us (18%)
  waiting for transfers between devices  38.2 us (17%)
  blocking collectives  16.7 us (7%)
  between operations  13.8 us (6%)
  local copies, waits for them, and re-layouts  6.66 us (3%)
    all_to_all x1, waiting for transfers between devices, body(): lax.all_to_all(jnp.broadcast_to(gamma[None, :], (2 * CHIPS, HD)), 'mlp',...  29.7 us
    ppermute x7, starting transfers between devices, body(): a = lax.ppermute(a, 'mlp', RING)  28.9 us
    pallas_call x1, Pallas kernels, body(): pl.pallas_call(attend_kernel, grid=(CHIPS,), out_shape=[shape((ROWS, HALF...  25.1 us
    ppermute x7, starting transfers between devices, body(): b = lax.ppermute(b, 'mlp', RING)  22 us
    all_to_all x1, blocking collectives, body(): out = lax.all_to_all(out, 'grp', split_axis=0, concat_axis=0, tiled=True)  16.7 us
    ppermute x1, starting transfers between devices, body(): beside = lax.ppermute(oth, 'mlp', PART)  8.77 us
    ppermute x1, starting transfers between devices, body(): got = lax.ppermute(send[ROWS:], 'mlp', PART)  7.86 us
    all_to_all x1, starting transfers between devices, body(): lax.all_to_all(jnp.broadcast_to(gamma[None, :], (2 * CHIPS, HD)), 'mlp',...  6.99 us
  transfers between devices with their start and end apart: 26, of which 9 were waited for; matrix products, arithmetic and copies ran while one was open for 2% of the time, Pallas kernels for 12%

profile of v1, /device:TPU:1, one launch (start us, length us, event | category | flops | bytes accessed | tf_op | source)
XLA Modules:
  0.0 223.1 jit_solution(6562944322176644102)
XLA Ops:
  11.0 6.2 %rope.1 = (bf16[3,128,2048]{2,1,0:T(8,128)(2,1)S(1)}, bf16[3,128,2048]{2,1,0:T(8,128)(2,1)}) custom-call(s32[4]{0:T(128)S(1)} %pad_add_fusion.scal_ref, s32[16,2]{1,0:T(8,128)S(1)} %copy.11.grid_ref, bf16[128,4096]{1,0:T(8,128)(2,1)S(1)} %copy-done, bf16[128,4096]{1,0:T(8,128)(2,1)S(1)} %copy-done.1, bf16[128,4096]{1,0:T(8,128)(2,1)S(1)} %copy-done.2), custom_call_target="tpu_custom_call" | custom-call | tf_op jit(solution)/shard_map/rope/pallas_call | solution.py:230
  17.2 8.8 %collective-permute-start = (bf16[3,128,2048]{2,1,0:T(8,128)(2,1)}, bf16[3,128,2048]{2,1,0:T(8,128)(2,1)S(1)}, u32[]{:S(2)}, u32[]{:S(2)}) collective-permute-start(bf16[3,128,2048]{2,1,0:T(8,128)(2,1)} %get-tuple-element.16), channel_id=1, source_target_pairs={{0,1},{1,0},{2,3},{3,2},{4,5},{5,4},{6,7},{7,6},{8,9},{9,8},{10,11... | collective-permute-start | bytes 4718600 | tf_op jit(solution)/shard_map/ppermute | solution.py:240
  27.9 6.6 %collective-permute-start.2 = (bf16[3,128,2048]{2,1,0:T(8,128)(2,1)}, bf16[3,128,2048]{2,1,0:T(8,128)(2,1)}, u32[]{:S(2)}, u32[]{:S(2)}) collective-permute-start(bf16[3,128,2048]{2,1,0:T(8,128)(2,1)} %get-tuple-element.16), channel_id=1, source_target_pairs={{1,30},{3,0},{5,2},{7,4},{9,6},{11,8},{13,10},{15,12},{17,14},{19,... | collective-permute-start | bytes 4718600 | tf_op jit(solution)/shard_map/ppermute | solution.py:239
  35.2 7.0 %all-to-all-start = ((bf16[32,1,128]{2,1,0:T(2,128)(2,1)}), bf16[32,1,128]{2,1,0:T(2,128)(2,1)S(1)}, u32[]{:S(2)}, u32[]{:S(2)}) async-start(bf16[32,1,128]{2,1,0:T(2,128)(2,1)} %broadcast_in_dim.2), calls=%async_computation | async-start | bytes 32768 | tf_op jit(solution)/shard_map/all_to_all | solution.py:242
  42.3 29.7 %all-to-all-done = bf16[32,1,128]{2,1,0:T(2,128)(2,1)S(1)} async-done(((bf16[32,1,128]{2,1,0:T(2,128)(2,1)}), bf16[32,1,128]{2,1,0:T(2,128)(2,1)S(1)}, u32[]{:S(2)}, u32[]{:S(2)}) %all-to-all-start) | async-done | bytes 8224 | tf_op jit(solution)/shard_map/all_to_all | solution.py:242
  72.0 25.1 %attend.1 = (bf16[64,2048]{1,0:T(8,128)(2,1)S(1)}, bf16[64,2048]{1,0:T(8,128)(2,1)S(1)}) custom-call(s32[4]{0:T(128)S(1)} %pad_add_fusion.scal_ref, s32[16,2]{1,0:T(8,128)S(1)} %copy.11.grid_ref, bf16[3,128,2048]{2,1,0:T(8,128)(2,1)S(1)} %get-tuple-element.15.a_ref, bf16[3,128,2048]{2,1,0:T(8,128)(2,1)S(1)} %collective-permute-done.b_ref, ...), custom_call_target="tpu_custom_call" | custom-call | tf_op jit(solution)/shard_map/attend/pallas_call | solution.py:260
  101.8 4.0 %collective-permute-start.3 = (bf16[64,2048]{1,0:T(8,128)(2,1)S(1)}, bf16[64,2048]{1,0:T(8,128)(2,1)S(1)}, u32[]{:S(2)}, u32[]{:S(2)}) collective-permute-start(bf16[64,2048]{1,0:T(8,128)(2,1)S(1)} %get-tuple-element.18), channel_id=1, source_target_pairs={{0,2},{2,4},{4,6},{6,8},{8,10},{10,12},{12,14},{14,16},{16,18},{18... | collective-permute-start | bytes 786440 | tf_op jit(solution)/shard_map/ppermute | solution.py:271
  105.8 2.9 %collective-permute-done.5 = bf16[64,2048]{1,0:T(8,128)(2,1)S(1)} collective-permute-done((bf16[64,2048]{1,0:T(8,128)(2,1)S(1)}, bf16[64,2048]{1,0:T(8,128)(2,1)S(1)}, u32[]{:S(2)}, u32[]{:S(2)}) %collective-permute-start.5) | collective-permute-done | bytes 262176 | tf_op jit(solution)/shard_map/ppermute | solution.py:272
  110.7 3.4 %collective-permute-start.6 = (bf16[64,2048]{1,0:T(8,128)(2,1)S(1)}, bf16[64,2048]{1,0:T(8,128)(2,1)S(1)}, u32[]{:S(2)}, u32[]{:S(2)}) collective-permute-start(bf16[64,2048]{1,0:T(8,128)(2,1)S(1)} %add.19.refs_0_), channel_id=1, source_target_pairs={{0,2},{2,4},{4,6},{6,8},{8,10},{10,12},{12,14},{14,16},{16,18},{18... | collective-permute-start | bytes 786440 | tf_op jit(solution)/shard_map/ppermute | solution.py:276
  119.0 3.5 %collective-permute-start.8 = (bf16[64,2048]{1,0:T(8,128)(2,1)S(1)}, bf16[64,2048]{1,0:T(8,128)(2,1)S(1)}, u32[]{:S(2)}, u32[]{:S(2)}) collective-permute-start(bf16[64,2048]{1,0:T(8,128)(2,1)S(1)} %collective-permute-done.6.refs_2_), channel_id=1, source_target_pairs={{0,2},{2,4},{4,6},{6,8},{8,10},{10,12},{12,14},{14,16},{16,18},{18... | collective-permute-start | bytes 786440 | tf_op jit(solution)/shard_map/ppermute | solution.py:276
  123.5 3.7 %collective-permute-start.11 = (bf16[64,2048]{1,0:T(8,128)(2,1)S(1)}, bf16[64,2048]{1,0:T(8,128)(2,1)S(1)}, u32[]{:S(2)}, u32[]{:S(2)}) collective-permute-start(bf16[64,2048]{1,0:T(8,128)(2,1)S(1)} %collective-permute-done.9.refs_5_), channel_id=1, source_target_pairs={{0,2},{2,4},{4,6},{6,8},{8,10},{10,12},{12,14},{14,16},{16,18},{18... | collective-permute-start | bytes 786440 | tf_op jit(solution)/shard_map/ppermute | solution.py:277
  127.3 3.5 %collective-permute-start.10 = (bf16[64,2048]{1,0:T(8,128)(2,1)S(1)}, bf16[64,2048]{1,0:T(8,128)(2,1)S(1)}, u32[]{:S(2)}, u32[]{:S(2)}) collective-permute-start(bf16[64,2048]{1,0:T(8,128)(2,1)S(1)} %collective-permute-done.8.refs_4_), channel_id=1, source_target_pairs={{0,2},{2,4},{4,6},{6,8},{8,10},{10,12},{12,14},{14,16},{16,18},{18... | collective-permute-start | bytes 786440 | tf_op jit(solution)/shard_map/ppermute | solution.py:276
  130.9 4.7 %collective-permute-start.13 = (bf16[64,2048]{1,0:T(8,128)(2,1)S(1)}, bf16[64,2048]{1,0:T(8,128)(2,1)S(1)}, u32[]{:S(2)}, u32[]{:S(2)}) collective-permute-start(bf16[64,2048]{1,0:T(8,128)(2,1)S(1)} %collective-permute-done.11.refs_7_), channel_id=1, source_target_pairs={{0,2},{2,4},{4,6},{6,8},{8,10},{10,12},{12,14},{14,16},{16,18},{18... | collective-permute-start | bytes 786440 | tf_op jit(solution)/shard_map/ppermute | solution.py:277
  135.6 3.5 %collective-permute-start.12 = (bf16[64,2048]{1,0:T(8,128)(2,1)S(1)}, bf16[64,2048]{1,0:T(8,128)(2,1)S(1)}, u32[]{:S(2)}, u32[]{:S(2)}) collective-permute-start(bf16[64,2048]{1,0:T(8,128)(2,1)S(1)} %collective-permute-done.10.refs_6_), channel_id=1, source_target_pairs={{0,2},{2,4},{4,6},{6,8},{8,10},{10,12},{12,14},{14,16},{16,18},{18... | collective-permute-start | bytes 786440 | tf_op jit(solution)/shard_map/ppermute | solution.py:276
  139.1 4.8 %collective-permute-start.15 = (bf16[64,2048]{1,0:T(8,128)(2,1)S(1)}, bf16[64,2048]{1,0:T(8,128)(2,1)S(1)}, u32[]{:S(2)}, u32[]{:S(2)}) collective-permute-start(bf16[64,2048]{1,0:T(8,128)(2,1)S(1)} %collective-permute-done.13.refs_9_), channel_id=1, source_target_pairs={{0,2},{2,4},{4,6},{6,8},{8,10},{10,12},{12,14},{14,16},{16,18},{18... | collective-permute-start | bytes 786440 | tf_op jit(solution)/shard_map/ppermute | solution.py:277
  143.9 5.3 %collective-permute-start.22 = (bf16[4096,128]{1,0:T(8,128)(2,1)}, bf16[4096,128]{1,0:T(8,128)(2,1)}, u32[]{:S(2)}, u32[]{:S(2)}) collective-permute-start(bf16[4096,128]{1,0:T(8,128)(2,1)} %all-gather.2.cloned.1.call-done), channel_id=1, source_target_pairs={{0,1},{1,0},{2,3},{3,2},{4,5},{5,4},{6,7},{7,6},{8,9},{9,8},{10,11... | collective-permute-start | bytes 3145736 | tf_op jit(solution)/shard_map/ppermute | solution.py:248
  149.2 4.9 %collective-permute-start.14 = (bf16[64,2048]{1,0:T(8,128)(2,1)S(1)}, bf16[64,2048]{1,0:T(8,128)(2,1)S(1)}, u32[]{:S(2)}, u32[]{:S(2)}) collective-permute-start(bf16[64,2048]{1,0:T(8,128)(2,1)S(1)} %collective-permute-done.12.refs_8_), channel_id=1, source_target_pairs={{0,2},{2,4},{4,6},{6,8},{8,10},{10,12},{12,14},{14,16},{16,18},{18... | collective-permute-start | bytes 786440 | tf_op jit(solution)/shard_map/ppermute | solution.py:276
  157.4 5.0 %collective-permute-start.16 = (bf16[64,2048]{1,0:T(8,128)(2,1)S(1)}, bf16[64,2048]{1,0:T(8,128)(2,1)}, u32[]{:S(2)}, u32[]{:S(2)}) collective-permute-start(bf16[64,2048]{1,0:T(8,128)(2,1)S(1)} %collective-permute-done.14.refs_10_), channel_id=1, source_target_pairs={{0,2},{2,4},{4,6},{6,8},{8,10},{10,12},{12,14},{14,16},{16,18},{18... | collective-permute-start | bytes 786440 | tf_op jit(solution)/shard_map/ppermute | solution.py:276
  165.7 5.1 %collective-permute-start.18 = (bf16[64,2048]{1,0:T(8,128)(2,1)}, bf16[64,2048]{1,0:T(8,128)(2,1)S(1)}, u32[]{:S(2)}, u32[]{:S(2)}) collective-permute-start(bf16[64,2048]{1,0:T(8,128)(2,1)} %collective-permute-done.16.refs_12_), channel_id=1, source_target_pairs={{0,2},{2,4},{4,6},{6,8},{8,10},{10,12},{12,14},{14,16},{16,18},{18... | collective-permute-start | bytes 786440 | tf_op jit(solution)/shard_map/ppermute | solution.py:276
  170.9 3.0 %collective-permute-start.21 = (bf16[32,2048]{1,0:T(8,128)(2,1)S(1)}, bf16[32,2048]{1,0:T(8,128)(2,1)S(1)}, u32[]{:S(2)}, u32[]{:S(2)}) collective-permute-start(bf16[32,2048]{1,0:T(8,128)(2,1)S(1)} %constant_dynamic-slice_fusion), channel_id=1, source_target_pairs={{0,2},{2,4},{4,6},{6,8},{8,10},{10,12},{12,14},{14,16},{16,18},{18... | collective-permute-start | bytes 393224 | tf_op jit(solution)/shard_map/ppermute | solution.py:280
  174.5 4.9 %collective-permute-start.20 = (bf16[32,2048]{1,0:T(8,128)(2,1)S(1)}, bf16[32,2048]{1,0:T(8,128)(2,1)S(1)}, u32[]{:S(2)}, u32[]{:S(2)}) collective-permute-start(bf16[32,2048]{1,0:T(8,128)(2,1)S(1)} %constant_dynamic-slice_fusion.1), channel_id=1, source_target_pairs={{0,2},{2,4},{4,6},{6,8},{8,10},{10,12},{12,14},{14,16},{16,18},{18... | collective-permute-start | bytes 393224 | tf_op jit(solution)/shard_map/ppermute | solution.py:279
  181.3 3.5 %project.1 = (bf16[544,128]{1,0:T(8,128)(2,1)S(1)}, bf16[544,128]{1,0:T(8,128)(2,1)S(1)}) custom-call(s32[4]{0:T(128)S(1)} %pad_add_fusion.scal_ref, bf16[64,2048]{1,0:T(8,128)(2,1)S(1)} %add.19.refs_0_, bf16[64,2048]{1,0:T(8,128)(2,1)S(1)} %add.20.refs_1_, bf16[64,2048]{1,0:T(8,128)(2,1)S(1)} %collective-permute-done.6.refs_2_, ...), custom_call_target="tpu_custom_call" | custom-call | tf_op jit(solution)/shard_map/project/pallas_call | solution.py:284
  184.8 7.9 %collective-permute-start.23 = (bf16[480,128]{1,0:T(8,128)(2,1)S(1)}, bf16[480,128]{1,0:T(8,128)(2,1)S(1)}, u32[]{:S(2)}, u32[]{:S(2)}) collective-permute-start(bf16[480,128]{1,0:T(8,128)(2,1)S(1)} %slice.3), channel_id=1, source_target_pairs={{0,1},{1,0},{2,3},{3,2},{4,5},{5,4},{6,7},{7,6},{8,9},{9,8},{10,11... | collective-permute-start | bytes 368648 | tf_op jit(solution)/shard_map/ppermute | solution.py:292
  197.6 16.7 %all_to_all.17 = bf16[16,128,128]{2,1,0:T(8,128)(2,1)S(1)} all-to-all(bf16[16,128,128]{2,1,0:T(8,128)(2,1)S(1)} %bitcast.9), channel_id=1, replica_groups=mesh['grp'=16,'mlp'=32] {'grp'}, dimensions={0} | all-to-all | bytes 1048576 | tf_op jit(solution)/shard_map/all_to_all | solution.py:302
  (59 shorter events, 35.7 us)
Async XLA Ops:
  6.5 137.4 %all-gather.2.cloned.1.call-start = ((), (), s32[]{:S(2)}) async-start(), calls=%async_computation.2 | async-start | bytes 1114112 | tf_op jit(solution)/shard_map/all_gather | solution.py:247
  17.2 54.7 %collective-permute-start = (bf16[3,128,2048]{2,1,0:T(8,128)(2,1)}, bf16[3,128,2048]{2,1,0:T(8,128)(2,1)S(1)}, u32[]{:S(2)}, u32[]{:S(2)}) collective-permute-start(bf16[3,128,2048]{2,1,0:T(8,128)(2,1)} %get-tuple-element.16), channel_id=1, source_target_pairs={{0,1},{1,0},{2,3},{3,2},{4,5},{5,4},{6,7},{7,6},{8,9},{9,8},{10,11... | collective-permute-start | bytes 4718600 | tf_op jit(solution)/shard_map/ppermute | solution.py:240
  26.0 46.0 %collective-permute-start.1 = (bf16[3,128,2048]{2,1,0:T(8,128)(2,1)S(1)}, bf16[3,128,2048]{2,1,0:T(8,128)(2,1)}, u32[]{:S(2)}, u32[]{:S(2)}) collective-permute-start(bf16[3,128,2048]{2,1,0:T(8,128)(2,1)S(1)} %get-tuple-element.15.a_ref), channel_id=1, source_target_pairs={{0,30},{2,0},{4,2},{6,4},{8,6},{10,8},{12,10},{14,12},{16,14},{18,... | collective-permute-start | bytes 4718600 | tf_op jit(solution)/shard_map/ppermute | solution.py:238
  27.9 44.0 %collective-permute-start.2 = (bf16[3,128,2048]{2,1,0:T(8,128)(2,1)}, bf16[3,128,2048]{2,1,0:T(8,128)(2,1)}, u32[]{:S(2)}, u32[]{:S(2)}) collective-permute-start(bf16[3,128,2048]{2,1,0:T(8,128)(2,1)} %get-tuple-element.16), channel_id=1, source_target_pairs={{1,30},{3,0},{5,2},{7,4},{9,6},{11,8},{13,10},{15,12},{17,14},{19,... | collective-permute-start | bytes 4718600 | tf_op jit(solution)/shard_map/ppermute | solution.py:239
  35.2 36.7 %all-to-all-start = ((bf16[32,1,128]{2,1,0:T(2,128)(2,1)}), bf16[32,1,128]{2,1,0:T(2,128)(2,1)S(1)}, u32[]{:S(2)}, u32[]{:S(2)}) async-start(bf16[32,1,128]{2,1,0:T(2,128)(2,1)} %broadcast_in_dim.2), calls=%async_computation | async-start | bytes 32768 | tf_op jit(solution)/shard_map/all_to_all | solution.py:242
  97.1 8.7 %collective-permute-start.4 = (bf16[64,2048]{1,0:T(8,128)(2,1)S(1)}, bf16[64,2048]{1,0:T(8,128)(2,1)S(1)}, u32[]{:S(2)}, u32[]{:S(2)}) collective-permute-start(bf16[64,2048]{1,0:T(8,128)(2,1)S(1)} %get-tuple-element.17), channel_id=1, source_target_pairs={{0,1},{1,0},{2,3},{3,2},{4,5},{5,4},{6,7},{7,6},{8,9},{9,8},{10,11... | collective-permute-start | bytes 786440 | tf_op jit(solution)/shard_map/ppermute | solution.py:272
  99.7 8.9 %collective-permute-start.5 = (bf16[64,2048]{1,0:T(8,128)(2,1)S(1)}, bf16[64,2048]{1,0:T(8,128)(2,1)S(1)}, u32[]{:S(2)}, u32[]{:S(2)}) collective-permute-start(bf16[64,2048]{1,0:T(8,128)(2,1)S(1)} %get-tuple-element.18), channel_id=1, source_target_pairs={{1,30},{3,0},{5,2},{7,4},{9,6},{11,8},{13,10},{15,12},{17,14},{19,... | collective-permute-start | bytes 786440 | tf_op jit(solution)/shard_map/ppermute | solution.py:272
  101.8 8.9 %collective-permute-start.3 = (bf16[64,2048]{1,0:T(8,128)(2,1)S(1)}, bf16[64,2048]{1,0:T(8,128)(2,1)S(1)}, u32[]{:S(2)}, u32[]{:S(2)}) collective-permute-start(bf16[64,2048]{1,0:T(8,128)(2,1)S(1)} %get-tuple-element.18), channel_id=1, source_target_pairs={{0,2},{2,4},{4,6},{6,8},{8,10},{10,12},{12,14},{14,16},{16,18},{18... | collective-permute-start | bytes 786440 | tf_op jit(solution)/shard_map/ppermute | solution.py:271
  108.7 7.4 %collective-permute-start.7 = (bf16[64,2048]{1,0:T(8,128)(2,1)S(1)}, bf16[64,2048]{1,0:T(8,128)(2,1)S(1)}, u32[]{:S(2)}, u32[]{:S(2)}) collective-permute-start(bf16[64,2048]{1,0:T(8,128)(2,1)S(1)} %add.20.refs_1_), channel_id=1, source_target_pairs={{0,2},{2,4},{4,6},{6,8},{8,10},{10,12},{12,14},{14,16},{16,18},{18... | collective-permute-start | bytes 786440 | tf_op jit(solution)/shard_map/ppermute | solution.py:277
  110.7 8.2 %collective-permute-start.6 = (bf16[64,2048]{1,0:T(8,128)(2,1)S(1)}, bf16[64,2048]{1,0:T(8,128)(2,1)S(1)}, u32[]{:S(2)}, u32[]{:S(2)}) collective-permute-start(bf16[64,2048]{1,0:T(8,128)(2,1)S(1)} %add.19.refs_0_), channel_id=1, source_target_pairs={{0,2},{2,4},{4,6},{6,8},{8,10},{10,12},{12,14},{14,16},{16,18},{18... | collective-permute-start | bytes 786440 | tf_op jit(solution)/shard_map/ppermute | solution.py:276
  116.1 7.4 %collective-permute-start.9 = (bf16[64,2048]{1,0:T(8,128)(2,1)S(1)}, bf16[64,2048]{1,0:T(8,128)(2,1)S(1)}, u32[]{:S(2)}, u32[]{:S(2)}) collective-permute-start(bf16[64,2048]{1,0:T(8,128)(2,1)S(1)} %collective-permute-done.7.refs_3_), channel_id=1, source_target_pairs={{0,2},{2,4},{4,6},{6,8},{8,10},{10,12},{12,14},{14,16},{16,18},{18... | collective-permute-start | bytes 786440 | tf_op jit(solution)/shard_map/ppermute | solution.py:277
  119.0 8.3 %collective-permute-start.8 = (bf16[64,2048]{1,0:T(8,128)(2,1)S(1)}, bf16[64,2048]{1,0:T(8,128)(2,1)S(1)}, u32[]{:S(2)}, u32[]{:S(2)}) collective-permute-start(bf16[64,2048]{1,0:T(8,128)(2,1)S(1)} %collective-permute-done.6.refs_2_), channel_id=1, source_target_pairs={{0,2},{2,4},{4,6},{6,8},{8,10},{10,12},{12,14},{14,16},{16,18},{18... | collective-permute-start | bytes 786440 | tf_op jit(solution)/shard_map/ppermute | solution.py:276
  127.3 8.3 %collective-permute-start.10 = (bf16[64,2048]{1,0:T(8,128)(2,1)S(1)}, bf16[64,2048]{1,0:T(8,128)(2,1)S(1)}, u32[]{:S(2)}, u32[]{:S(2)}) collective-permute-start(bf16[64,2048]{1,0:T(8,128)(2,1)S(1)} %collective-permute-done.8.refs_4_), channel_id=1, source_target_pairs={{0,2},{2,4},{4,6},{6,8},{8,10},{10,12},{12,14},{14,16},{16,18},{18... | collective-permute-start | bytes 786440 | tf_op jit(solution)/shard_map/ppermute | solution.py:276
  130.9 8.2 %collective-permute-start.13 = (bf16[64,2048]{1,0:T(8,128)(2,1)S(1)}, bf16[64,2048]{1,0:T(8,128)(2,1)S(1)}, u32[]{:S(2)}, u32[]{:S(2)}) collective-permute-start(bf16[64,2048]{1,0:T(8,128)(2,1)S(1)} %collective-permute-done.11.refs_7_), channel_id=1, source_target_pairs={{0,2},{2,4},{4,6},{6,8},{8,10},{10,12},{12,14},{14,16},{16,18},{18... | collective-permute-start | bytes 786440 | tf_op jit(solution)/shard_map/ppermute | solution.py:277
  135.6 13.7 %collective-permute-start.12 = (bf16[64,2048]{1,0:T(8,128)(2,1)S(1)}, bf16[64,2048]{1,0:T(8,128)(2,1)S(1)}, u32[]{:S(2)}, u32[]{:S(2)}) collective-permute-start(bf16[64,2048]{1,0:T(8,128)(2,1)S(1)} %collective-permute-done.10.refs_6_), channel_id=1, source_target_pairs={{0,2},{2,4},{4,6},{6,8},{8,10},{10,12},{12,14},{14,16},{16,18},{18... | collective-permute-start | bytes 786440 | tf_op jit(solution)/shard_map/ppermute | solution.py:276
  139.1 15.0 %collective-permute-start.15 = (bf16[64,2048]{1,0:T(8,128)(2,1)S(1)}, bf16[64,2048]{1,0:T(8,128)(2,1)S(1)}, u32[]{:S(2)}, u32[]{:S(2)}) collective-permute-start(bf16[64,2048]{1,0:T(8,128)(2,1)S(1)} %collective-permute-done.13.refs_9_), channel_id=1, source_target_pairs={{0,2},{2,4},{4,6},{6,8},{8,10},{10,12},{12,14},{14,16},{16,18},{18... | collective-permute-start | bytes 786440 | tf_op jit(solution)/shard_map/ppermute | solution.py:277
  143.9 35.5 %collective-permute-start.22 = (bf16[4096,128]{1,0:T(8,128)(2,1)}, bf16[4096,128]{1,0:T(8,128)(2,1)}, u32[]{:S(2)}, u32[]{:S(2)}) collective-permute-start(bf16[4096,128]{1,0:T(8,128)(2,1)} %all-gather.2.cloned.1.call-done), channel_id=1, source_target_pairs={{0,1},{1,0},{2,3},{3,2},{4,5},{5,4},{6,7},{7,6},{8,9},{9,8},{10,11... | collective-permute-start | bytes 3145736 | tf_op jit(solution)/shard_map/ppermute | solution.py:248
  149.2 8.2 %collective-permute-start.14 = (bf16[64,2048]{1,0:T(8,128)(2,1)S(1)}, bf16[64,2048]{1,0:T(8,128)(2,1)S(1)}, u32[]{:S(2)}, u32[]{:S(2)}) collective-permute-start(bf16[64,2048]{1,0:T(8,128)(2,1)S(1)} %collective-permute-done.12.refs_8_), channel_id=1, source_target_pairs={{0,2},{2,4},{4,6},{6,8},{8,10},{10,12},{12,14},{14,16},{16,18},{18... | collective-permute-start | bytes 786440 | tf_op jit(solution)/shard_map/ppermute | solution.py:276
  154.1 9.0 %collective-permute-start.17 = (bf16[64,2048]{1,0:T(8,128)(2,1)S(1)}, bf16[64,2048]{1,0:T(8,128)(2,1)}, u32[]{:S(2)}, u32[]{:S(2)}) collective-permute-start(bf16[64,2048]{1,0:T(8,128)(2,1)S(1)} %collective-permute-done.15.refs_11_), channel_id=1, source_target_pairs={{0,2},{2,4},{4,6},{6,8},{8,10},{10,12},{12,14},{14,16},{16,18},{18... | collective-permute-start | bytes 786440 | tf_op jit(solution)/shard_map/ppermute | solution.py:277
  157.4 8.3 %collective-permute-start.16 = (bf16[64,2048]{1,0:T(8,128)(2,1)S(1)}, bf16[64,2048]{1,0:T(8,128)(2,1)}, u32[]{:S(2)}, u32[]{:S(2)}) collective-permute-start(bf16[64,2048]{1,0:T(8,128)(2,1)S(1)} %collective-permute-done.14.refs_10_), channel_id=1, source_target_pairs={{0,2},{2,4},{4,6},{6,8},{8,10},{10,12},{12,14},{14,16},{16,18},{18... | collective-permute-start | bytes 786440 | tf_op jit(solution)/shard_map/ppermute | solution.py:276
  163.1 7.7 %collective-permute-start.19 = (bf16[64,2048]{1,0:T(8,128)(2,1)}, bf16[64,2048]{1,0:T(8,128)(2,1)S(1)}, u32[]{:S(2)}, u32[]{:S(2)}) collective-permute-start(bf16[64,2048]{1,0:T(8,128)(2,1)} %collective-permute-done.17.refs_13_), channel_id=1, source_target_pairs={{0,2},{2,4},{4,6},{6,8},{8,10},{10,12},{12,14},{14,16},{16,18},{18... | collective-permute-start | bytes 786440 | tf_op jit(solution)/shard_map/ppermute | solution.py:277
  165.7 8.7 %collective-permute-start.18 = (bf16[64,2048]{1,0:T(8,128)(2,1)}, bf16[64,2048]{1,0:T(8,128)(2,1)S(1)}, u32[]{:S(2)}, u32[]{:S(2)}) collective-permute-start(bf16[64,2048]{1,0:T(8,128)(2,1)} %collective-permute-done.16.refs_12_), channel_id=1, source_target_pairs={{0,2},{2,4},{4,6},{6,8},{8,10},{10,12},{12,14},{14,16},{16,18},{18... | collective-permute-start | bytes 786440 | tf_op jit(solution)/shard_map/ppermute | solution.py:276
  170.9 10.3 %collective-permute-start.21 = (bf16[32,2048]{1,0:T(8,128)(2,1)S(1)}, bf16[32,2048]{1,0:T(8,128)(2,1)S(1)}, u32[]{:S(2)}, u32[]{:S(2)}) collective-permute-start(bf16[32,2048]{1,0:T(8,128)(2,1)S(1)} %constant_dynamic-slice_fusion), channel_id=1, source_target_pairs={{0,2},{2,4},{4,6},{6,8},{8,10},{10,12},{12,14},{14,16},{16,18},{18... | collective-permute-start | bytes 393224 | tf_op jit(solution)/shard_map/ppermute | solution.py:280
  184.8 10.9 %collective-permute-start.23 = (bf16[480,128]{1,0:T(8,128)(2,1)S(1)}, bf16[480,128]{1,0:T(8,128)(2,1)S(1)}, u32[]{:S(2)}, u32[]{:S(2)}) collective-permute-start(bf16[480,128]{1,0:T(8,128)(2,1)S(1)} %slice.3), channel_id=1, source_target_pairs={{0,1},{1,0},{2,3},{3,2},{4,5},{5,4},{6,7},{7,6},{8,9},{9,8},{10,11... | collective-permute-start | bytes 368648 | tf_op jit(solution)/shard_map/ppermute | solution.py:292
  (8 other events, 44.1 us)
Sparse Core Ops, SparseCore 0:
  34.7 52.1 all-gather.1

commit v2 on v1

v2 whole, which is shorter than its diff:
```python
import math

import jax
import jax.numpy as jnp
from jax import lax
from jax.experimental import pallas as pl
from jax.experimental.pallas import tpu as pltpu
from jax.sharding import PartitionSpec as P

HD = 128
HALF = 2048
IMGS = 16
BLK = 128
CHIPS = 16
CHUNKS = 2
HEADS = 8
WIDE = HEADS * HD
STEP = 4
NB = 4
ROWS = 64
CAP = 128
GROUPS = 16
GPOOL = 1024
SCALE = HD ** -0.5 / math.log(2.0)
F32 = jnp.float32
BF16 = jnp.bfloat16
I32 = jnp.int32
FIRST = (-1, 0, 1)
SECOND = (-2,)


def at(z, c):
    return (z % CHIPS) * 2 + c


def jump(k):
    return [(at(z, c), at(z + k, c)) for z in range(CHIPS) for c in range(2)]


SAME = [(at(z, 0), at(z - 1, 0)) for z in range(CHIPS)] + [(at(z, 1), at(z + 1, 1)) for z in range(CHIPS)]
OPP = [(at(z, 1), at(z - 1, 0)) for z in range(CHIPS)] + [(at(z, 0), at(z + 1, 1)) for z in range(CHIPS)]
RING = [(at(z, 0), at(z + 1, 0)) for z in range(CHIPS)] + [(at(z, 1), at(z - 1, 1)) for z in range(CHIPS)]
UP = [(at(z, c), at(z + 1, c)) for z in range(CHIPS) for c in range(2)]
DOWN = [(at(z, c), at(z - 1, c)) for z in range(CHIPS) for c in range(2)]
PART = [(at(z, c), at(z, 1 - c)) for z in range(CHIPS) for c in range(2)]


def vmem():
    return pl.BlockSpec(memory_space=pltpu.VMEM)


def smem():
    return pl.BlockSpec(memory_space=pltpu.SMEM)


def params(mib):
    return pltpu.CompilerParams(vmem_limit_bytes=mib << 20)


def cost(us):
    return pl.CostEstimate(flops=int(us * 1.15e9), bytes_accessed=int(us * 3.5e6), transcendentals=0)


def images_of(tok, grid_ref):
    image = jnp.where(tok < 0, -1, 0)
    first = jnp.zeros_like(tok)
    width = jnp.full_like(tok, grid_ref[0, 1])
    end = jnp.full_like(tok, grid_ref[0, 0] * grid_ref[0, 1])
    upto = jnp.int32(0)
    for n in range(IMGS):
        upto = upto + grid_ref[n, 0] * grid_ref[n, 1]
        past = tok >= upto
        image = jnp.where(past, n + 1, image)
        first = jnp.where(past, upto, first)
        if n + 1 < IMGS:
            width = jnp.where(past, grid_ref[n + 1, 1], width)
            end = jnp.where(past, upto + grid_ref[n + 1, 0] * grid_ref[n + 1, 1], end)
        else:
            width = jnp.where(past, 2, width)
    return image, first, width, end


def divide(a, b):
    return jnp.floor((a.astype(F32) + 0.5) / b.astype(F32)).astype(I32)


def rope_kernel(scal_ref, grid_ref, q_ref, k_ref, v_ref, own_ref, oth_ref, cos_ref, sin_ref):
    lane = lax.broadcasted_iota(I32, (BLK, HD), 1)
    low = (lane % 64) < 32
    step = pl.program_id(0)

    @pl.when(step == 0)
    def _():
        tok = scal_ref[0] * BLK + lax.broadcasted_iota(I32, (BLK, HD), 0)
        _, first, width, _ = images_of(tok, grid_ref)
        local = tok - first
        row = divide(local, width)
        col = local - row * width
        freq = jnp.exp((lane % 32).astype(F32) * (-math.log(100.0) / 32.0))
        ang = jnp.where(lane < 64, row, col).astype(F32) * freq
        cos_ref[...] = jnp.cos(ang)
        sin = jnp.sin(ang)
        sin_ref[...] = jnp.where(low, -sin, sin)

    def fill(out_ref):
        cos = cos_ref[...]
        sin = sin_ref[...]
        for h in range(STEP):
            lanes = slice(h * HD, (h + 1) * HD)
            for i, ref in ((0, q_ref), (1, k_ref)):
                x = ref[:, lanes].astype(F32)
                swap = jnp.where(low, pltpu.roll(x, 96, 1), pltpu.roll(x, 32, 1))
                out_ref[i, :, lanes] = (x * cos + swap * sin).astype(BF16)
        out_ref[2] = v_ref[...]

    n = HEADS // STEP

    @pl.when(step < n)
    def _():
        fill(oth_ref)

    @pl.when(step >= n)
    def _():
        fill(own_ref)


def rope(scal, grids, queries, keys, values, chunk):
    n = HEADS // STEP
    lanes = STEP * HD

    def src(i, scal_ref):
        half = jnp.where(i < n, 1 - scal_ref[1], scal_ref[1])
        return (0, half * (HALF // lanes) + chunk * n + i % n)

    return pl.pallas_call(
        rope_kernel,
        out_shape=[jax.ShapeDtypeStruct((3, BLK, WIDE), BF16)] * 2,
        grid_spec=pltpu.PrefetchScalarGridSpec(
            num_scalar_prefetch=1,
            grid=(2 * n,),
            in_specs=[smem()] + [pl.BlockSpec((BLK, lanes), src)] * 3,
            out_specs=[
                pl.BlockSpec((3, BLK, lanes), lambda i, _: (0, 0, jnp.maximum(i - n, 0))),
                pl.BlockSpec((3, BLK, lanes), lambda i, _: (0, 0, jnp.minimum(i, n - 1))),
            ],
            scratch_shapes=[pltpu.VMEM((BLK, HD), F32)] * 2,
        ),
        compiler_params=params(56),
        cost_estimate=cost(4),
        name="rope",
    )(scal, grids, queries, keys, values)


def layout_kernel(scal_ref, grid_ref, qhot_ref, khot_ref, pool_ref):
    chip = scal_ref[0] // 2
    core = scal_ref[1]
    lo = chip * 2 * BLK
    hi = lo + 2 * BLK
    for i in range(NB):
        tok = lo + BLK * jnp.where(core == 0, i, 1 - i) + lax.broadcasted_iota(I32, (BLK, HD), 0)
        image, _, _, _ = images_of(tok, grid_ref)
        hot = image + 1 == lax.broadcasted_iota(I32, (BLK, HD), 1)
        qhot_ref[i * BLK : (i + 1) * BLK, :] = jnp.where(hot, 256.0, 0.0).astype(BF16)
        khot_ref[i * BLK : (i + 1) * BLK, :] = jnp.where(hot, 128.0, 0.0).astype(BF16)
    lane = lax.broadcasted_iota(I32, (8, NB * BLK), 1)
    place = lane // BLK
    tok = lo + lane % BLK + BLK * jnp.where(core == 0, place, 1 - place)
    image, first, width, end = images_of(tok, grid_ref)
    local = tok - first
    prow = divide(jnp.maximum(local, 0), width)
    pcol = local - prow * width
    target = first // 4 + (prow // 2) * (width // 2) + pcol // 2
    begins = (first >= lo) & (first < hi)
    ends = (end > lo) & (end <= hi)
    owned = jnp.where(core == 0, begins.astype(I32), ends.astype(I32)) > 0
    target = jnp.where(owned & (image >= 0) & (image < IMGS), target, -1)[:1]
    r = lax.broadcasted_iota(I32, (2 * ROWS, NB * BLK), 0)
    far = jnp.where(core == 0, ROWS, -ROWS)
    mine = chip * ROWS + jnp.where(r < ROWS, r, r - ROWS + far)
    pool_ref[...] = jnp.where((target == mine) & (target >= 0), 1.0, 0.0).astype(BF16)


def attend_kernel(a_ref, b_ref, c_ref, d_ref, qhot_ref, khot_ref, pool_ref, mid_ref, edge_ref):
    refs = (a_ref, b_ref, c_ref, d_ref)
    pairs = NB // 2
    ones = jnp.ones((16, NB * BLK), BF16)
    nt = (((1,), (1,)), ((), ()))

    def score(h, i):
        lanes = slice(h * HD, (h + 1) * HD)
        keys = jnp.concatenate([ref[1, :, lanes] for ref in refs], axis=0)
        keys = jnp.concatenate([keys, khot_ref[...]], axis=1)
        q = jnp.concatenate([ref[0, :, lanes] for ref in refs[2 * i : 2 * i + 2]], axis=0)
        q = jnp.concatenate([q, qhot_ref[i * 2 * BLK : (i + 1) * 2 * BLK, :]], axis=1)
        return lax.dot_general(keys, q, nt, preferred_element_type=F32)

    def mix(h, s):
        lanes = slice(h * HD, (h + 1) * HD)
        e = jnp.exp2((s - jnp.max(s, axis=0, keepdims=True)) * SCALE).astype(BF16)
        vals = jnp.concatenate([ref[2, :, lanes] for ref in refs], axis=0)
        o = jnp.dot(jnp.concatenate([vals.T, ones], axis=0), e, preferred_element_type=F32)
        return (o[:HD] / o[HD : HD + 1]).astype(BF16)

    order = [(h, i) for h in range(STEP) for i in range(pairs)]
    later = score(*order[0])
    done = []
    for t, (h, i) in enumerate(order):
        now = later
        if t + 1 < len(order):
            later = score(*order[t + 1])
        done.append(mix(h, now))
        if len(done) == pairs:
            branch = jnp.concatenate(done, axis=1)
            done = []
            pooled = lax.dot_general(pool_ref[...], branch, nt, preferred_element_type=F32)
            pooled = (0.25 * pooled).astype(BF16)
            lanes = slice(h * HD, (h + 1) * HD)
            mid_ref[:, lanes] = pooled[:ROWS]
            edge_ref[:, lanes] = pooled[ROWS:]


def attend(parts, tables):
    part = pl.BlockSpec((3, BLK, STEP * HD), lambda h: (0, 0, h))
    whole = [pl.BlockSpec(t.shape, lambda h: (0, 0)) for t in tables]
    return pl.pallas_call(
        attend_kernel,
        grid=(HEADS // STEP,),
        out_shape=[jax.ShapeDtypeStruct((ROWS, WIDE), BF16)] * 2,
        in_specs=[part] * NB + whole,
        out_specs=[pl.BlockSpec((ROWS, STEP * HD), lambda h: (0, h))] * 2,
        compiler_params=params(56),
        cost_estimate=cost(6),
        name="attend",
    )(*parts, *tables)


def project_kernel(scal_ref, *refs):
    w_ref, got_ref, mine_ref, send_ref = refs[-4:]
    rows = jnp.concatenate([ref[...] for ref in refs[:-4]], axis=0)
    mine_ref[...] = jnp.dot(rows, w_ref[0], preferred_element_type=F32)
    send_ref[...] = jnp.dot(rows, got_ref[...], preferred_element_type=F32)


def project(scal, shards, cols, got):
    n = len(shards)
    shape = jax.ShapeDtypeStruct((n * ROWS, 4 * HD), F32)
    col = pl.BlockSpec((HALF, HD), lambda j, _: (0, j))
    out = pl.BlockSpec((n * ROWS, HD), lambda j, _: (0, j))
    return pl.pallas_call(
        project_kernel,
        out_shape=[shape] * 2,
        grid_spec=pltpu.PrefetchScalarGridSpec(
            num_scalar_prefetch=1,
            grid=(4,),
            in_specs=[pl.BlockSpec((ROWS, HALF), lambda j, _: (0, 0))] * n
            + [pl.BlockSpec((1, HALF, HD), lambda j, s: (s[1], 0, j)), col],
            out_specs=[out, out],
        ),
        compiler_params=params(24),
        cost_estimate=cost(4),
        name="project",
    )(scal, *shards, cols, got)


def join_kernel(mine_ref, got_ref, *out_refs):
    for k, ref in enumerate(out_refs):
        lanes = slice(k * HD, (k + 1) * HD)
        ref[...] = (mine_ref[:, lanes] + got_ref[:, lanes]).astype(BF16)


def join(mine, got):
    return pl.pallas_call(
        join_kernel,
        out_shape=[jax.ShapeDtypeStruct((mine.shape[0], HD), BF16)] * 4,
        in_specs=[vmem(), vmem()],
        out_specs=[vmem()] * 4,
        compiler_params=params(16),
        cost_estimate=cost(1),
        name="join",
    )(mine, got)


def index_kernel(scal_ref, pos_ref, to_ref, from_ref):
    group = scal_ref[2]
    i = lax.broadcasted_iota(I32, (GPOOL, GPOOL), 0)
    j = lax.broadcasted_iota(I32, (GPOOL, GPOOL), 1)
    before = jnp.where(i < j, 1.0, 0.0).astype(BF16)
    own = pos_ref[pl.ds(group, 1), :] // GPOOL
    hot = (own == lax.broadcasted_iota(I32, (GROUPS, GPOOL), 0)).astype(F32)
    count = jnp.dot(hot.astype(BF16), before, preferred_element_type=F32)
    rank = jnp.sum(hot * count, axis=0, keepdims=True)
    to_ref[...] = own * CAP + rank.astype(I32)
    pos = pos_ref[...]
    here = pos // GPOOL == group
    rank = jnp.dot(here.astype(F32).astype(BF16), before, preferred_element_type=F32).astype(I32)
    rank = jnp.where(here, rank, -1)
    local = pos % GPOOL + 1
    high = (local // 32).astype(F32)
    low = (local % 32).astype(F32)
    r = lax.broadcasted_iota(I32, (CAP, GPOOL), 0)
    for g in range(GROUPS):
        pick = (rank[g : g + 1] == r).astype(F32).astype(BF16)
        pair = jnp.concatenate([high[g : g + 1], low[g : g + 1], jnp.zeros((6, GPOOL), F32)], axis=0)
        got = lax.dot_general(pair.astype(BF16), pick, (((1,), (1,)), ((), ())), preferred_element_type=F32)
        value = got[0:1] * 32.0 + got[1:2] - 1.0
        from_ref[:, g * CAP : (g + 1) * CAP] = value.astype(I32)


def pack_kernel(scal_ref, to_ref, *refs):
    chip = scal_ref[0] // 2
    out_ref, all_ref = refs[-2:]
    for refs_k, shards in ((refs[:4], FIRST), (refs[4:8], SECOND)):
        for k, ref in enumerate(refs_k):
            for i, off in enumerate(shards):
                row = ((chip - 4 * k + off + 2 * CHIPS) % CHIPS) * ROWS
                all_ref[pl.ds(pl.multiple_of(row, ROWS), ROWS), :] = ref[i * ROWS : (i + 1) * ROWS, :]
    rows = 256
    for i in range(GROUPS * CAP // rows):
        r = i * rows + lax.broadcasted_iota(I32, (rows, GPOOL), 0)
        pick = jnp.where(to_ref[...] == r, 1.0, 0.0).astype(BF16)
        out_ref[i * rows : (i + 1) * rows, :] = jnp.dot(pick, all_ref[...], preferred_element_type=F32).astype(BF16)


def place_kernel(from_ref, got_ref, out_ref):
    rows = 256
    for i in range(GPOOL // rows):
        r = i * rows + lax.broadcasted_iota(I32, (rows, GROUPS * CAP), 0)
        pick = jnp.where(from_ref[...] == r, 1.0, 0.0).astype(BF16)
        out_ref[i * rows : (i + 1) * rows, :] = jnp.dot(pick, got_ref[...], preferred_element_type=F32).astype(BF16)


def body(queries, keys, values, gamma, w_merge, grids, positions):
    me = lax.axis_index("mlp")
    core = me % 2
    scal = jnp.stack([me, core, lax.axis_index("grp"), me]).astype(I32)
    shape = jax.ShapeDtypeStruct

    def move(x, perm):
        return lax.ppermute(x, "mlp", perm)

    cols = jnp.concatenate([w_merge] + [move(w_merge, jump(-4 * k)) for k in (1, 2, 3)], axis=1)
    cols = lax.all_gather(cols, "grp", axis=0, tiled=True).reshape(2, HALF, 4 * HD)

    parts = []
    for chunk in range(CHUNKS):
        own, oth = rope(scal, grids, queries, keys, values, chunk)
        parts.append([own, move(oth, PART), move(own, SAME), move(oth, OPP)])

    tables = pl.pallas_call(
        layout_kernel,
        out_shape=[shape((NB * BLK, HD), BF16)] * 2 + [shape((2 * ROWS, NB * BLK), BF16)],
        in_specs=[smem(), smem()],
        out_specs=[vmem()] * 3,
        compiler_params=params(16),
        name="layout",
    )(scal, grids)
    to, frm = pl.pallas_call(
        index_kernel,
        out_shape=[shape((1, GPOOL), I32), shape((1, GROUPS * CAP), I32)],
        in_specs=[smem(), vmem()],
        out_specs=[vmem(), vmem()],
        compiler_params=params(24),
        name="index",
    )(scal, positions.reshape(GROUPS, GPOOL))
    owns, tables, to, frm = lax.optimization_barrier(([p[0] for p in parts], tables, to, frm))
    gains = jnp.broadcast_to(gamma[None, :], (2 * CHIPS, HD))
    pooled = []
    for chunk in range(CHUNKS):
        mid, edge = attend([owns[chunk]] + parts[chunk][1:], tables)
        edge = move(edge, RING)
        pooled.append((mid, edge))
        if chunk == 0:
            gains, _ = lax.optimization_barrier((gains, mid))
            gains = lax.all_to_all(gains, "mlp", split_axis=0, concat_axis=0, tiled=True)
            gains = lax.dynamic_slice_in_dim(gains, core * CHIPS, CHIPS, 0).reshape(1, HALF).astype(F32)
        tables, _ = lax.optimization_barrier((tables, edge))
    rows = jnp.concatenate([mid + edge for mid, edge in pooled], axis=1)
    rows = (rows.astype(F32) * gains).astype(BF16)
    below = move(rows, UP)
    above = move(rows, DOWN)
    last = move(below, UP)
    cols, _ = lax.optimization_barrier((cols, (below, above)))
    cols_got = move(lax.dynamic_index_in_dim(cols, 1 - core, 0, keepdims=False), PART)

    pieces = []
    for shards in ((below, rows, above), (last,)):
        mine, send = project(scal, shards, cols, cols_got)
        blocks = join(mine, move(send, PART))
        pieces += [blocks[0]] + [move(blocks[k], jump(4 * k)) for k in (1, 2, 3)]

    out = pl.pallas_call(
        pack_kernel,
        out_shape=shape((GROUPS * CAP, HD), BF16),
        in_specs=[smem()] + [vmem()] * (1 + len(pieces)),
        out_specs=vmem(),
        scratch_shapes=[pltpu.VMEM((GPOOL, HD), BF16)],
        compiler_params=params(24),
        name="pack",
    )(scal, to, *pieces)
    out = lax.all_to_all(out, "grp", split_axis=0, concat_axis=0, tiled=True)
    return pl.pallas_call(
        place_kernel,
        out_shape=shape((GPOOL, HD), BF16),
        in_specs=[vmem(), vmem()],
        out_specs=vmem(),
        compiler_params=params(24),
        name="place",
    )(frm, out)


def solution(mesh):
    return jax.shard_map(
        body,
        mesh=mesh,
        in_specs=(
            P(("grp", "mlp"), None),
            P(("grp", "mlp"), None),
            P(("grp", "mlp"), None),
            P("mlp"),
            P("grp", "mlp"),
            P("grp", None),
            P(),
        ),
        out_specs=P("grp", "mlp"),
        check_vma=False,
    )
```

time: 224 us -> 217 us (0.969); the launches traced: 223 us -> 214 us
  waiting for transfers between devices: 38.2 us -> 23.5 us
  starting transfers between devices: 105 us -> 110 us
    all_to_all x1, waiting for transfers between devices: 29.7 us -> 0.01 us  [body(): lax.all_to_all(gains, 'mlp', split_axis=0, concat_axis=0, tiled=True)]
    ppermute x24 -> x23, waiting for transfers between devices: 8.47 us -> 23.5 us  [move(): return lax.ppermute(x, 'mlp', perm)]
    ppermute x24 -> x23, starting transfers between devices: 98 us -> 102 us  [move(): return lax.ppermute(x, 'mlp', perm)]
    pallas_call x4 -> x10, Pallas kernels: 36.6 us -> 34.3 us  [the longest x2 14.1 us: attend(): pl.pallas_call(attend_kernel, grid=(HEADS // STEP,), out_shape=[jax.Shape...]
    unnamed x13 -> x27, local copies, waits for them, and re-layouts: 5.14 us -> 6.25 us
  transfers between devices with their start and end apart: 26 -> 25, of which waited for: 9 -> 8; matrix products, arithmetic and copies ran while one was open for 2% -> 2% of each run, Pallas kernels for 12% -> 16%
where the time goes in v2:
time: 217 us; the launch traced here: 214 us
  starting transfers between devices  110 us (51%)
  Pallas kernels  38.5 us (18%)
  waiting for transfers between devices  23.5 us (11%)
  blocking collectives  15.5 us (7%)
  between operations  13.9 us (6%)
  local copies, waits for them, and re-layouts  8.77 us (4%)
  other arithmetic  3.23 us (1%)
    ppermute x23, starting transfers between devices, move(): return lax.ppermute(x, 'mlp', perm)  102 us
    ppermute x23, waiting for transfers between devices, move(): return lax.ppermute(x, 'mlp', perm)  23.5 us
    all_to_all x1, blocking collectives, body(): out = lax.all_to_all(out, 'grp', split_axis=0, concat_axis=0, tiled=True)  15.5 us
    pallas_call x2, Pallas kernels, attend(): pl.pallas_call(attend_kernel, grid=(HEADS // STEP,), out_shape=[jax.Shape...  14.1 us
    pallas_call x2, Pallas kernels, rope(): pl.pallas_call(rope_kernel, out_shape=[jax.ShapeDtypeStruct((3, BLK, WIDE...  10.9 us
    all_to_all x1, starting transfers between devices, body(): lax.all_to_all(gains, 'mlp', split_axis=0, concat_axis=0, tiled=True)  8.36 us
    unnamed x27, local copies, waits for them, and re-layouts  6.25 us
    pallas_call x2, Pallas kernels, project(): pl.pallas_call(project_kernel, out_shape=[shape] * 2, grid_spec=pltpu.Pre...  6.24 us
  transfers between devices with their start and end apart: 25, of which 8 were waited for; matrix products, arithmetic and copies ran while one was open for 2% of the time, Pallas kernels for 16%

profile of v2, /device:TPU:1, one launch (start us, length us, event | category | flops | bytes accessed | tf_op | source)
XLA Modules:
  0.0 213.8 jit_solution(8193711225906492028)
XLA Ops:
  6.5 9.6 %collective-permute-start.12 = (bf16[256,128]{1,0:T(8,128)(2,1)}, bf16[256,128]{1,0:T(8,128)(2,1)S(1)}, u32[]{:S(2)}, u32[]{:S(2)}) collective-permute-start(bf16[256,128]{1,0:T(8,128)(2,1)} %param.11), channel_id=1, source_target_pairs={{0,8},{1,9},{2,10},{3,11},{4,12},{5,13},{6,14},{7,15},{8,16},{9,17... | collective-permute-start | bytes 196616 | tf_op jit(solution)/shard_map/ppermute | solution.py:339
  16.2 10.6 %collective-permute-start.11 = (bf16[256,128]{1,0:T(8,128)(2,1)}, bf16[256,128]{1,0:T(8,128)(2,1)S(1)}, u32[]{:S(2)}, u32[]{:S(2)}) collective-permute-start(bf16[256,128]{1,0:T(8,128)(2,1)} %param.11), channel_id=1, source_target_pairs={{0,16},{1,17},{2,18},{3,19},{4,20},{5,21},{6,22},{7,23},{8,24},{9,... | collective-permute-start | bytes 196616 | tf_op jit(solution)/shard_map/ppermute | solution.py:339
  26.8 5.2 %collective-permute-start.10 = (bf16[256,128]{1,0:T(8,128)(2,1)}, bf16[256,128]{1,0:T(8,128)(2,1)S(1)}, u32[]{:S(2)}, u32[]{:S(2)}) collective-permute-start(bf16[256,128]{1,0:T(8,128)(2,1)} %param.11), channel_id=1, source_target_pairs={{0,24},{1,25},{2,26},{3,27},{4,28},{5,29},{6,30},{7,31},{8,0},{9,1... | collective-permute-start | bytes 196616 | tf_op jit(solution)/shard_map/ppermute | solution.py:339
  34.2 6.9 %collective-permute-done.10 = bf16[256,128]{1,0:T(8,128)(2,1)S(1)} collective-permute-done((bf16[256,128]{1,0:T(8,128)(2,1)}, bf16[256,128]{1,0:T(8,128)(2,1)S(1)}, u32[]{:S(2)}, u32[]{:S(2)}) %collective-permute-start.10) | collective-permute-done | bytes 65568 | tf_op jit(solution)/shard_map/ppermute | solution.py:339
  44.7 5.4 %rope.2 = (bf16[3,128,1024]{2,1,0:T(8,128)(2,1)}, bf16[3,128,1024]{2,1,0:T(8,128)(2,1)}) custom-call(s32[4]{0:T(128)} %pad_add_fusion.scal_ref, s32[16,2]{1,0:T(8,128)} %copy.14.grid_ref, bf16[128,4096]{1,0:T(8,128)(2,1)} %q_ref.3, bf16[128,4096]{1,0:T(8,128)(2,1)} %k_ref.3, bf16[128,4096]{1,0:T(8,128)(2,1)} %v_ref.3), custom_call_target="tpu_custom_call" | custom-call | flops 4600000000 | bytes 14000000 | tf_op jit(solution)/shard_map/rope/pallas_call | solution.py:135
  54.6 4.0 %collective-permute-start.2 = (bf16[3,128,1024]{2,1,0:T(8,128)(2,1)}, bf16[3,128,1024]{2,1,0:T(8,128)(2,1)}, u32[]{:S(2)}, u32[]{:S(2)}) collective-permute-start(bf16[3,128,1024]{2,1,0:T(8,128)(2,1)} %get-tuple-element.52), channel_id=1, source_target_pairs={{1,30},{3,0},{5,2},{7,4},{9,6},{11,8},{13,10},{15,12},{17,14},{19,... | collective-permute-start | bytes 2359304 | tf_op jit(solution)/shard_map/ppermute | solution.py:339
  58.6 5.5 %rope.3 = (bf16[3,128,1024]{2,1,0:T(8,128)(2,1)}, bf16[3,128,1024]{2,1,0:T(8,128)(2,1)}) custom-call(s32[4]{0:T(128)} %pad_add_fusion.scal_ref, s32[16,2]{1,0:T(8,128)} %copy.14.grid_ref, bf16[128,4096]{1,0:T(8,128)(2,1)} %q_ref.3, bf16[128,4096]{1,0:T(8,128)(2,1)} %k_ref.3, bf16[128,4096]{1,0:T(8,128)(2,1)} %v_ref.3), custom_call_target="tpu_custom_call" | custom-call | flops 4600000000 | bytes 14000000 | tf_op jit(solution)/shard_map/rope/pallas_call | solution.py:135
  69.2 5.1 %collective-permute-start.6 = (bf16[3,128,1024]{2,1,0:T(8,128)(2,1)}, bf16[3,128,1024]{2,1,0:T(8,128)(2,1)S(1)}, u32[]{:S(2)}, u32[]{:S(2)}) collective-permute-start(bf16[3,128,1024]{2,1,0:T(8,128)(2,1)} %get-tuple-element.59), channel_id=1, source_target_pairs={{1,30},{3,0},{5,2},{7,4},{9,6},{11,8},{13,10},{15,12},{17,14},{19,... | collective-permute-start | bytes 2359304 | tf_op jit(solution)/shard_map/ppermute | solution.py:339
  79.8 7.1 %attend.2 = (bf16[64,1024]{1,0:T(8,128)(2,1)}, bf16[64,1024]{1,0:T(8,128)(2,1)}) custom-call(bf16[3,128,1024]{2,1,0:T(8,128)(2,1)} %get-tuple-element.51.a_ref, bf16[3,128,1024]{2,1,0:T(8,128)(2,1)} %copy-done.12, bf16[3,128,1024]{2,1,0:T(8,128)(2,1)} %collective-permute-done.1.c_ref, bf16[3,128,1024]{2,1,0:T(8,128)(2,1)} %collective-permute-done.2.d_ref, ...), custom_call_target="tpu_custom_call" | custom-call | flops 6899999744 | bytes 21000000 | tf_op jit(solution)/shard_map/attend/pallas_call | solution.py:225
  89.4 8.4 %all-to-all-start = ((bf16[32,1,128]{2,1,0:T(2,128)(2,1)}), bf16[32,1,128]{2,1,0:T(2,128)(2,1)S(1)}, u32[]{:S(2)}, u32[]{:S(2)}) async-start(bf16[32,1,128]{2,1,0:T(2,128)(2,1)} %copy.17), calls=%async_computation | async-start | bytes 32768 | tf_op jit(solution)/shard_map/all_to_all | solution.py:374
  99.9 7.0 %attend.3 = (bf16[64,1024]{1,0:T(8,128)(2,1)}, bf16[64,1024]{1,0:T(8,128)(2,1)}) custom-call(bf16[3,128,1024]{2,1,0:T(8,128)(2,1)} %get-tuple-element.58.a_ref, bf16[3,128,1024]{2,1,0:T(8,128)(2,1)} %copy-done.9, bf16[3,128,1024]{2,1,0:T(8,128)(2,1)} %copy-done.10, bf16[3,128,1024]{2,1,0:T(8,128)(2,1)} %copy-done.11, bf16[512,128]{1,0:T(8,128)(2,1)} %copy-done.3, ...), custom_call_target="tpu_custom_call" | custom-call | flops 6899999744 | bytes 21000000 | tf_op jit(solution)/shard_map/attend/pallas_call | solution.py:225
  106.9 4.6 %collective-permute-start.7 = (bf16[64,1024]{1,0:T(8,128)(2,1)}, bf16[64,1024]{1,0:T(8,128)(2,1)S(1)}, u32[]{:S(2)}, u32[]{:S(2)}) collective-permute-start(bf16[64,1024]{1,0:T(8,128)(2,1)} %get-tuple-element.64), channel_id=1, source_target_pairs={{0,2},{2,4},{4,6},{6,8},{8,10},{10,12},{12,14},{14,16},{16,18},{18... | collective-permute-start | bytes 393224 | tf_op jit(solution)/shard_map/ppermute | solution.py:339
  117.4 4.2 %collective-permute-start.9 = (bf16[64,2048]{1,0:T(8,128)(2,1)S(1)}, bf16[64,2048]{1,0:T(8,128)(2,1)S(1)}, u32[]{:S(2)}, u32[]{:S(2)}) collective-permute-start(bf16[64,2048]{1,0:T(8,128)(2,1)S(1)} %multiply_convert_fusion.refs_1_), channel_id=1, source_target_pairs={{0,30},{1,31},{2,0},{3,1},{4,2},{5,3},{6,4},{7,5},{8,6},{9,7},{10,... | collective-permute-start | bytes 786440 | tf_op jit(solution)/shard_map/ppermute | solution.py:339
  121.6 3.0 %collective-permute-done.8.refs_0_ = bf16[64,2048]{1,0:T(8,128)(2,1)S(1)} collective-permute-done((bf16[64,2048]{1,0:T(8,128)(2,1)S(1)}, bf16[64,2048]{1,0:T(8,128)(2,1)S(1)}, u32[]{:S(2)}, u32[]{:S(2)}) %collective-permute-start.8) | collective-permute-done | bytes 262176 | tf_op jit(solution)/shard_map/ppermute | solution.py:339
  127.4 4.4 %collective-permute-start.13 = (bf16[2048,512]{1,0:T(8,128)(2,1)S(1)}, bf16[2048,512]{1,0:T(8,128)(2,1)S(1)}, u32[]{:S(2)}, u32[]{:S(2)}) collective-permute-start(bf16[2048,512]{1,0:T(8,128)(2,1)S(1)} %dynamic-slice_bitcast_fusion), channel_id=1, source_target_pairs={{0,1},{1,0},{2,3},{3,2},{4,5},{5,4},{6,7},{7,6},{8,9},{9,8},{10,11... | collective-permute-start | bytes 6291464 | tf_op jit(solution)/shard_map/ppermute | solution.py:339
  131.9 3.7 %collective-permute-start.18 = (bf16[64,2048]{1,0:T(8,128)(2,1)S(1)}, bf16[64,2048]{1,0:T(8,128)(2,1)S(1)}, u32[]{:S(2)}, u32[]{:S(2)}) collective-permute-start(bf16[64,2048]{1,0:T(8,128)(2,1)S(1)} %collective-permute-done.8.refs_0_), channel_id=1, source_target_pairs={{0,2},{1,3},{2,4},{3,5},{4,6},{5,7},{6,8},{7,9},{8,10},{9,11},{10,... | collective-permute-start | bytes 786440 | tf_op jit(solution)/shard_map/ppermute | solution.py:339
  135.6 3.7 %project.2 = (f32[192,512]{1,0:T(8,128)S(1)}, f32[192,512]{1,0:T(8,128)S(1)}) custom-call(s32[4]{0:T(128)S(1)} %copy-done.2, bf16[64,2048]{1,0:T(8,128)(2,1)S(1)} %collective-permute-done.8.refs_0_, bf16[64,2048]{1,0:T(8,128)(2,1)S(1)} %multiply_convert_fusion.refs_1_, bf16[64,2048]{1,0:T(8,128)(2,1)S(1)} %collective-permute-done.9.refs_2_, ...), custom_call_target="tpu_custom_call" | custom-call | flops 4600000000 | bytes 14000000 | tf_op jit(solution)/shard_map/project/pallas_call | solution.py:249
  146.4 2.7 %collective-permute-start.19 = (f32[64,512]{1,0:T(8,128)S(1)}, f32[64,512]{1,0:T(8,128)S(1)}, u32[]{:S(2)}, u32[]{:S(2)}) collective-permute-start(f32[64,512]{1,0:T(8,128)S(1)} %get-tuple-element.74), channel_id=1, source_target_pairs={{0,1},{1,0},{2,3},{3,2},{4,5},{5,4},{6,7},{7,6},{8,9},{9,8},{10,11... | collective-permute-start | bytes 393224 | tf_op jit(solution)/shard_map/ppermute | solution.py:339
  149.2 6.7 %collective-permute-start.15 = (bf16[192,128]{1,0:T(8,128)(2,1)S(1)}, bf16[192,128]{1,0:T(8,128)(2,1)S(1)}, u32[]{:S(2)}, u32[]{:S(2)}) collective-permute-start(bf16[192,128]{1,0:T(8,128)(2,1)S(1)} %get-tuple-element.70), channel_id=1, source_target_pairs={{0,8},{1,9},{2,10},{3,11},{4,12},{5,13},{6,14},{7,15},{8,16},{9,17... | collective-permute-start | bytes 147464 | tf_op jit(solution)/shard_map/ppermute | solution.py:339
  155.9 7.3 %collective-permute-start.16 = (bf16[192,128]{1,0:T(8,128)(2,1)S(1)}, bf16[192,128]{1,0:T(8,128)(2,1)S(1)}, u32[]{:S(2)}, u32[]{:S(2)}) collective-permute-start(bf16[192,128]{1,0:T(8,128)(2,1)S(1)} %get-tuple-element.71), channel_id=1, source_target_pairs={{0,16},{1,17},{2,18},{3,19},{4,20},{5,21},{6,22},{7,23},{8,24},{9,... | collective-permute-start | bytes 147464 | tf_op jit(solution)/shard_map/ppermute | solution.py:339
  163.2 6.6 %collective-permute-start.17 = (bf16[192,128]{1,0:T(8,128)(2,1)S(1)}, bf16[192,128]{1,0:T(8,128)(2,1)S(1)}, u32[]{:S(2)}, u32[]{:S(2)}) collective-permute-start(bf16[192,128]{1,0:T(8,128)(2,1)S(1)} %get-tuple-element.72), channel_id=1, source_target_pairs={{0,24},{1,25},{2,26},{3,27},{4,28},{5,29},{6,30},{7,31},{8,0},{9,1... | collective-permute-start | bytes 147464 | tf_op jit(solution)/shard_map/ppermute | solution.py:339
  172.4 6.7 %collective-permute-start.21 = (bf16[64,128]{1,0:T(8,128)(2,1)S(1)}, bf16[64,128]{1,0:T(8,128)(2,1)S(1)}, u32[]{:S(2)}, u32[]{:S(2)}) collective-permute-start(bf16[64,128]{1,0:T(8,128)(2,1)S(1)} %get-tuple-element.77), channel_id=1, source_target_pairs={{0,16},{1,17},{2,18},{3,19},{4,20},{5,21},{6,22},{7,23},{8,24},{9,... | collective-permute-start | bytes 49160 | tf_op jit(solution)/shard_map/ppermute | solution.py:339
  181.7 4.0 %collective-permute-done.21.refs_6_ = bf16[64,128]{1,0:T(8,128)(2,1)S(1)} collective-permute-done((bf16[64,128]{1,0:T(8,128)(2,1)S(1)}, bf16[64,128]{1,0:T(8,128)(2,1)S(1)}, u32[]{:S(2)}, u32[]{:S(2)}) %collective-permute-start.21) | collective-permute-done | bytes 16416 | tf_op jit(solution)/shard_map/ppermute | solution.py:339
  189.5 15.5 %all_to_all.20 = bf16[16,128,128]{2,1,0:T(8,128)(2,1)S(1)} all-to-all(bf16[16,128,128]{2,1,0:T(8,128)(2,1)S(1)} %bitcast.10), channel_id=1, replica_groups=mesh['grp'=16,'mlp'=32] {'grp'}, dimensions={0} | all-to-all | bytes 1048576 | tf_op jit(solution)/shard_map/all_to_all | solution.py:400
  (77 shorter events, 52.0 us)
Async XLA Ops:
  6.5 119.0 %all-gather.2.cloned.1.call-start = ((), (), s32[]{:S(2)}) async-start(), calls=%async_computation.2 | async-start | bytes 4456448 | tf_op jit(solution)/shard_map/all_gather | solution.py:342
  6.5 25.5 %collective-permute-start.12 = (bf16[256,128]{1,0:T(8,128)(2,1)}, bf16[256,128]{1,0:T(8,128)(2,1)S(1)}, u32[]{:S(2)}, u32[]{:S(2)}) collective-permute-start(bf16[256,128]{1,0:T(8,128)(2,1)} %param.11), channel_id=1, source_target_pairs={{0,8},{1,9},{2,10},{3,11},{4,12},{5,13},{6,14},{7,15},{8,16},{9,17... | collective-permute-start | bytes 196616 | tf_op jit(solution)/shard_map/ppermute | solution.py:339
  16.2 18.0 %collective-permute-start.11 = (bf16[256,128]{1,0:T(8,128)(2,1)}, bf16[256,128]{1,0:T(8,128)(2,1)S(1)}, u32[]{:S(2)}, u32[]{:S(2)}) collective-permute-start(bf16[256,128]{1,0:T(8,128)(2,1)} %param.11), channel_id=1, source_target_pairs={{0,16},{1,17},{2,18},{3,19},{4,20},{5,21},{6,22},{7,23},{8,24},{9,... | collective-permute-start | bytes 196616 | tf_op jit(solution)/shard_map/ppermute | solution.py:339
  26.8 14.3 %collective-permute-start.10 = (bf16[256,128]{1,0:T(8,128)(2,1)}, bf16[256,128]{1,0:T(8,128)(2,1)S(1)}, u32[]{:S(2)}, u32[]{:S(2)}) collective-permute-start(bf16[256,128]{1,0:T(8,128)(2,1)} %param.11), channel_id=1, source_target_pairs={{0,24},{1,25},{2,26},{3,27},{4,28},{5,29},{6,30},{7,31},{8,0},{9,1... | collective-permute-start | bytes 196616 | tf_op jit(solution)/shard_map/ppermute | solution.py:339
  50.1 18.3 %collective-permute-start = (bf16[3,128,1024]{2,1,0:T(8,128)(2,1)}, bf16[3,128,1024]{2,1,0:T(8,128)(2,1)S(1)}, u32[]{:S(2)}, u32[]{:S(2)}) collective-permute-start(bf16[3,128,1024]{2,1,0:T(8,128)(2,1)} %get-tuple-element.52), channel_id=1, source_target_pairs={{0,1},{1,0},{2,3},{3,2},{4,5},{5,4},{6,7},{7,6},{8,9},{9,8},{10,11... | collective-permute-start | bytes 2359304 | tf_op jit(solution)/shard_map/ppermute | solution.py:339
  52.5 27.3 %collective-permute-start.1 = (bf16[3,128,1024]{2,1,0:T(8,128)(2,1)}, bf16[3,128,1024]{2,1,0:T(8,128)(2,1)}, u32[]{:S(2)}, u32[]{:S(2)}) collective-permute-start(bf16[3,128,1024]{2,1,0:T(8,128)(2,1)} %get-tuple-element.51.a_ref), channel_id=1, source_target_pairs={{0,30},{2,0},{4,2},{6,4},{8,6},{10,8},{12,10},{14,12},{16,14},{18,... | collective-permute-start | bytes 2359304 | tf_op jit(solution)/shard_map/ppermute | solution.py:339
  54.6 25.2 %collective-permute-start.2 = (bf16[3,128,1024]{2,1,0:T(8,128)(2,1)}, bf16[3,128,1024]{2,1,0:T(8,128)(2,1)}, u32[]{:S(2)}, u32[]{:S(2)}) collective-permute-start(bf16[3,128,1024]{2,1,0:T(8,128)(2,1)} %get-tuple-element.52), channel_id=1, source_target_pairs={{1,30},{3,0},{5,2},{7,4},{9,6},{11,8},{13,10},{15,12},{17,14},{19,... | collective-permute-start | bytes 2359304 | tf_op jit(solution)/shard_map/ppermute | solution.py:339
  64.1 33.7 %collective-permute-start.4 = (bf16[3,128,1024]{2,1,0:T(8,128)(2,1)}, bf16[3,128,1024]{2,1,0:T(8,128)(2,1)S(1)}, u32[]{:S(2)}, u32[]{:S(2)}) collective-permute-start(bf16[3,128,1024]{2,1,0:T(8,128)(2,1)} %get-tuple-element.59), channel_id=1, source_target_pairs={{0,1},{1,0},{2,3},{3,2},{4,5},{5,4},{6,7},{7,6},{8,9},{9,8},{10,11... | collective-permute-start | bytes 2359304 | tf_op jit(solution)/shard_map/ppermute | solution.py:339
  66.4 31.4 %collective-permute-start.5 = (bf16[3,128,1024]{2,1,0:T(8,128)(2,1)}, bf16[3,128,1024]{2,1,0:T(8,128)(2,1)S(1)}, u32[]{:S(2)}, u32[]{:S(2)}) collective-permute-start(bf16[3,128,1024]{2,1,0:T(8,128)(2,1)} %get-tuple-element.58.a_ref), channel_id=1, source_target_pairs={{0,30},{2,0},{4,2},{6,4},{8,6},{10,8},{12,10},{14,12},{16,14},{18,... | collective-permute-start | bytes 2359304 | tf_op jit(solution)/shard_map/ppermute | solution.py:339
  69.2 28.6 %collective-permute-start.6 = (bf16[3,128,1024]{2,1,0:T(8,128)(2,1)}, bf16[3,128,1024]{2,1,0:T(8,128)(2,1)S(1)}, u32[]{:S(2)}, u32[]{:S(2)}) collective-permute-start(bf16[3,128,1024]{2,1,0:T(8,128)(2,1)} %get-tuple-element.59), channel_id=1, source_target_pairs={{1,30},{3,0},{5,2},{7,4},{9,6},{11,8},{13,10},{15,12},{17,14},{19,... | collective-permute-start | bytes 2359304 | tf_op jit(solution)/shard_map/ppermute | solution.py:339
  86.8 10.9 %collective-permute-start.3 = (bf16[64,1024]{1,0:T(8,128)(2,1)}, bf16[64,1024]{1,0:T(8,128)(2,1)S(1)}, u32[]{:S(2)}, u32[]{:S(2)}) collective-permute-start(bf16[64,1024]{1,0:T(8,128)(2,1)} %get-tuple-element.57), channel_id=1, source_target_pairs={{0,2},{2,4},{4,6},{6,8},{8,10},{10,12},{12,14},{14,16},{16,18},{18... | collective-permute-start | bytes 393224 | tf_op jit(solution)/shard_map/ppermute | solution.py:339
  89.4 22.1 %all-to-all-start = ((bf16[32,1,128]{2,1,0:T(2,128)(2,1)}), bf16[32,1,128]{2,1,0:T(2,128)(2,1)S(1)}, u32[]{:S(2)}, u32[]{:S(2)}) async-start(bf16[32,1,128]{2,1,0:T(2,128)(2,1)} %copy.17), calls=%async_computation | async-start | bytes 32768 | tf_op jit(solution)/shard_map/all_to_all | solution.py:374
  114.7 9.8 %collective-permute-start.8 = (bf16[64,2048]{1,0:T(8,128)(2,1)S(1)}, bf16[64,2048]{1,0:T(8,128)(2,1)S(1)}, u32[]{:S(2)}, u32[]{:S(2)}) collective-permute-start(bf16[64,2048]{1,0:T(8,128)(2,1)S(1)} %multiply_convert_fusion.refs_1_), channel_id=1, source_target_pairs={{0,2},{1,3},{2,4},{3,5},{4,6},{5,7},{6,8},{7,9},{8,10},{9,11},{10,... | collective-permute-start | bytes 786440 | tf_op jit(solution)/shard_map/ppermute | solution.py:339
  117.4 8.1 %collective-permute-start.9 = (bf16[64,2048]{1,0:T(8,128)(2,1)S(1)}, bf16[64,2048]{1,0:T(8,128)(2,1)S(1)}, u32[]{:S(2)}, u32[]{:S(2)}) collective-permute-start(bf16[64,2048]{1,0:T(8,128)(2,1)S(1)} %multiply_convert_fusion.refs_1_), channel_id=1, source_target_pairs={{0,30},{1,31},{2,0},{3,1},{4,2},{5,3},{6,4},{7,5},{8,6},{9,7},{10,... | collective-permute-start | bytes 786440 | tf_op jit(solution)/shard_map/ppermute | solution.py:339
  127.4 8.2 %collective-permute-start.13 = (bf16[2048,512]{1,0:T(8,128)(2,1)S(1)}, bf16[2048,512]{1,0:T(8,128)(2,1)S(1)}, u32[]{:S(2)}, u32[]{:S(2)}) collective-permute-start(bf16[2048,512]{1,0:T(8,128)(2,1)S(1)} %dynamic-slice_bitcast_fusion), channel_id=1, source_target_pairs={{0,1},{1,0},{2,3},{3,2},{4,5},{5,4},{6,7},{7,6},{8,9},{9,8},{10,11... | collective-permute-start | bytes 6291464 | tf_op jit(solution)/shard_map/ppermute | solution.py:339
  131.9 12.0 %collective-permute-start.18 = (bf16[64,2048]{1,0:T(8,128)(2,1)S(1)}, bf16[64,2048]{1,0:T(8,128)(2,1)S(1)}, u32[]{:S(2)}, u32[]{:S(2)}) collective-permute-start(bf16[64,2048]{1,0:T(8,128)(2,1)S(1)} %collective-permute-done.8.refs_0_), channel_id=1, source_target_pairs={{0,2},{1,3},{2,4},{3,5},{4,6},{5,7},{6,8},{7,9},{8,10},{9,11},{10,... | collective-permute-start | bytes 786440 | tf_op jit(solution)/shard_map/ppermute | solution.py:339
  139.3 9.8 %collective-permute-start.14 = (f32[192,512]{1,0:T(8,128)S(1)}, f32[192,512]{1,0:T(8,128)S(1)}, u32[]{:S(2)}, u32[]{:S(2)}) collective-permute-start(f32[192,512]{1,0:T(8,128)S(1)} %get-tuple-element.68), channel_id=1, source_target_pairs={{0,1},{1,0},{2,3},{3,2},{4,5},{5,4},{6,7},{7,6},{8,9},{9,8},{10,11... | collective-permute-start | bytes 1179656 | tf_op jit(solution)/shard_map/ppermute | solution.py:339
  146.4 23.4 %collective-permute-start.19 = (f32[64,512]{1,0:T(8,128)S(1)}, f32[64,512]{1,0:T(8,128)S(1)}, u32[]{:S(2)}, u32[]{:S(2)}) collective-permute-start(f32[64,512]{1,0:T(8,128)S(1)} %get-tuple-element.74), channel_id=1, source_target_pairs={{0,1},{1,0},{2,3},{3,2},{4,5},{5,4},{6,7},{7,6},{8,9},{9,8},{10,11... | collective-permute-start | bytes 393224 | tf_op jit(solution)/shard_map/ppermute | solution.py:339
  149.2 38.4 %collective-permute-start.15 = (bf16[192,128]{1,0:T(8,128)(2,1)S(1)}, bf16[192,128]{1,0:T(8,128)(2,1)S(1)}, u32[]{:S(2)}, u32[]{:S(2)}) collective-permute-start(bf16[192,128]{1,0:T(8,128)(2,1)S(1)} %get-tuple-element.70), channel_id=1, source_target_pairs={{0,8},{1,9},{2,10},{3,11},{4,12},{5,13},{6,14},{7,15},{8,16},{9,17... | collective-permute-start | bytes 147464 | tf_op jit(solution)/shard_map/ppermute | solution.py:339
  155.9 31.8 %collective-permute-start.16 = (bf16[192,128]{1,0:T(8,128)(2,1)S(1)}, bf16[192,128]{1,0:T(8,128)(2,1)S(1)}, u32[]{:S(2)}, u32[]{:S(2)}) collective-permute-start(bf16[192,128]{1,0:T(8,128)(2,1)S(1)} %get-tuple-element.71), channel_id=1, source_target_pairs={{0,16},{1,17},{2,18},{3,19},{4,20},{5,21},{6,22},{7,23},{8,24},{9,... | collective-permute-start | bytes 147464 | tf_op jit(solution)/shard_map/ppermute | solution.py:339
  163.2 24.5 %collective-permute-start.17 = (bf16[192,128]{1,0:T(8,128)(2,1)S(1)}, bf16[192,128]{1,0:T(8,128)(2,1)S(1)}, u32[]{:S(2)}, u32[]{:S(2)}) collective-permute-start(bf16[192,128]{1,0:T(8,128)(2,1)S(1)} %get-tuple-element.72), channel_id=1, source_target_pairs={{0,24},{1,25},{2,26},{3,27},{4,28},{5,29},{6,30},{7,31},{8,0},{9,1... | collective-permute-start | bytes 147464 | tf_op jit(solution)/shard_map/ppermute | solution.py:339
  169.9 9.2 %collective-permute-start.20 = (bf16[64,128]{1,0:T(8,128)(2,1)S(1)}, bf16[64,128]{1,0:T(8,128)(2,1)S(1)}, u32[]{:S(2)}, u32[]{:S(2)}) collective-permute-start(bf16[64,128]{1,0:T(8,128)(2,1)S(1)} %get-tuple-element.76), channel_id=1, source_target_pairs={{0,8},{1,9},{2,10},{3,11},{4,12},{5,13},{6,14},{7,15},{8,16},{9,17... | collective-permute-start | bytes 49160 | tf_op jit(solution)/shard_map/ppermute | solution.py:339
  172.4 13.2 %collective-permute-start.21 = (bf16[64,128]{1,0:T(8,128)(2,1)S(1)}, bf16[64,128]{1,0:T(8,128)(2,1)S(1)}, u32[]{:S(2)}, u32[]{:S(2)}) collective-permute-start(bf16[64,128]{1,0:T(8,128)(2,1)S(1)} %get-tuple-element.77), channel_id=1, source_target_pairs={{0,16},{1,17},{2,18},{3,19},{4,20},{5,21},{6,22},{7,23},{8,24},{9,... | collective-permute-start | bytes 49160 | tf_op jit(solution)/shard_map/ppermute | solution.py:339
  179.1 8.5 %collective-permute-start.22 = (bf16[64,128]{1,0:T(8,128)(2,1)S(1)}, bf16[64,128]{1,0:T(8,128)(2,1)S(1)}, u32[]{:S(2)}, u32[]{:S(2)}) collective-permute-start(bf16[64,128]{1,0:T(8,128)(2,1)S(1)} %get-tuple-element.78), channel_id=1, source_target_pairs={{0,24},{1,25},{2,26},{3,27},{4,28},{5,29},{6,30},{7,31},{8,0},{9,1... | collective-permute-start | bytes 49160 | tf_op jit(solution)/shard_map/ppermute | solution.py:339
  (14 other events, 114.4 us)
Sparse Core Ops, SparseCore 0:
  42.8 64.9 all-gather.1

commit v3 on v2

--- a/solution.py
+++ b/solution.py
@@ -25,16 +25,12 @@
 F32 = jnp.float32
 BF16 = jnp.bfloat16
 I32 = jnp.int32
-FIRST = (-1, 0, 1)
-SECOND = (-2,)
+WINDOW = (-1, 0, 1, -2)
+QUADS = 4
 
 
 def at(z, c):
     return (z % CHIPS) * 2 + c
-
-
-def jump(k):
-    return [(at(z, c), at(z + k, c)) for z in range(CHIPS) for c in range(2)]
 
 
 SAME = [(at(z, 0), at(z - 1, 0)) for z in range(CHIPS)] + [(at(z, 1), at(z + 1, 1)) for z in range(CHIPS)]
@@ -42,6 +38,7 @@
 RING = [(at(z, 0), at(z + 1, 0)) for z in range(CHIPS)] + [(at(z, 1), at(z - 1, 1)) for z in range(CHIPS)]
 UP = [(at(z, c), at(z + 1, c)) for z in range(CHIPS) for c in range(2)]
 DOWN = [(at(z, c), at(z - 1, c)) for z in range(CHIPS) for c in range(2)]
+FOURS = [[at(r + QUADS * k, c) for k in range(QUADS)] for r in range(QUADS) for c in range(2)]
 PART = [(at(z, c), at(z, 1 - c)) for z in range(CHIPS) for c in range(2)]
 
 
@@ -235,49 +232,34 @@
 
 
 def project_kernel(scal_ref, *refs):
-    w_ref, got_ref, mine_ref, send_ref = refs[-4:]
-    rows = jnp.concatenate([ref[...] for ref in refs[:-4]], axis=0)
-    mine_ref[...] = jnp.dot(rows, w_ref[0], preferred_element_type=F32)
-    send_ref[...] = jnp.dot(rows, got_ref[...], preferred_element_type=F32)
-
-
-def project(scal, shards, cols, got):
-    n = len(shards)
-    shape = jax.ShapeDtypeStruct((n * ROWS, 4 * HD), F32)
-    col = pl.BlockSpec((HALF, HD), lambda j, _: (0, j))
-    out = pl.BlockSpec((n * ROWS, HD), lambda j, _: (0, j))
+    w_own_ref, w_oth_ref, out_ref = refs[-3:]
+    own = jnp.concatenate([ref[...] for ref in refs[:NB]], axis=0)
+    oth = jnp.concatenate([ref[...] for ref in refs[NB : 2 * NB]], axis=0)
+    total = jnp.dot(own, w_own_ref[...].reshape(HALF, HD), preferred_element_type=F32)
+    total += jnp.dot(oth, w_oth_ref[...].reshape(HALF, HD), preferred_element_type=F32)
+    out_ref[0] = total.astype(BF16)
+
+
+def project(scal, own, oth, cols):
+    rows = NB * ROWS
+    half = (GROUPS // 2, 1, 2 * BLK, HD)
     return pl.pallas_call(
         project_kernel,
-        out_shape=[shape] * 2,
+        out_shape=jax.ShapeDtypeStruct((QUADS, rows, HD), BF16),
         grid_spec=pltpu.PrefetchScalarGridSpec(
             num_scalar_prefetch=1,
-            grid=(4,),
-            in_specs=[pl.BlockSpec((ROWS, HALF), lambda j, _: (0, 0))] * n
-            + [pl.BlockSpec((1, HALF, HD), lambda j, s: (s[1], 0, j)), col],
-            out_specs=[out, out],
+            grid=(QUADS,),
+            in_specs=[pl.BlockSpec((ROWS, HALF), lambda j, _: (0, 0))] * (2 * NB)
+            + [
+                pl.BlockSpec(half, lambda j, s: (s[1], j, 0, 0)),
+                pl.BlockSpec(half, lambda j, s: (1 - s[1], j, 0, 0)),
+            ],
+            out_specs=pl.BlockSpec((1, rows, HD), lambda j, _: (j, 0, 0)),
         ),
         compiler_params=params(24),
         cost_estimate=cost(4),
         name="project",
-    )(scal, *shards, cols, got)
-
-
-def join_kernel(mine_ref, got_ref, *out_refs):
-    for k, ref in enumerate(out_refs):
-        lanes = slice(k * HD, (k + 1) * HD)
-        ref[...] = (mine_ref[:, lanes] + got_ref[:, lanes]).astype(BF16)
-
-
-def join(mine, got):
-    return pl.pallas_call(
-        join_kernel,
-        out_shape=[jax.ShapeDtypeStruct((mine.shape[0], HD), BF16)] * 4,
-        in_specs=[vmem(), vmem()],
-        out_specs=[vmem()] * 4,
-        compiler_params=params(16),
-        cost_estimate=cost(1),
-        name="join",
-    )(mine, got)
+    )(scal, *own, *oth, cols, cols)
 
 
 def index_kernel(scal_ref, pos_ref, to_ref, from_ref):
@@ -306,14 +288,13 @@
         from_ref[:, g * CAP : (g + 1) * CAP] = value.astype(I32)
 
 
-def pack_kernel(scal_ref, to_ref, *refs):
+def pack_kernel(scal_ref, to_ref, got_ref, out_ref, all_ref):
     chip = scal_ref[0] // 2
-    out_ref, all_ref = refs[-2:]
-    for refs_k, shards in ((refs[:4], FIRST), (refs[4:8], SECOND)):
-        for k, ref in enumerate(refs_k):
-            for i, off in enumerate(shards):
-                row = ((chip - 4 * k + off + 2 * CHIPS) % CHIPS) * ROWS
-                all_ref[pl.ds(pl.multiple_of(row, ROWS), ROWS), :] = ref[i * ROWS : (i + 1) * ROWS, :]
+    for k in range(QUADS):
+        source = chip % QUADS + QUADS * k
+        for i, off in enumerate(WINDOW):
+            row = ((source + off + CHIPS) % CHIPS) * ROWS
+            all_ref[pl.ds(pl.multiple_of(row, ROWS), ROWS), :] = got_ref[k, i * ROWS : (i + 1) * ROWS, :]
     rows = 256
     for i in range(GROUPS * CAP // rows):
         r = i * rows + lax.broadcasted_iota(I32, (rows, GPOOL), 0)
@@ -338,8 +319,8 @@
     def move(x, perm):
         return lax.ppermute(x, "mlp", perm)
 
-    cols = jnp.concatenate([w_merge] + [move(w_merge, jump(-4 * k)) for k in (1, 2, 3)], axis=1)
-    cols = lax.all_gather(cols, "grp", axis=0, tiled=True).reshape(2, HALF, 4 * HD)
+    cols = lax.all_gather(w_merge, "mlp", axis=0, axis_index_groups=FOURS)
+    cols = lax.all_gather(cols, "grp", axis=0)
 
     parts = []
     for chunk in range(CHUNKS):
@@ -379,24 +360,21 @@
     below = move(rows, UP)
     above = move(rows, DOWN)
     last = move(below, UP)
+    own = (below, rows, above, last)
+    oth = [move(x, PART) for x in own]
     cols, _ = lax.optimization_barrier((cols, (below, above)))
-    cols_got = move(lax.dynamic_index_in_dim(cols, 1 - core, 0, keepdims=False), PART)
-
-    pieces = []
-    for shards in ((below, rows, above), (last,)):
-        mine, send = project(scal, shards, cols, cols_got)
-        blocks = join(mine, move(send, PART))
-        pieces += [blocks[0]] + [move(blocks[k], jump(4 * k)) for k in (1, 2, 3)]
+    out = project(scal, own, oth, cols)
+    out = lax.all_to_all(out, "mlp", split_axis=0, concat_axis=0, tiled=True, axis_index_groups=FOURS)
 
     out = pl.pallas_call(
         pack_kernel,
         out_shape=shape((GROUPS * CAP, HD), BF16),
-        in_specs=[smem()] + [vmem()] * (1 + len(pieces)),
+        in_specs=[smem(), vmem(), vmem()],
         out_specs=vmem(),
         scratch_shapes=[pltpu.VMEM((GPOOL, HD), BF16)],
         compiler_params=params(24),
         name="pack",
-    )(scal, to, *pieces)
+    )(scal, to, out)
     out = lax.all_to_all(out, "grp", split_axis=0, concat_axis=0, tiled=True)
     return pl.pallas_call(
         place_kernel,

time: 217 us -> 194 us (0.89)
  the two profiles are of different devices: /device:TPU:1 before, /device:TPU:64 now
where the time goes in v3:
time: 194 us; the launch traced here: 193 us
  blocking collectives  74.6 us (38%)
  starting transfers between devices  49.8 us (26%)
  Pallas kernels  35.8 us (18%)
  between operations  13.8 us (7%)
  local copies, waits for them, and re-layouts  9.03 us (5%)
  waiting for transfers between devices  8.32 us (4%)
    ppermute x15, starting transfers between devices, move(): return lax.ppermute(x, 'mlp', perm)  41.6 us
    all_to_all x1, blocking collectives, body(): lax.all_to_all(out, 'mlp', split_axis=0, concat_axis=0, tiled=True, axis_...  30.5 us
    all_gather x1, blocking collectives, body(): cols = lax.all_gather(w_merge, 'mlp', axis=0, axis_index_groups=FOURS)  25.9 us
    all_to_all x1, blocking collectives, body(): out = lax.all_to_all(out, 'grp', split_axis=0, concat_axis=0, tiled=True)  18.2 us
    pallas_call x2, Pallas kernels, attend(): pl.pallas_call(attend_kernel, grid=(HEADS // STEP,), out_shape=[jax.Shape...  14.1 us
    pallas_call x2, Pallas kernels, rope(): pl.pallas_call(rope_kernel, out_shape=[jax.ShapeDtypeStruct((3, BLK, WIDE...  10.8 us
    unnamed x27, local copies, waits for them, and re-layouts  8.39 us
    ppermute x15, waiting for transfers between devices, move(): return lax.ppermute(x, 'mlp', perm)  8.28 us
  transfers between devices with their start and end apart: 17, of which 3 were waited for; matrix products, arithmetic and copies ran while one was open for 2% of the time, Pallas kernels for 15%

profile of v3, /device:TPU:64, one launch (start us, length us, event | category | flops | bytes accessed | tf_op | source)
XLA Modules:
  0.0 193.0 jit_solution(14479203586020643441)
XLA Ops:
  6.5 25.9 %all-gather = bf16[1024,128]{1,0:T(8,128)(2,1)} all-gather(bf16[256,128]{1,0:T(8,128)(2,1)} %param.11), channel_id=2, replica_groups={{0,8,16,24},{1,9,17,25},{2,10,18,26},{3,11,19,27},{4,12,20,28},{5,13,21..., dimensions={0}, use_global_device_ids=true | all-gather | bytes 327680 | tf_op jit(solution)/shard_map/all_gather | solution.py:322
  34.4 5.4 %rope.2 = (bf16[3,128,1024]{2,1,0:T(8,128)(2,1)}, bf16[3,128,1024]{2,1,0:T(8,128)(2,1)}) custom-call(s32[4]{0:T(128)} %pad_add_fusion.scal_ref, s32[16,2]{1,0:T(8,128)} %copy.14.grid_ref, bf16[128,4096]{1,0:T(8,128)(2,1)} %q_ref.3, bf16[128,4096]{1,0:T(8,128)(2,1)} %k_ref.3, bf16[128,4096]{1,0:T(8,128)(2,1)} %v_ref.3), custom_call_target="tpu_custom_call" | custom-call | flops 4600000000 | bytes 14000000 | tf_op jit(solution)/shard_map/rope/pallas_call | solution.py:132
  41.8 3.0 %collective-permute-start.1 = (bf16[3,128,1024]{2,1,0:T(8,128)(2,1)}, bf16[3,128,1024]{2,1,0:T(8,128)(2,1)}, u32[]{:S(2)}, u32[]{:S(2)}) collective-permute-start(bf16[3,128,1024]{2,1,0:T(8,128)(2,1)} %get-tuple-element.39.a_ref), channel_id=1, source_target_pairs={{0,30},{2,0},{4,2},{6,4},{8,6},{10,8},{12,10},{14,12},{16,14},{18,... | collective-permute-start | bytes 2359304 | tf_op jit(solution)/shard_map/ppermute | solution.py:320
  44.9 4.0 %collective-permute-start.2 = (bf16[3,128,1024]{2,1,0:T(8,128)(2,1)}, bf16[3,128,1024]{2,1,0:T(8,128)(2,1)}, u32[]{:S(2)}, u32[]{:S(2)}) collective-permute-start(bf16[3,128,1024]{2,1,0:T(8,128)(2,1)} %get-tuple-element.40), channel_id=1, source_target_pairs={{1,30},{3,0},{5,2},{7,4},{9,6},{11,8},{13,10},{15,12},{17,14},{19,... | collective-permute-start | bytes 2359304 | tf_op jit(solution)/shard_map/ppermute | solution.py:320
  48.9 5.4 %rope.3 = (bf16[3,128,1024]{2,1,0:T(8,128)(2,1)}, bf16[3,128,1024]{2,1,0:T(8,128)(2,1)}) custom-call(s32[4]{0:T(128)} %pad_add_fusion.scal_ref, s32[16,2]{1,0:T(8,128)} %copy.14.grid_ref, bf16[128,4096]{1,0:T(8,128)(2,1)} %q_ref.3, bf16[128,4096]{1,0:T(8,128)(2,1)} %k_ref.3, bf16[128,4096]{1,0:T(8,128)(2,1)} %v_ref.3), custom_call_target="tpu_custom_call" | custom-call | flops 4600000000 | bytes 14000000 | tf_op jit(solution)/shard_map/rope/pallas_call | solution.py:132
  56.2 3.2 %collective-permute-start.5 = (bf16[3,128,1024]{2,1,0:T(8,128)(2,1)}, bf16[3,128,1024]{2,1,0:T(8,128)(2,1)S(1)}, u32[]{:S(2)}, u32[]{:S(2)}) collective-permute-start(bf16[3,128,1024]{2,1,0:T(8,128)(2,1)} %get-tuple-element.46.a_ref), channel_id=1, source_target_pairs={{0,30},{2,0},{4,2},{6,4},{8,6},{10,8},{12,10},{14,12},{16,14},{18,... | collective-permute-start | bytes 2359304 | tf_op jit(solution)/shard_map/ppermute | solution.py:320
  60.4 2.2 %collective-permute-start.6 = (bf16[3,128,1024]{2,1,0:T(8,128)(2,1)}, bf16[3,128,1024]{2,1,0:T(8,128)(2,1)S(1)}, u32[]{:S(2)}, u32[]{:S(2)}) collective-permute-start(bf16[3,128,1024]{2,1,0:T(8,128)(2,1)} %get-tuple-element.47), channel_id=1, source_target_pairs={{1,30},{3,0},{5,2},{7,4},{9,6},{11,8},{13,10},{15,12},{17,14},{19,... | collective-permute-start | bytes 2359304 | tf_op jit(solution)/shard_map/ppermute | solution.py:320
  65.7 2.2 %index.1 = (s32[1,1024]{1,0:T(1,128)S(1)}, s32[1,2048]{1,0:T(1,128)S(1)}) custom-call(s32[4]{0:T(128)S(1)} %copy-done.1, s32[16,1024]{1,0:T(8,128)S(1)} %reshape.20.pos_ref), custom_call_target="tpu_custom_call" | custom-call | tf_op jit(solution)/shard_map/index/pallas_call | solution.py:338
  67.9 7.0 %attend.2 = (bf16[64,1024]{1,0:T(8,128)(2,1)}, bf16[64,1024]{1,0:T(8,128)(2,1)}) custom-call(bf16[3,128,1024]{2,1,0:T(8,128)(2,1)} %get-tuple-element.39.a_ref, bf16[3,128,1024]{2,1,0:T(8,128)(2,1)} %copy-done.12, bf16[3,128,1024]{2,1,0:T(8,128)(2,1)} %collective-permute-done.1.c_ref, bf16[3,128,1024]{2,1,0:T(8,128)(2,1)} %collective-permute-done.2.d_ref, ...), custom_call_target="tpu_custom_call" | custom-call | flops 6899999744 | bytes 21000000 | tf_op jit(solution)/shard_map/attend/pallas_call | solution.py:222
  75.0 3.2 %collective-permute-start.3 = (bf16[64,1024]{1,0:T(8,128)(2,1)}, bf16[64,1024]{1,0:T(8,128)(2,1)S(1)}, u32[]{:S(2)}, u32[]{:S(2)}) collective-permute-start(bf16[64,1024]{1,0:T(8,128)(2,1)} %get-tuple-element.45), channel_id=1, source_target_pairs={{0,2},{2,4},{4,6},{6,8},{8,10},{10,12},{12,14},{14,16},{16,18},{18... | collective-permute-start | bytes 393224 | tf_op jit(solution)/shard_map/ppermute | solution.py:320
  78.8 8.1 %all-to-all-start = ((bf16[32,1,128]{2,1,0:T(2,128)(2,1)}), bf16[32,1,128]{2,1,0:T(2,128)(2,1)S(1)}, u32[]{:S(2)}, u32[]{:S(2)}) async-start(bf16[32,1,128]{2,1,0:T(2,128)(2,1)} %copy.17), calls=%async_computation | async-start | bytes 32768 | tf_op jit(solution)/shard_map/all_to_all | solution.py:355
  89.0 7.1 %attend.3 = (bf16[64,1024]{1,0:T(8,128)(2,1)}, bf16[64,1024]{1,0:T(8,128)(2,1)}) custom-call(bf16[3,128,1024]{2,1,0:T(8,128)(2,1)} %get-tuple-element.46.a_ref, bf16[3,128,1024]{2,1,0:T(8,128)(2,1)} %copy-done.9, bf16[3,128,1024]{2,1,0:T(8,128)(2,1)} %copy-done.10, bf16[3,128,1024]{2,1,0:T(8,128)(2,1)} %copy-done.11, bf16[512,128]{1,0:T(8,128)(2,1)} %copy-done.3, ...), custom_call_target="tpu_custom_call" | custom-call | flops 6899999744 | bytes 21000000 | tf_op jit(solution)/shard_map/attend/pallas_call | solution.py:222
  96.1 3.4 %collective-permute-start.7 = (bf16[64,1024]{1,0:T(8,128)(2,1)}, bf16[64,1024]{1,0:T(8,128)(2,1)S(1)}, u32[]{:S(2)}, u32[]{:S(2)}) collective-permute-start(bf16[64,1024]{1,0:T(8,128)(2,1)} %get-tuple-element.52), channel_id=1, source_target_pairs={{0,2},{2,4},{4,6},{6,8},{8,10},{10,12},{12,14},{14,16},{16,18},{18... | collective-permute-start | bytes 393224 | tf_op jit(solution)/shard_map/ppermute | solution.py:320
  99.6 3.6 %collective-permute-done.7 = bf16[64,1024]{1,0:T(8,128)(2,1)S(1)} collective-permute-done((bf16[64,1024]{1,0:T(8,128)(2,1)}, bf16[64,1024]{1,0:T(8,128)(2,1)S(1)}, u32[]{:S(2)}, u32[]{:S(2)}) %collective-permute-start.7) | collective-permute-done | bytes 131104 | tf_op jit(solution)/shard_map/ppermute | solution.py:320
  104.1 3.7 %collective-permute-start.8 = (bf16[64,2048]{1,0:T(8,128)(2,1)S(1)}, bf16[64,2048]{1,0:T(8,128)(2,1)S(1)}, u32[]{:S(2)}, u32[]{:S(2)}) collective-permute-start(bf16[64,2048]{1,0:T(8,128)(2,1)S(1)} %multiply_convert_fusion.refs_1_), channel_id=1, source_target_pairs={{0,2},{1,3},{2,4},{3,5},{4,6},{5,7},{6,8},{7,9},{8,10},{9,11},{10,... | collective-permute-start | bytes 786440 | tf_op jit(solution)/shard_map/ppermute | solution.py:320
  107.9 2.1 %collective-permute-start.9 = (bf16[64,2048]{1,0:T(8,128)(2,1)S(1)}, bf16[64,2048]{1,0:T(8,128)(2,1)S(1)}, u32[]{:S(2)}, u32[]{:S(2)}) collective-permute-start(bf16[64,2048]{1,0:T(8,128)(2,1)S(1)} %multiply_convert_fusion.refs_1_), channel_id=1, source_target_pairs={{0,30},{1,31},{2,0},{3,1},{4,2},{5,3},{6,4},{7,5},{8,6},{9,7},{10,... | collective-permute-start | bytes 786440 | tf_op jit(solution)/shard_map/ppermute | solution.py:320
  110.0 3.6 %collective-permute-done.8.refs_0_ = bf16[64,2048]{1,0:T(8,128)(2,1)S(1)} collective-permute-done((bf16[64,2048]{1,0:T(8,128)(2,1)S(1)}, bf16[64,2048]{1,0:T(8,128)(2,1)S(1)}, u32[]{:S(2)}, u32[]{:S(2)}) %collective-permute-start.8) | collective-permute-done | bytes 262176 | tf_op jit(solution)/shard_map/ppermute | solution.py:320
  113.6 4.3 %collective-permute-start.10 = (bf16[64,2048]{1,0:T(8,128)(2,1)S(1)}, bf16[64,2048]{1,0:T(8,128)(2,1)S(1)}, u32[]{:S(2)}, u32[]{:S(2)}) collective-permute-start(bf16[64,2048]{1,0:T(8,128)(2,1)S(1)} %collective-permute-done.8.refs_0_), channel_id=1, source_target_pairs={{0,2},{1,3},{2,4},{3,5},{4,6},{5,7},{6,8},{7,9},{8,10},{9,11},{10,... | collective-permute-start | bytes 786440 | tf_op jit(solution)/shard_map/ppermute | solution.py:320
  119.8 2.4 %collective-permute-start.11 = (bf16[64,2048]{1,0:T(8,128)(2,1)S(1)}, bf16[64,2048]{1,0:T(8,128)(2,1)S(1)}, u32[]{:S(2)}, u32[]{:S(2)}) collective-permute-start(bf16[64,2048]{1,0:T(8,128)(2,1)S(1)} %collective-permute-done.8.refs_0_), channel_id=1, source_target_pairs={{0,1},{1,0},{2,3},{3,2},{4,5},{5,4},{6,7},{7,6},{8,9},{9,8},{10,11... | collective-permute-start | bytes 786440 | tf_op jit(solution)/shard_map/ppermute | solution.py:320
  124.2 2.4 %collective-permute-start.14 = (bf16[64,2048]{1,0:T(8,128)(2,1)S(1)}, bf16[64,2048]{1,0:T(8,128)(2,1)S(1)}, u32[]{:S(2)}, u32[]{:S(2)}) collective-permute-start(bf16[64,2048]{1,0:T(8,128)(2,1)S(1)} %collective-permute-done.10.refs_3_), channel_id=1, source_target_pairs={{0,1},{1,0},{2,3},{3,2},{4,5},{5,4},{6,7},{7,6},{8,9},{9,8},{10,11... | collective-permute-start | bytes 786440 | tf_op jit(solution)/shard_map/ppermute | solution.py:320
  127.7 2.2 %copy-done.2 = bf16[64,256,128]{2,1,0:T(8,128)(2,1)S(1)} copy-done((bf16[64,256,128]{2,1,0:T(8,128)(2,1)S(1)}, bf16[64,256,128]{2,1,0:T(8,128)(2,1)}, u32[]{:S(2)}) %copy-start.2) | copy-done | bytes 4194328
  129.9 3.7 %project.1 = bf16[4,256,128]{2,1,0:T(8,128)(2,1)S(1)} custom-call(s32[4]{0:T(128)S(1)} %copy-done.1, bf16[64,2048]{1,0:T(8,128)(2,1)S(1)} %collective-permute-done.8.refs_0_, bf16[64,2048]{1,0:T(8,128)(2,1)S(1)} %multiply_convert_fusion.refs_1_, bf16[64,2048]{1,0:T(8,128)(2,1)S(1)} %collective-permute-done.9.refs_2_, ...), custom_call_target="tpu_custom_call" | custom-call | flops 4600000000 | bytes 14000000 | tf_op jit(solution)/shard_map/project/pallas_call | solution.py:246
  133.6 30.5 %all_to_all.25.got_ref = bf16[4,256,128]{2,1,0:T(8,128)(2,1)S(1)} all-to-all(bf16[4,256,128]{2,1,0:T(8,128)(2,1)S(1)} %project.1), channel_id=1, replica_groups={{0,8,16,24},{1,9,17,25},{2,10,18,26},{3,11,19,27},{4,12,20,28},{5,13,21..., dimensions={0} | all-to-all | bytes 524288 | tf_op jit(solution)/shard_map/all_to_all | solution.py:367
  166.0 18.2 %all_to_all.26 = bf16[16,128,128]{2,1,0:T(8,128)(2,1)S(1)} all-to-all(bf16[16,128,128]{2,1,0:T(8,128)(2,1)S(1)} %bitcast.9), channel_id=1, replica_groups=mesh['grp'=16,'mlp'=32] {'grp'}, dimensions={0} | all-to-all | bytes 1048576 | tf_op jit(solution)/shard_map/all_to_all | solution.py:378
  (58 shorter events, 22.2 us)
Async XLA Ops:
  6.5 120.1 %all-gather.4.cloned.1.call-start = ((), (), s32[]{:S(2)}) async-start(), calls=%async_computation.3 | async-start | bytes 4456448 | tf_op jit(solution)/shard_map/all_gather | solution.py:323
  39.9 19.6 %collective-permute-start = (bf16[3,128,1024]{2,1,0:T(8,128)(2,1)}, bf16[3,128,1024]{2,1,0:T(8,128)(2,1)S(1)}, u32[]{:S(2)}, u32[]{:S(2)}) collective-permute-start(bf16[3,128,1024]{2,1,0:T(8,128)(2,1)} %get-tuple-element.40), channel_id=1, source_target_pairs={{0,1},{1,0},{2,3},{3,2},{4,5},{5,4},{6,7},{7,6},{8,9},{9,8},{10,11... | collective-permute-start | bytes 2359304 | tf_op jit(solution)/shard_map/ppermute | solution.py:320
  41.8 20.8 %copy-start = (s32[16,2]{1,0:T(8,128)S(1)}, s32[16,2]{1,0:T(8,128)}, u32[]{:S(2)}) copy-start(s32[16,2]{1,0:T(8,128)} %copy.14.grid_ref) | copy-start | bytes 388
  41.8 20.8 %copy-start.1 = (s32[4]{0:T(128)S(1)}, s32[4]{0:T(128)}, u32[]{:S(2)}) copy-start(s32[4]{0:T(128)} %pad_add_fusion.scal_ref) | copy-start | bytes 52
  41.8 23.9 %copy-start.7 = (s32[16384]{0:T(1024)S(1)}, s32[16384]{0:T(1024)}, u32[]{:S(2)}) copy-start(s32[16384]{0:T(1024)} %param.13) | copy-start | bytes 196612
  41.8 26.1 %collective-permute-start.1 = (bf16[3,128,1024]{2,1,0:T(8,128)(2,1)}, bf16[3,128,1024]{2,1,0:T(8,128)(2,1)}, u32[]{:S(2)}, u32[]{:S(2)}) collective-permute-start(bf16[3,128,1024]{2,1,0:T(8,128)(2,1)} %get-tuple-element.39.a_ref), channel_id=1, source_target_pairs={{0,30},{2,0},{4,2},{6,4},{8,6},{10,8},{12,10},{14,12},{16,14},{18,... | collective-permute-start | bytes 2359304 | tf_op jit(solution)/shard_map/ppermute | solution.py:320
  44.9 23.1 %collective-permute-start.2 = (bf16[3,128,1024]{2,1,0:T(8,128)(2,1)}, bf16[3,128,1024]{2,1,0:T(8,128)(2,1)}, u32[]{:S(2)}, u32[]{:S(2)}) collective-permute-start(bf16[3,128,1024]{2,1,0:T(8,128)(2,1)} %get-tuple-element.40), channel_id=1, source_target_pairs={{1,30},{3,0},{5,2},{7,4},{9,6},{11,8},{13,10},{15,12},{17,14},{19,... | collective-permute-start | bytes 2359304 | tf_op jit(solution)/shard_map/ppermute | solution.py:320
  54.3 32.7 %collective-permute-start.4 = (bf16[3,128,1024]{2,1,0:T(8,128)(2,1)}, bf16[3,128,1024]{2,1,0:T(8,128)(2,1)S(1)}, u32[]{:S(2)}, u32[]{:S(2)}) collective-permute-start(bf16[3,128,1024]{2,1,0:T(8,128)(2,1)} %get-tuple-element.47), channel_id=1, source_target_pairs={{0,1},{1,0},{2,3},{3,2},{4,5},{5,4},{6,7},{7,6},{8,9},{9,8},{10,11... | collective-permute-start | bytes 2359304 | tf_op jit(solution)/shard_map/ppermute | solution.py:320
  56.2 30.8 %collective-permute-start.5 = (bf16[3,128,1024]{2,1,0:T(8,128)(2,1)}, bf16[3,128,1024]{2,1,0:T(8,128)(2,1)S(1)}, u32[]{:S(2)}, u32[]{:S(2)}) collective-permute-start(bf16[3,128,1024]{2,1,0:T(8,128)(2,1)} %get-tuple-element.46.a_ref), channel_id=1, source_target_pairs={{0,30},{2,0},{4,2},{6,4},{8,6},{10,8},{12,10},{14,12},{16,14},{18,... | collective-permute-start | bytes 2359304 | tf_op jit(solution)/shard_map/ppermute | solution.py:320
  60.4 26.7 %collective-permute-start.6 = (bf16[3,128,1024]{2,1,0:T(8,128)(2,1)}, bf16[3,128,1024]{2,1,0:T(8,128)(2,1)S(1)}, u32[]{:S(2)}, u32[]{:S(2)}) collective-permute-start(bf16[3,128,1024]{2,1,0:T(8,128)(2,1)} %get-tuple-element.47), channel_id=1, source_target_pairs={{1,30},{3,0},{5,2},{7,4},{9,6},{11,8},{13,10},{15,12},{17,14},{19,... | collective-permute-start | bytes 2359304 | tf_op jit(solution)/shard_map/ppermute | solution.py:320
  67.9 10.3 %copy-start.8 = (bf16[128]{0:T(256)(128)(2,1)S(1)}, bf16[128]{0:T(256)(128)(2,1)}, u32[]{:S(2)}) copy-start(bf16[128]{0:T(256)(128)(2,1)} %param.10) | copy-start | bytes 772
  75.0 12.0 %collective-permute-start.3 = (bf16[64,1024]{1,0:T(8,128)(2,1)}, bf16[64,1024]{1,0:T(8,128)(2,1)S(1)}, u32[]{:S(2)}, u32[]{:S(2)}) collective-permute-start(bf16[64,1024]{1,0:T(8,128)(2,1)} %get-tuple-element.45), channel_id=1, source_target_pairs={{0,2},{2,4},{4,6},{6,8},{8,10},{10,12},{12,14},{14,16},{16,18},{18... | collective-permute-start | bytes 393224 | tf_op jit(solution)/shard_map/ppermute | solution.py:320
  78.8 20.7 %all-to-all-start = ((bf16[32,1,128]{2,1,0:T(2,128)(2,1)}), bf16[32,1,128]{2,1,0:T(2,128)(2,1)S(1)}, u32[]{:S(2)}, u32[]{:S(2)}) async-start(bf16[32,1,128]{2,1,0:T(2,128)(2,1)} %copy.17), calls=%async_computation | async-start | bytes 32768 | tf_op jit(solution)/shard_map/all_to_all | solution.py:355
  87.0 12.6 %copy-start.6 = (bf16[64,1024]{1,0:T(8,128)(2,1)S(1)}, bf16[64,1024]{1,0:T(8,128)(2,1)}, u32[]{:S(2)}) copy-start(bf16[64,1024]{1,0:T(8,128)(2,1)} %get-tuple-element.44) | copy-start | bytes 393220
  87.0 1.1 copy-start.10
  96.1 7.1 %collective-permute-start.7 = (bf16[64,1024]{1,0:T(8,128)(2,1)}, bf16[64,1024]{1,0:T(8,128)(2,1)S(1)}, u32[]{:S(2)}, u32[]{:S(2)}) collective-permute-start(bf16[64,1024]{1,0:T(8,128)(2,1)} %get-tuple-element.52), channel_id=1, source_target_pairs={{0,2},{2,4},{4,6},{6,8},{8,10},{10,12},{12,14},{14,16},{16,18},{18... | collective-permute-start | bytes 393224 | tf_op jit(solution)/shard_map/ppermute | solution.py:320
  104.1 9.4 %collective-permute-start.8 = (bf16[64,2048]{1,0:T(8,128)(2,1)S(1)}, bf16[64,2048]{1,0:T(8,128)(2,1)S(1)}, u32[]{:S(2)}, u32[]{:S(2)}) collective-permute-start(bf16[64,2048]{1,0:T(8,128)(2,1)S(1)} %multiply_convert_fusion.refs_1_), channel_id=1, source_target_pairs={{0,2},{1,3},{2,4},{3,5},{4,6},{5,7},{6,8},{7,9},{8,10},{9,11},{10,... | collective-permute-start | bytes 786440 | tf_op jit(solution)/shard_map/ppermute | solution.py:320
  107.9 14.3 %collective-permute-start.9 = (bf16[64,2048]{1,0:T(8,128)(2,1)S(1)}, bf16[64,2048]{1,0:T(8,128)(2,1)S(1)}, u32[]{:S(2)}, u32[]{:S(2)}) collective-permute-start(bf16[64,2048]{1,0:T(8,128)(2,1)S(1)} %multiply_convert_fusion.refs_1_), channel_id=1, source_target_pairs={{0,30},{1,31},{2,0},{3,1},{4,2},{5,3},{6,4},{7,5},{8,6},{9,7},{10,... | collective-permute-start | bytes 786440 | tf_op jit(solution)/shard_map/ppermute | solution.py:320
  113.6 10.6 %collective-permute-start.10 = (bf16[64,2048]{1,0:T(8,128)(2,1)S(1)}, bf16[64,2048]{1,0:T(8,128)(2,1)S(1)}, u32[]{:S(2)}, u32[]{:S(2)}) collective-permute-start(bf16[64,2048]{1,0:T(8,128)(2,1)S(1)} %collective-permute-done.8.refs_0_), channel_id=1, source_target_pairs={{0,2},{1,3},{2,4},{3,5},{4,6},{5,7},{6,8},{7,9},{8,10},{9,11},{10,... | collective-permute-start | bytes 786440 | tf_op jit(solution)/shard_map/ppermute | solution.py:320
  117.9 8.7 %collective-permute-start.12 = (bf16[64,2048]{1,0:T(8,128)(2,1)S(1)}, bf16[64,2048]{1,0:T(8,128)(2,1)S(1)}, u32[]{:S(2)}, u32[]{:S(2)}) collective-permute-start(bf16[64,2048]{1,0:T(8,128)(2,1)S(1)} %multiply_convert_fusion.refs_1_), channel_id=1, source_target_pairs={{0,1},{1,0},{2,3},{3,2},{4,5},{5,4},{6,7},{7,6},{8,9},{9,8},{10,11... | collective-permute-start | bytes 786440 | tf_op jit(solution)/shard_map/ppermute | solution.py:320
  119.8 6.8 %collective-permute-start.11 = (bf16[64,2048]{1,0:T(8,128)(2,1)S(1)}, bf16[64,2048]{1,0:T(8,128)(2,1)S(1)}, u32[]{:S(2)}, u32[]{:S(2)}) collective-permute-start(bf16[64,2048]{1,0:T(8,128)(2,1)S(1)} %collective-permute-done.8.refs_0_), channel_id=1, source_target_pairs={{0,1},{1,0},{2,3},{3,2},{4,5},{5,4},{6,7},{7,6},{8,9},{9,8},{10,11... | collective-permute-start | bytes 786440 | tf_op jit(solution)/shard_map/ppermute | solution.py:320
  122.2 4.4 %collective-permute-start.13 = (bf16[64,2048]{1,0:T(8,128)(2,1)S(1)}, bf16[64,2048]{1,0:T(8,128)(2,1)S(1)}, u32[]{:S(2)}, u32[]{:S(2)}) collective-permute-start(bf16[64,2048]{1,0:T(8,128)(2,1)S(1)} %collective-permute-done.9.refs_2_), channel_id=1, source_target_pairs={{0,1},{1,0},{2,3},{3,2},{4,5},{5,4},{6,7},{7,6},{8,9},{9,8},{10,11... | collective-permute-start | bytes 786440 | tf_op jit(solution)/shard_map/ppermute | solution.py:320
  124.2 3.6 %collective-permute-start.14 = (bf16[64,2048]{1,0:T(8,128)(2,1)S(1)}, bf16[64,2048]{1,0:T(8,128)(2,1)S(1)}, u32[]{:S(2)}, u32[]{:S(2)}) collective-permute-start(bf16[64,2048]{1,0:T(8,128)(2,1)S(1)} %collective-permute-done.10.refs_3_), channel_id=1, source_target_pairs={{0,1},{1,0},{2,3},{3,2},{4,5},{5,4},{6,7},{7,6},{8,9},{9,8},{10,11... | collective-permute-start | bytes 786440 | tf_op jit(solution)/shard_map/ppermute | solution.py:320
  127.7 2.2 %copy-start.2 = (bf16[64,256,128]{2,1,0:T(8,128)(2,1)S(1)}, bf16[64,256,128]{2,1,0:T(8,128)(2,1)}, u32[]{:S(2)}) copy-start(bf16[64,256,128]{2,1,0:T(8,128)(2,1)} %all-gather.4.cloned.1.call-done) | copy-start | bytes 12582916
  (6 other events, 4.6 us)
Sparse Core Ops, SparseCore 0:
  32.6 64.0 all-gather.3

commit v4 on v3

--- a/solution.py
+++ b/solution.py
@@ -5,6 +5,7 @@
 from jax import lax
 from jax.experimental import pallas as pl
 from jax.experimental.pallas import tpu as pltpu
+from jax.sharding import Mesh
 from jax.sharding import PartitionSpec as P
 
 HD = 128
@@ -25,6 +26,7 @@
 F32 = jnp.float32
 BF16 = jnp.bfloat16
 I32 = jnp.int32
+MLP = ("zq", "zr", "core")
 WINDOW = (-1, 0, 1, -2)
 QUADS = 4
 
@@ -38,7 +40,6 @@
 RING = [(at(z, 0), at(z + 1, 0)) for z in range(CHIPS)] + [(at(z, 1), at(z - 1, 1)) for z in range(CHIPS)]
 UP = [(at(z, c), at(z + 1, c)) for z in range(CHIPS) for c in range(2)]
 DOWN = [(at(z, c), at(z - 1, c)) for z in range(CHIPS) for c in range(2)]
-FOURS = [[at(r + QUADS * k, c) for k in range(QUADS)] for r in range(QUADS) for c in range(2)]
 PART = [(at(z, c), at(z, 1 - c)) for z in range(CHIPS) for c in range(2)]
 
 
@@ -124,6 +125,7 @@
 def rope(scal, grids, queries, keys, values, chunk):
     n = HEADS // STEP
     lanes = STEP * HD
+    queries, keys, values = (pltpu.with_memory_space_constraint(x, pltpu.HBM) for x in (queries, keys, values))
 
     def src(i, scal_ref):
         half = jnp.where(i < n, 1 - scal_ref[1], scal_ref[1])
@@ -142,7 +144,7 @@
             ],
             scratch_shapes=[pltpu.VMEM((BLK, HD), F32)] * 2,
         ),
-        compiler_params=params(56),
+        compiler_params=params(16),
         cost_estimate=cost(4),
         name="rope",
     )(scal, grids, queries, keys, values)
@@ -225,7 +227,7 @@
         out_shape=[jax.ShapeDtypeStruct((ROWS, WIDE), BF16)] * 2,
         in_specs=[part] * NB + whole,
         out_specs=[pl.BlockSpec((ROWS, STEP * HD), lambda h: (0, h))] * 2,
-        compiler_params=params(56),
+        compiler_params=params(32),
         cost_estimate=cost(6),
         name="attend",
     )(*parts, *tables)
@@ -243,6 +245,7 @@
 def project(scal, own, oth, cols):
     rows = NB * ROWS
     half = (GROUPS // 2, 1, 2 * BLK, HD)
+    cols = pltpu.with_memory_space_constraint(cols, pltpu.HBM)
     return pl.pallas_call(
         project_kernel,
         out_shape=jax.ShapeDtypeStruct((QUADS, rows, HD), BF16),
@@ -311,20 +314,24 @@
 
 
 def body(queries, keys, values, gamma, w_merge, grids, positions):
-    me = lax.axis_index("mlp")
+    me = lax.axis_index(MLP)
     core = me % 2
     scal = jnp.stack([me, core, lax.axis_index("grp"), me]).astype(I32)
     shape = jax.ShapeDtypeStruct
 
     def move(x, perm):
-        return lax.ppermute(x, "mlp", perm)
-
-    cols = lax.all_gather(w_merge, "mlp", axis=0, axis_index_groups=FOURS)
-    cols = lax.all_gather(cols, "grp", axis=0)
+        return lax.ppermute(x, MLP, perm)
 
     parts = []
+    order = scal
     for chunk in range(CHUNKS):
-        own, oth = rope(scal, grids, queries, keys, values, chunk)
+        own, oth = rope(order, grids, queries, keys, values, chunk)
+        if chunk == 1:
+            w_merge, own, oth = lax.optimization_barrier((w_merge, own, oth))
+            cols = lax.all_gather(w_merge, "zq", axis=0)
+            own, oth, cols = lax.optimization_barrier((own, oth, cols))
+            cols = lax.all_gather(cols, "grp", axis=0)
+        order, own, oth = lax.optimization_barrier((order, own, oth))
         parts.append([own, move(oth, PART), move(own, SAME), move(oth, OPP)])
 
     tables = pl.pallas_call(
@@ -343,17 +350,15 @@
         compiler_params=params(24),
         name="index",
     )(scal, positions.reshape(GROUPS, GPOOL))
-    owns, tables, to, frm = lax.optimization_barrier(([p[0] for p in parts], tables, to, frm))
-    gains = jnp.broadcast_to(gamma[None, :], (2 * CHIPS, HD))
+    owns, tables = lax.optimization_barrier(([p[0] for p in parts], tables))
+    gains, _ = lax.optimization_barrier((jnp.broadcast_to(gamma[None, :], (2 * CHIPS, HD)), owns))
+    gains = lax.all_to_all(gains, MLP, split_axis=0, concat_axis=0, tiled=True)
+    gains = lax.dynamic_slice_in_dim(gains, core * CHIPS, CHIPS, 0).reshape(1, HALF).astype(F32)
     pooled = []
     for chunk in range(CHUNKS):
         mid, edge = attend([owns[chunk]] + parts[chunk][1:], tables)
         edge = move(edge, RING)
         pooled.append((mid, edge))
-        if chunk == 0:
-            gains, _ = lax.optimization_barrier((gains, mid))
-            gains = lax.all_to_all(gains, "mlp", split_axis=0, concat_axis=0, tiled=True)
-            gains = lax.dynamic_slice_in_dim(gains, core * CHIPS, CHIPS, 0).reshape(1, HALF).astype(F32)
         tables, _ = lax.optimization_barrier((tables, edge))
     rows = jnp.concatenate([mid + edge for mid, edge in pooled], axis=1)
     rows = (rows.astype(F32) * gains).astype(BF16)
@@ -362,9 +367,9 @@
     last = move(below, UP)
     own = (below, rows, above, last)
     oth = [move(x, PART) for x in own]
-    cols, _ = lax.optimization_barrier((cols, (below, above)))
+    cols, to, frm, _ = lax.optimization_barrier((cols, to, frm, (below, above)))
     out = project(scal, own, oth, cols)
-    out = lax.all_to_all(out, "mlp", split_axis=0, concat_axis=0, tiled=True, axis_index_groups=FOURS)
+    out = lax.all_to_all(out, "zq", split_axis=0, concat_axis=0, tiled=True)
 
     out = pl.pallas_call(
         pack_kernel,
@@ -387,18 +392,12 @@
 
 
 def solution(mesh):
+    mesh = Mesh(mesh.devices.reshape(GROUPS, CHIPS // QUADS, QUADS, 2), ("grp",) + MLP)
+    every = P(("grp",) + MLP, None)
     return jax.shard_map(
         body,
         mesh=mesh,
-        in_specs=(
-            P(("grp", "mlp"), None),
-            P(("grp", "mlp"), None),
-            P(("grp", "mlp"), None),
-            P("mlp"),
-            P("grp", "mlp"),
-            P("grp", None),
-            P(),
-        ),
-        out_specs=P("grp", "mlp"),
+        in_specs=(every, every, every, P(MLP), P("grp", MLP), P("grp", None), P()),
+        out_specs=P("grp", MLP),
         check_vma=False,
     )

time: 194 us -> 194 us (level)
  the two profiles are of different devices: /device:TPU:64 before, /device:TPU:1 now
where the time goes in v4:
time: 194 us; the launch traced here: 190 us
  blocking collectives  67.9 us (35%)
  starting transfers between devices  55.6 us (29%)
  Pallas kernels  33.5 us (17%)
  waiting for transfers between devices  14.4 us (7%)
  between operations  13.8 us (7%)
  local copies, waits for them, and re-layouts  4.12 us (2%)
    ppermute x15, starting transfers between devices, move(): return lax.ppermute(x, MLP, perm)  48.7 us
    all_to_all x1, blocking collectives, body(): out = lax.all_to_all(out, 'zq', split_axis=0, concat_axis=0, tiled=True)  26.2 us
    all_gather x1, blocking collectives, body(): cols = lax.all_gather(w_merge, 'zq', axis=0)  25.6 us
    all_to_all x1, blocking collectives, body(): out = lax.all_to_all(out, 'grp', split_axis=0, concat_axis=0, tiled=True)  16.1 us
    ppermute x15, waiting for transfers between devices, move(): return lax.ppermute(x, MLP, perm)  14.4 us
    pallas_call x2, Pallas kernels, attend(): pl.pallas_call(attend_kernel, grid=(HEADS // STEP,), out_shape=[jax.Shape...  11.8 us
    pallas_call x2, Pallas kernels, rope(): pl.pallas_call(rope_kernel, out_shape=[jax.ShapeDtypeStruct((3, BLK, WIDE...  9.36 us
    all_to_all x1, starting transfers between devices, body(): gains = lax.all_to_all(gains, MLP, split_axis=0, concat_axis=0, tiled=True)  6.93 us
  transfers between devices with their start and end apart: 17, of which 4 were waited for; matrix products, arithmetic and copies ran while one was open for 1% of the time, Pallas kernels for 8%

profile of v4, /device:TPU:1, one launch (start us, length us, event | category | flops | bytes accessed | tf_op | source)
XLA Modules:
  0.0 190.4 jit_solution(3631815183697954588)
XLA Ops:
  7.4 5.3 %rope.2 = (bf16[3,128,1024]{2,1,0:T(8,128)(2,1)}, bf16[3,128,1024]{2,1,0:T(8,128)(2,1)}) custom-call(s32[4]{0:T(128)S(1)} %pad_add_fusion.scal_ref, s32[16,2]{1,0:T(8,128)S(1)} %copy.14.grid_ref, bf16[128,4096]{1,0:T(8,128)(2,1)} %q_ref.3, bf16[128,4096]{1,0:T(8,128)(2,1)} %k_ref.3, bf16[128,4096]{1,0:T(8,128)(2,1)} %v_ref.3), custom_call_target="tpu_custom_call" | custom-call | flops 4600000000 | bytes 14000000 | tf_op jit(solution)/shard_map/rope/pallas_call | solution.py:134
  12.7 4.0 %rope.3 = (bf16[3,128,1024]{2,1,0:T(8,128)(2,1)S(1)}, bf16[3,128,1024]{2,1,0:T(8,128)(2,1)S(1)}) custom-call(s32[4]{0:T(128)S(1)} %pad_add_fusion.scal_ref, s32[16,2]{1,0:T(8,128)S(1)} %copy.14.grid_ref, bf16[128,4096]{1,0:T(8,128)(2,1)} %q_ref.3, bf16[128,4096]{1,0:T(8,128)(2,1)} %k_ref.3, bf16[128,4096]{1,0:T(8,128)(2,1)} %v_ref.3), custom_call_target="tpu_custom_call" | custom-call | flops 4600000000 | bytes 14000000 | tf_op jit(solution)/shard_map/rope/pallas_call | solution.py:134
  16.8 25.6 %all-gather = bf16[1024,128]{1,0:T(8,128)(2,1)} all-gather(bf16[256,128]{1,0:T(8,128)(2,1)S(1)} %copy-done.6), channel_id=2, replica_groups=mesh['grp'=16,'zq'=4,'zr'=4,'core'=2] {'zq'}, dimensions={0}, use_global_device_ids=true | all-gather | bytes 327680 | tf_op jit(solution)/shard_map/all_gather | solution.py:331
  42.4 5.5 %collective-permute-start = (bf16[3,128,1024]{2,1,0:T(8,128)(2,1)}, bf16[3,128,1024]{2,1,0:T(8,128)(2,1)S(1)}, u32[]{:S(2)}, u32[]{:S(2)}) collective-permute-start(bf16[3,128,1024]{2,1,0:T(8,128)(2,1)} %get-tuple-element.60), channel_id=1, source_target_pairs={{0,1},{1,0},{2,3},{3,2},{4,5},{5,4},{6,7},{7,6},{8,9},{9,8},{10,11... | collective-permute-start | bytes 2359304 | tf_op jit(solution)/shard_map/ppermute | solution.py:323
  47.8 2.6 %collective-permute-start.1 = (bf16[3,128,1024]{2,1,0:T(8,128)(2,1)}, bf16[3,128,1024]{2,1,0:T(8,128)(2,1)S(1)}, u32[]{:S(2)}, u32[]{:S(2)}) collective-permute-start(bf16[3,128,1024]{2,1,0:T(8,128)(2,1)} %get-tuple-element.59.a_ref), channel_id=1, source_target_pairs={{0,30},{2,0},{4,2},{6,4},{8,6},{10,8},{12,10},{14,12},{16,14},{18,... | collective-permute-start | bytes 2359304 | tf_op jit(solution)/shard_map/ppermute | solution.py:323
  50.4 3.1 %collective-permute-start.2 = (bf16[3,128,1024]{2,1,0:T(8,128)(2,1)}, bf16[3,128,1024]{2,1,0:T(8,128)(2,1)S(1)}, u32[]{:S(2)}, u32[]{:S(2)}) collective-permute-start(bf16[3,128,1024]{2,1,0:T(8,128)(2,1)} %get-tuple-element.60), channel_id=1, source_target_pairs={{1,30},{3,0},{5,2},{7,4},{9,6},{11,8},{13,10},{15,12},{17,14},{19,... | collective-permute-start | bytes 2359304 | tf_op jit(solution)/shard_map/ppermute | solution.py:323
  55.8 3.3 %collective-permute-start.5 = (bf16[3,128,1024]{2,1,0:T(8,128)(2,1)S(1)}, bf16[3,128,1024]{2,1,0:T(8,128)(2,1)S(1)}, u32[]{:S(2)}, u32[]{:S(2)}) collective-permute-start(bf16[3,128,1024]{2,1,0:T(8,128)(2,1)S(1)} %get-tuple-element.66.a_ref), channel_id=1, source_target_pairs={{0,30},{2,0},{4,2},{6,4},{8,6},{10,8},{12,10},{14,12},{16,14},{18,... | collective-permute-start | bytes 2359304 | tf_op jit(solution)/shard_map/ppermute | solution.py:323
  59.1 3.3 %collective-permute-start.6 = (bf16[3,128,1024]{2,1,0:T(8,128)(2,1)S(1)}, bf16[3,128,1024]{2,1,0:T(8,128)(2,1)}, u32[]{:S(2)}, u32[]{:S(2)}) collective-permute-start(bf16[3,128,1024]{2,1,0:T(8,128)(2,1)S(1)} %get-tuple-element.67), channel_id=1, source_target_pairs={{1,30},{3,0},{5,2},{7,4},{9,6},{11,8},{13,10},{15,12},{17,14},{19,... | collective-permute-start | bytes 2359304 | tf_op jit(solution)/shard_map/ppermute | solution.py:323
  63.6 3.6 %collective-permute-done.1.c_ref = bf16[3,128,1024]{2,1,0:T(8,128)(2,1)S(1)} collective-permute-done((bf16[3,128,1024]{2,1,0:T(8,128)(2,1)}, bf16[3,128,1024]{2,1,0:T(8,128)(2,1)S(1)}, u32[]{:S(2)}, u32[]{:S(2)}) %collective-permute-start.1) | collective-permute-done | bytes 786464 | tf_op jit(solution)/shard_map/ppermute | solution.py:323
  67.2 6.4 %collective-permute-done.2.d_ref = bf16[3,128,1024]{2,1,0:T(8,128)(2,1)S(1)} collective-permute-done((bf16[3,128,1024]{2,1,0:T(8,128)(2,1)}, bf16[3,128,1024]{2,1,0:T(8,128)(2,1)S(1)}, u32[]{:S(2)}, u32[]{:S(2)}) %collective-permute-start.2) | collective-permute-done | bytes 786464 | tf_op jit(solution)/shard_map/ppermute | solution.py:323
  73.6 5.8 %attend.2 = (bf16[64,1024]{1,0:T(8,128)(2,1)S(1)}, bf16[64,1024]{1,0:T(8,128)(2,1)S(1)}) custom-call(bf16[3,128,1024]{2,1,0:T(8,128)(2,1)} %get-tuple-element.59.a_ref, bf16[3,128,1024]{2,1,0:T(8,128)(2,1)S(1)} %collective-permute-done.b_ref, bf16[3,128,1024]{2,1,0:T(8,128)(2,1)S(1)} %collective-permute-done.1.c_ref, ...), custom_call_target="tpu_custom_call" | custom-call | flops 6899999744 | bytes 21000000 | tf_op jit(solution)/shard_map/attend/pallas_call | solution.py:224
  79.5 3.1 %collective-permute-start.3 = (bf16[64,1024]{1,0:T(8,128)(2,1)S(1)}, bf16[64,1024]{1,0:T(8,128)(2,1)}, u32[]{:S(2)}, u32[]{:S(2)}) collective-permute-start(bf16[64,1024]{1,0:T(8,128)(2,1)S(1)} %get-tuple-element.65), channel_id=1, source_target_pairs={{0,2},{2,4},{4,6},{6,8},{8,10},{10,12},{12,14},{14,16},{16,18},{18... | collective-permute-start | bytes 393224 | tf_op jit(solution)/shard_map/ppermute | solution.py:323
  83.2 6.9 %all-to-all-start = ((bf16[32,1,128]{2,1,0:T(2,128)(2,1)}), bf16[32,1,128]{2,1,0:T(2,128)(2,1)S(1)}, u32[]{:S(2)}, u32[]{:S(2)}) async-start(bf16[32,1,128]{2,1,0:T(2,128)(2,1)} %copy.17), calls=%async_computation | async-start | bytes 32768 | tf_op jit(solution)/shard_map/all_to_all | solution.py:355
  92.9 6.0 %attend.3 = (bf16[64,1024]{1,0:T(8,128)(2,1)S(1)}, bf16[64,1024]{1,0:T(8,128)(2,1)S(1)}) custom-call(bf16[3,128,1024]{2,1,0:T(8,128)(2,1)S(1)} %get-tuple-element.66.a_ref, bf16[3,128,1024]{2,1,0:T(8,128)(2,1)S(1)} %collective-permute-done.4.b_ref, bf16[3,128,1024]{2,1,0:T(8,128)(2,1)S(1)} %collective-permute-done.5.c_ref, ...), custom_call_target="tpu_custom_call" | custom-call | flops 6899999744 | bytes 21000000 | tf_op jit(solution)/shard_map/attend/pallas_call | solution.py:224
  98.9 4.6 %collective-permute-start.7 = (bf16[64,1024]{1,0:T(8,128)(2,1)S(1)}, bf16[64,1024]{1,0:T(8,128)(2,1)S(1)}, u32[]{:S(2)}, u32[]{:S(2)}) collective-permute-start(bf16[64,1024]{1,0:T(8,128)(2,1)S(1)} %get-tuple-element.72), channel_id=1, source_target_pairs={{0,2},{2,4},{4,6},{6,8},{8,10},{10,12},{12,14},{14,16},{16,18},{18... | collective-permute-start | bytes 393224 | tf_op jit(solution)/shard_map/ppermute | solution.py:323
  105.5 2.9 %collective-permute-start.8 = (bf16[64,2048]{1,0:T(8,128)(2,1)S(1)}, bf16[64,2048]{1,0:T(8,128)(2,1)S(1)}, u32[]{:S(2)}, u32[]{:S(2)}) collective-permute-start(bf16[64,2048]{1,0:T(8,128)(2,1)S(1)} %multiply_convert_fusion.refs_1_), channel_id=1, source_target_pairs={{0,2},{1,3},{2,4},{3,5},{4,6},{5,7},{6,8},{7,9},{8,10},{9,11},{10,... | collective-permute-start | bytes 786440 | tf_op jit(solution)/shard_map/ppermute | solution.py:323
  108.4 4.4 %collective-permute-start.9 = (bf16[64,2048]{1,0:T(8,128)(2,1)S(1)}, bf16[64,2048]{1,0:T(8,128)(2,1)S(1)}, u32[]{:S(2)}, u32[]{:S(2)}) collective-permute-start(bf16[64,2048]{1,0:T(8,128)(2,1)S(1)} %multiply_convert_fusion.refs_1_), channel_id=1, source_target_pairs={{0,30},{1,31},{2,0},{3,1},{4,2},{5,3},{6,4},{7,5},{8,6},{9,7},{10,... | collective-permute-start | bytes 786440 | tf_op jit(solution)/shard_map/ppermute | solution.py:323
  112.9 3.4 %collective-permute-done.8.refs_0_ = bf16[64,2048]{1,0:T(8,128)(2,1)S(1)} collective-permute-done((bf16[64,2048]{1,0:T(8,128)(2,1)S(1)}, bf16[64,2048]{1,0:T(8,128)(2,1)S(1)}, u32[]{:S(2)}, u32[]{:S(2)}) %collective-permute-start.8) | collective-permute-done | bytes 262176 | tf_op jit(solution)/shard_map/ppermute | solution.py:323
  118.2 3.8 %collective-permute-start.12 = (bf16[64,2048]{1,0:T(8,128)(2,1)S(1)}, bf16[64,2048]{1,0:T(8,128)(2,1)S(1)}, u32[]{:S(2)}, u32[]{:S(2)}) collective-permute-start(bf16[64,2048]{1,0:T(8,128)(2,1)S(1)} %multiply_convert_fusion.refs_1_), channel_id=1, source_target_pairs={{0,1},{1,0},{2,3},{3,2},{4,5},{5,4},{6,7},{7,6},{8,9},{9,8},{10,11... | collective-permute-start | bytes 786440 | tf_op jit(solution)/shard_map/ppermute | solution.py:323
  123.9 2.4 %collective-permute-start.13 = (bf16[64,2048]{1,0:T(8,128)(2,1)S(1)}, bf16[64,2048]{1,0:T(8,128)(2,1)S(1)}, u32[]{:S(2)}, u32[]{:S(2)}) collective-permute-start(bf16[64,2048]{1,0:T(8,128)(2,1)S(1)} %collective-permute-done.9.refs_2_), channel_id=1, source_target_pairs={{0,1},{1,0},{2,3},{3,2},{4,5},{5,4},{6,7},{7,6},{8,9},{9,8},{10,11... | collective-permute-start | bytes 786440 | tf_op jit(solution)/shard_map/ppermute | solution.py:323
  126.4 3.6 %collective-permute-start.14 = (bf16[64,2048]{1,0:T(8,128)(2,1)S(1)}, bf16[64,2048]{1,0:T(8,128)(2,1)S(1)}, u32[]{:S(2)}, u32[]{:S(2)}) collective-permute-start(bf16[64,2048]{1,0:T(8,128)(2,1)S(1)} %collective-permute-done.10.refs_3_), channel_id=1, source_target_pairs={{0,1},{1,0},{2,3},{3,2},{4,5},{5,4},{6,7},{7,6},{8,9},{9,8},{10,11... | collective-permute-start | bytes 786440 | tf_op jit(solution)/shard_map/ppermute | solution.py:323
  132.3 5.2 %project.1 = bf16[4,256,128]{2,1,0:T(8,128)(2,1)S(1)} custom-call(s32[4]{0:T(128)S(1)} %pad_add_fusion.scal_ref, bf16[64,2048]{1,0:T(8,128)(2,1)S(1)} %collective-permute-done.8.refs_0_, bf16[64,2048]{1,0:T(8,128)(2,1)S(1)} %multiply_convert_fusion.refs_1_, bf16[64,2048]{1,0:T(8,128)(2,1)S(1)} %collective-permute-done.9.refs_2_, ...), custom_call_target="tpu_custom_call" | custom-call | flops 4600000000 | bytes 14000000 | tf_op jit(solution)/shard_map/project/pallas_call | solution.py:249
  137.5 26.2 %all_to_all.25.got_ref = bf16[4,256,128]{2,1,0:T(8,128)(2,1)S(1)} all-to-all(bf16[4,256,128]{2,1,0:T(8,128)(2,1)S(1)} %project.1), channel_id=1, replica_groups=mesh['grp'=16,'zq'=4,'zr'=4,'core'=2] {'zq'}, dimensions={0} | all-to-all | bytes 524288 | tf_op jit(solution)/shard_map/all_to_all | solution.py:372
  165.6 16.1 %all_to_all.26 = bf16[16,128,128]{2,1,0:T(8,128)(2,1)S(1)} all-to-all(bf16[16,128,128]{2,1,0:T(8,128)(2,1)S(1)} %bitcast.9), channel_id=1, replica_groups=mesh['grp'=16,'zq'=4,'zr'=4,'core'=2] {'grp'}, dimensions={0} | all-to-all | bytes 1048576 | tf_op jit(solution)/shard_map/all_to_all | solution.py:383
  (50 shorter events, 19.5 us)
Async XLA Ops:
  6.5 125.7 %all-gather.4.cloned.1.call-start = ((), (), s32[]{:S(2)}) async-start(), calls=%async_computation.3 | async-start | bytes 4456448 | tf_op jit(solution)/shard_map/all_gather | solution.py:333
  12.7 4.1 %copy-start.6 = (bf16[256,128]{1,0:T(8,128)(2,1)S(1)}, bf16[256,128]{1,0:T(8,128)(2,1)}, u32[]{:S(2)}) copy-start(bf16[256,128]{1,0:T(8,128)(2,1)} %param.11) | copy-start | bytes 196612
  42.4 16.7 %collective-permute-start = (bf16[3,128,1024]{2,1,0:T(8,128)(2,1)}, bf16[3,128,1024]{2,1,0:T(8,128)(2,1)S(1)}, u32[]{:S(2)}, u32[]{:S(2)}) collective-permute-start(bf16[3,128,1024]{2,1,0:T(8,128)(2,1)} %get-tuple-element.60), channel_id=1, source_target_pairs={{0,1},{1,0},{2,3},{3,2},{4,5},{5,4},{6,7},{7,6},{8,9},{9,8},{10,11... | collective-permute-start | bytes 2359304 | tf_op jit(solution)/shard_map/ppermute | solution.py:323
  47.8 19.4 %collective-permute-start.1 = (bf16[3,128,1024]{2,1,0:T(8,128)(2,1)}, bf16[3,128,1024]{2,1,0:T(8,128)(2,1)S(1)}, u32[]{:S(2)}, u32[]{:S(2)}) collective-permute-start(bf16[3,128,1024]{2,1,0:T(8,128)(2,1)} %get-tuple-element.59.a_ref), channel_id=1, source_target_pairs={{0,30},{2,0},{4,2},{6,4},{8,6},{10,8},{12,10},{14,12},{16,14},{18,... | collective-permute-start | bytes 2359304 | tf_op jit(solution)/shard_map/ppermute | solution.py:323
  50.4 23.2 %collective-permute-start.2 = (bf16[3,128,1024]{2,1,0:T(8,128)(2,1)}, bf16[3,128,1024]{2,1,0:T(8,128)(2,1)S(1)}, u32[]{:S(2)}, u32[]{:S(2)}) collective-permute-start(bf16[3,128,1024]{2,1,0:T(8,128)(2,1)} %get-tuple-element.60), channel_id=1, source_target_pairs={{1,30},{3,0},{5,2},{7,4},{9,6},{11,8},{13,10},{15,12},{17,14},{19,... | collective-permute-start | bytes 2359304 | tf_op jit(solution)/shard_map/ppermute | solution.py:323
  53.5 36.7 %collective-permute-start.4 = (bf16[3,128,1024]{2,1,0:T(8,128)(2,1)S(1)}, bf16[3,128,1024]{2,1,0:T(8,128)(2,1)S(1)}, u32[]{:S(2)}, u32[]{:S(2)}) collective-permute-start(bf16[3,128,1024]{2,1,0:T(8,128)(2,1)S(1)} %get-tuple-element.67), channel_id=1, source_target_pairs={{0,1},{1,0},{2,3},{3,2},{4,5},{5,4},{6,7},{7,6},{8,9},{9,8},{10,11... | collective-permute-start | bytes 2359304 | tf_op jit(solution)/shard_map/ppermute | solution.py:323
  55.8 34.4 %collective-permute-start.5 = (bf16[3,128,1024]{2,1,0:T(8,128)(2,1)S(1)}, bf16[3,128,1024]{2,1,0:T(8,128)(2,1)S(1)}, u32[]{:S(2)}, u32[]{:S(2)}) collective-permute-start(bf16[3,128,1024]{2,1,0:T(8,128)(2,1)S(1)} %get-tuple-element.66.a_ref), channel_id=1, source_target_pairs={{0,30},{2,0},{4,2},{6,4},{8,6},{10,8},{12,10},{14,12},{16,14},{18,... | collective-permute-start | bytes 2359304 | tf_op jit(solution)/shard_map/ppermute | solution.py:323
  59.1 31.1 %collective-permute-start.6 = (bf16[3,128,1024]{2,1,0:T(8,128)(2,1)S(1)}, bf16[3,128,1024]{2,1,0:T(8,128)(2,1)}, u32[]{:S(2)}, u32[]{:S(2)}) collective-permute-start(bf16[3,128,1024]{2,1,0:T(8,128)(2,1)S(1)} %get-tuple-element.67), channel_id=1, source_target_pairs={{1,30},{3,0},{5,2},{7,4},{9,6},{11,8},{13,10},{15,12},{17,14},{19,... | collective-permute-start | bytes 2359304 | tf_op jit(solution)/shard_map/ppermute | solution.py:323
  63.6 15.8 %copy-start = (bf16[512,128]{1,0:T(8,128)(2,1)}, bf16[512,128]{1,0:T(8,128)(2,1)S(1)}, u32[]{:S(2)}) copy-start(bf16[512,128]{1,0:T(8,128)(2,1)S(1)} %get-tuple-element.68.qhot_ref) | copy-start | bytes 393220
  63.6 15.8 %copy-start.2 = (bf16[512,128]{1,0:T(8,128)(2,1)}, bf16[512,128]{1,0:T(8,128)(2,1)S(1)}, u32[]{:S(2)}) copy-start(bf16[512,128]{1,0:T(8,128)(2,1)S(1)} %get-tuple-element.69.khot_ref) | copy-start | bytes 393220
  63.6 15.8 %copy-start.4 = (bf16[128,512]{1,0:T(8,128)(2,1)}, bf16[128,512]{1,0:T(8,128)(2,1)S(1)}, u32[]{:S(2)}) copy-start(bf16[128,512]{1,0:T(8,128)(2,1)S(1)} %get-tuple-element.70.pool_ref) | copy-start | bytes 393220
  63.6 19.0 %copy-start.8 = (bf16[128]{0:T(256)(128)(2,1)S(1)}, bf16[128]{0:T(256)(128)(2,1)}, u32[]{:S(2)}) copy-start(bf16[128]{0:T(256)(128)(2,1)} %param.10) | copy-start | bytes 772
  79.5 10.7 %collective-permute-start.3 = (bf16[64,1024]{1,0:T(8,128)(2,1)S(1)}, bf16[64,1024]{1,0:T(8,128)(2,1)}, u32[]{:S(2)}, u32[]{:S(2)}) collective-permute-start(bf16[64,1024]{1,0:T(8,128)(2,1)S(1)} %get-tuple-element.65), channel_id=1, source_target_pairs={{0,2},{2,4},{4,6},{6,8},{8,10},{10,12},{12,14},{14,16},{16,18},{18... | collective-permute-start | bytes 393224 | tf_op jit(solution)/shard_map/ppermute | solution.py:323
  83.2 20.3 %all-to-all-start = ((bf16[32,1,128]{2,1,0:T(2,128)(2,1)}), bf16[32,1,128]{2,1,0:T(2,128)(2,1)S(1)}, u32[]{:S(2)}, u32[]{:S(2)}) async-start(bf16[32,1,128]{2,1,0:T(2,128)(2,1)} %copy.17), calls=%async_computation | async-start | bytes 32768 | tf_op jit(solution)/shard_map/all_to_all | solution.py:355
  90.2 0.9 copy-start.1
  92.9 37.1 %copy-start.7 = (s32[16384]{0:T(1024)S(1)}, s32[16384]{0:T(1024)}, u32[]{:S(2)}) copy-start(s32[16384]{0:T(1024)} %param.13) | copy-start | bytes 196612
  98.9 6.5 %collective-permute-start.7 = (bf16[64,1024]{1,0:T(8,128)(2,1)S(1)}, bf16[64,1024]{1,0:T(8,128)(2,1)S(1)}, u32[]{:S(2)}, u32[]{:S(2)}) collective-permute-start(bf16[64,1024]{1,0:T(8,128)(2,1)S(1)} %get-tuple-element.72), channel_id=1, source_target_pairs={{0,2},{2,4},{4,6},{6,8},{8,10},{10,12},{12,14},{14,16},{16,18},{18... | collective-permute-start | bytes 393224 | tf_op jit(solution)/shard_map/ppermute | solution.py:323
  105.5 10.8 %collective-permute-start.8 = (bf16[64,2048]{1,0:T(8,128)(2,1)S(1)}, bf16[64,2048]{1,0:T(8,128)(2,1)S(1)}, u32[]{:S(2)}, u32[]{:S(2)}) collective-permute-start(bf16[64,2048]{1,0:T(8,128)(2,1)S(1)} %multiply_convert_fusion.refs_1_), channel_id=1, source_target_pairs={{0,2},{1,3},{2,4},{3,5},{4,6},{5,7},{6,8},{7,9},{8,10},{9,11},{10,... | collective-permute-start | bytes 786440 | tf_op jit(solution)/shard_map/ppermute | solution.py:323
  108.4 15.5 %collective-permute-start.9 = (bf16[64,2048]{1,0:T(8,128)(2,1)S(1)}, bf16[64,2048]{1,0:T(8,128)(2,1)S(1)}, u32[]{:S(2)}, u32[]{:S(2)}) collective-permute-start(bf16[64,2048]{1,0:T(8,128)(2,1)S(1)} %multiply_convert_fusion.refs_1_), channel_id=1, source_target_pairs={{0,30},{1,31},{2,0},{3,1},{4,2},{5,3},{6,4},{7,5},{8,6},{9,7},{10,... | collective-permute-start | bytes 786440 | tf_op jit(solution)/shard_map/ppermute | solution.py:323
  116.3 10.1 %collective-permute-start.10 = (bf16[64,2048]{1,0:T(8,128)(2,1)S(1)}, bf16[64,2048]{1,0:T(8,128)(2,1)S(1)}, u32[]{:S(2)}, u32[]{:S(2)}) collective-permute-start(bf16[64,2048]{1,0:T(8,128)(2,1)S(1)} %collective-permute-done.8.refs_0_), channel_id=1, source_target_pairs={{0,2},{1,3},{2,4},{3,5},{4,6},{5,7},{6,8},{7,9},{8,10},{9,11},{10,... | collective-permute-start | bytes 786440 | tf_op jit(solution)/shard_map/ppermute | solution.py:323
  118.2 14.0 %collective-permute-start.12 = (bf16[64,2048]{1,0:T(8,128)(2,1)S(1)}, bf16[64,2048]{1,0:T(8,128)(2,1)S(1)}, u32[]{:S(2)}, u32[]{:S(2)}) collective-permute-start(bf16[64,2048]{1,0:T(8,128)(2,1)S(1)} %multiply_convert_fusion.refs_1_), channel_id=1, source_target_pairs={{0,1},{1,0},{2,3},{3,2},{4,5},{5,4},{6,7},{7,6},{8,9},{9,8},{10,11... | collective-permute-start | bytes 786440 | tf_op jit(solution)/shard_map/ppermute | solution.py:323
  122.0 10.2 %collective-permute-start.11 = (bf16[64,2048]{1,0:T(8,128)(2,1)S(1)}, bf16[64,2048]{1,0:T(8,128)(2,1)S(1)}, u32[]{:S(2)}, u32[]{:S(2)}) collective-permute-start(bf16[64,2048]{1,0:T(8,128)(2,1)S(1)} %collective-permute-done.8.refs_0_), channel_id=1, source_target_pairs={{0,1},{1,0},{2,3},{3,2},{4,5},{5,4},{6,7},{7,6},{8,9},{9,8},{10,11... | collective-permute-start | bytes 786440 | tf_op jit(solution)/shard_map/ppermute | solution.py:323
  123.9 8.3 %collective-permute-start.13 = (bf16[64,2048]{1,0:T(8,128)(2,1)S(1)}, bf16[64,2048]{1,0:T(8,128)(2,1)S(1)}, u32[]{:S(2)}, u32[]{:S(2)}) collective-permute-start(bf16[64,2048]{1,0:T(8,128)(2,1)S(1)} %collective-permute-done.9.refs_2_), channel_id=1, source_target_pairs={{0,1},{1,0},{2,3},{3,2},{4,5},{5,4},{6,7},{7,6},{8,9},{9,8},{10,11... | collective-permute-start | bytes 786440 | tf_op jit(solution)/shard_map/ppermute | solution.py:323
  126.4 5.9 %collective-permute-start.14 = (bf16[64,2048]{1,0:T(8,128)(2,1)S(1)}, bf16[64,2048]{1,0:T(8,128)(2,1)S(1)}, u32[]{:S(2)}, u32[]{:S(2)}) collective-permute-start(bf16[64,2048]{1,0:T(8,128)(2,1)S(1)} %collective-permute-done.10.refs_3_), channel_id=1, source_target_pairs={{0,1},{1,0},{2,3},{3,2},{4,5},{5,4},{6,7},{7,6},{8,9},{9,8},{10,11... | collective-permute-start | bytes 786440 | tf_op jit(solution)/shard_map/ppermute | solution.py:323
  (2 other events, 1.8 us)
Sparse Core Ops, SparseCore 0:
  42.5 65.7 all-gather.3

commit v5 on v4

--- a/solution.py
+++ b/solution.py
@@ -82,7 +82,9 @@
     return jnp.floor((a.astype(F32) + 0.5) / b.astype(F32)).astype(I32)
 
 
-def rope_kernel(scal_ref, grid_ref, q_ref, k_ref, v_ref, own_ref, oth_ref, cos_ref, sin_ref):
+def rope_kernel(scal_ref, grid_ref, q_ref, k_ref, v_ref, *refs):
+    outs = refs[: 2 * CHUNKS]
+    cos_ref, sin_ref = refs[2 * CHUNKS :]
     lane = lax.broadcasted_iota(I32, (BLK, HD), 1)
     low = (lane % 64) < 32
     step = pl.program_id(0)
@@ -103,7 +105,7 @@
     def fill(out_ref):
         cos = cos_ref[...]
         sin = sin_ref[...]
-        for h in range(STEP):
+        for h in range(HEADS):
             lanes = slice(h * HD, (h + 1) * HD)
             for i, ref in ((0, q_ref), (1, k_ref)):
                 x = ref[:, lanes].astype(F32)
@@ -111,43 +113,35 @@
                 out_ref[i, :, lanes] = (x * cos + swap * sin).astype(BF16)
         out_ref[2] = v_ref[...]
 
-    n = HEADS // STEP
-
-    @pl.when(step < n)
-    def _():
-        fill(oth_ref)
-
-    @pl.when(step >= n)
-    def _():
-        fill(own_ref)
-
-
-def rope(scal, grids, queries, keys, values, chunk):
-    n = HEADS // STEP
-    lanes = STEP * HD
+    for i in range(2 * CHUNKS):
+
+        @pl.when(step == i)
+        def _(out_ref=outs[i]):
+            fill(out_ref)
+
+
+def rope(scal, grids, queries, keys, values):
     queries, keys, values = (pltpu.with_memory_space_constraint(x, pltpu.HBM) for x in (queries, keys, values))
 
     def src(i, scal_ref):
-        half = jnp.where(i < n, 1 - scal_ref[1], scal_ref[1])
-        return (0, half * (HALF // lanes) + chunk * n + i % n)
-
-    return pl.pallas_call(
+        half = jnp.where(i % 2 == 0, scal_ref[1], 1 - scal_ref[1])
+        return (0, half * (HALF // WIDE) + i // 2)
+
+    outs = pl.pallas_call(
         rope_kernel,
-        out_shape=[jax.ShapeDtypeStruct((3, BLK, WIDE), BF16)] * 2,
+        out_shape=[jax.ShapeDtypeStruct((3, BLK, WIDE), BF16)] * (2 * CHUNKS),
         grid_spec=pltpu.PrefetchScalarGridSpec(
             num_scalar_prefetch=1,
-            grid=(2 * n,),
-            in_specs=[smem()] + [pl.BlockSpec((BLK, lanes), src)] * 3,
-            out_specs=[
-                pl.BlockSpec((3, BLK, lanes), lambda i, _: (0, 0, jnp.maximum(i - n, 0))),
-                pl.BlockSpec((3, BLK, lanes), lambda i, _: (0, 0, jnp.minimum(i, n - 1))),
-            ],
+            grid=(2 * CHUNKS,),
+            in_specs=[smem()] + [pl.BlockSpec((BLK, WIDE), src)] * 3,
+            out_specs=[pl.BlockSpec((3, BLK, WIDE), lambda i, _: (0, 0, 0))] * (2 * CHUNKS),
             scratch_shapes=[pltpu.VMEM((BLK, HD), F32)] * 2,
         ),
-        compiler_params=params(16),
-        cost_estimate=cost(4),
+        compiler_params=params(24),
+        cost_estimate=cost(6),
         name="rope",
     )(scal, grids, queries, keys, values)
+    return [outs[2 * c : 2 * c + 2] for c in range(CHUNKS)]
 
 
 def layout_kernel(scal_ref, grid_ref, qhot_ref, khot_ref, pool_ref):
@@ -220,6 +214,7 @@
 
 def attend(parts, tables):
     part = pl.BlockSpec((3, BLK, STEP * HD), lambda h: (0, 0, h))
+    tables = [pltpu.with_memory_space_constraint(t, pltpu.HBM) for t in tables]
     whole = [pl.BlockSpec(t.shape, lambda h: (0, 0)) for t in tables]
     return pl.pallas_call(
         attend_kernel,
@@ -237,27 +232,32 @@
     w_own_ref, w_oth_ref, out_ref = refs[-3:]
     own = jnp.concatenate([ref[...] for ref in refs[:NB]], axis=0)
     oth = jnp.concatenate([ref[...] for ref in refs[NB : 2 * NB]], axis=0)
-    total = jnp.dot(own, w_own_ref[...].reshape(HALF, HD), preferred_element_type=F32)
-    total += jnp.dot(oth, w_oth_ref[...].reshape(HALF, HD), preferred_element_type=F32)
-    out_ref[0] = total.astype(BF16)
+
+    def pair(ref):
+        return jnp.concatenate([ref[:, i].reshape(HALF, HD) for i in range(2)], axis=1)
+
+    total = jnp.dot(own, pair(w_own_ref), preferred_element_type=F32)
+    total += jnp.dot(oth, pair(w_oth_ref), preferred_element_type=F32)
+    for i in range(2):
+        out_ref[i] = total[:, i * HD : (i + 1) * HD].astype(BF16)
 
 
 def project(scal, own, oth, cols):
     rows = NB * ROWS
-    half = (GROUPS // 2, 1, 2 * BLK, HD)
+    half = (GROUPS // 2, 2, 2 * BLK, HD)
     cols = pltpu.with_memory_space_constraint(cols, pltpu.HBM)
     return pl.pallas_call(
         project_kernel,
         out_shape=jax.ShapeDtypeStruct((QUADS, rows, HD), BF16),
         grid_spec=pltpu.PrefetchScalarGridSpec(
             num_scalar_prefetch=1,
-            grid=(QUADS,),
+            grid=(QUADS // 2,),
             in_specs=[pl.BlockSpec((ROWS, HALF), lambda j, _: (0, 0))] * (2 * NB)
             + [
                 pl.BlockSpec(half, lambda j, s: (s[1], j, 0, 0)),
                 pl.BlockSpec(half, lambda j, s: (1 - s[1], j, 0, 0)),
             ],
-            out_specs=pl.BlockSpec((1, rows, HD), lambda j, _: (j, 0, 0)),
+            out_specs=pl.BlockSpec((2, rows, HD), lambda j, _: (j, 0, 0)),
         ),
         compiler_params=params(24),
         cost_estimate=cost(4),
@@ -322,17 +322,12 @@
     def move(x, perm):
         return lax.ppermute(x, MLP, perm)
 
-    parts = []
-    order = scal
-    for chunk in range(CHUNKS):
-        own, oth = rope(order, grids, queries, keys, values, chunk)
-        if chunk == 1:
-            w_merge, own, oth = lax.optimization_barrier((w_merge, own, oth))
-            cols = lax.all_gather(w_merge, "zq", axis=0)
-            own, oth, cols = lax.optimization_barrier((own, oth, cols))
-            cols = lax.all_gather(cols, "grp", axis=0)
-        order, own, oth = lax.optimization_barrier((order, own, oth))
-        parts.append([own, move(oth, PART), move(own, SAME), move(oth, OPP)])
+    halves = rope(scal, grids, queries, keys, values)
+    w_merge, halves = lax.optimization_barrier((w_merge, halves))
+    cols = lax.all_gather(w_merge, "zq", axis=0)
+    halves, cols = lax.optimization_barrier((halves, cols))
+    cols = lax.all_gather(cols, "grp", axis=0)
+    parts = [[own, move(oth, PART), move(own, SAME), move(oth, OPP)] for own, oth in halves]
 
     tables = pl.pallas_call(
         layout_kernel,
@@ -350,10 +345,10 @@
         compiler_params=params(24),
         name="index",
     )(scal, positions.reshape(GROUPS, GPOOL))
-    owns, tables = lax.optimization_barrier(([p[0] for p in parts], tables))
-    gains, _ = lax.optimization_barrier((jnp.broadcast_to(gamma[None, :], (2 * CHIPS, HD)), owns))
+    gains, _ = lax.optimization_barrier((jnp.broadcast_to(gamma[None, :], (2 * CHIPS, HD)), halves))
     gains = lax.all_to_all(gains, MLP, split_axis=0, concat_axis=0, tiled=True)
     gains = lax.dynamic_slice_in_dim(gains, core * CHIPS, CHIPS, 0).reshape(1, HALF).astype(F32)
+    owns, tables, to, frm, gains = lax.optimization_barrier(([p[0] for p in parts], tables, to, frm, gains))
     pooled = []
     for chunk in range(CHUNKS):
         mid, edge = attend([owns[chunk]] + parts[chunk][1:], tables)
@@ -367,7 +362,7 @@
     last = move(below, UP)
     own = (below, rows, above, last)
     oth = [move(x, PART) for x in own]
-    cols, to, frm, _ = lax.optimization_barrier((cols, to, frm, (below, above)))
+    cols, _ = lax.optimization_barrier((cols, (below, above)))
     out = project(scal, own, oth, cols)
     out = lax.all_to_all(out, "zq", split_axis=0, concat_axis=0, tiled=True)
 

time: 194 us -> 181 us (0.933)
  the two profiles are of different devices: /device:TPU:1 before, /device:TPU:32 now
where the time goes in v5:
time: 181 us
  blocking collectives  74.4 us (41%)
  starting transfers between devices  52.7 us (29%)
  Pallas kernels  27.8 us (15%)
  between operations  13.7 us (8%)
  waiting for transfers between devices  8.51 us (5%)
  local copies, waits for them, and re-layouts  3.36 us (2%)
    ppermute x15, starting transfers between devices, move(): return lax.ppermute(x, MLP, perm)  44.2 us
    all_to_all x1, blocking collectives, body(): out = lax.all_to_all(out, 'zq', split_axis=0, concat_axis=0, tiled=True)  30.7 us
    all_gather x1, blocking collectives, body(): cols = lax.all_gather(w_merge, 'zq', axis=0)  26.6 us
    all_to_all x1, blocking collectives, body(): out = lax.all_to_all(out, 'grp', split_axis=0, concat_axis=0, tiled=True)  17.1 us
    pallas_call x2, Pallas kernels, attend(): pl.pallas_call(attend_kernel, grid=(HEADS // STEP,), out_shape=[jax.Shape...  12.4 us
    all_to_all x1, starting transfers between devices, body(): gains = lax.all_to_all(gains, MLP, split_axis=0, concat_axis=0, tiled=True)  8.49 us
    ppermute x15, waiting for transfers between devices, move(): return lax.ppermute(x, MLP, perm)  8.47 us
    pallas_call x1, Pallas kernels, rope(): pl.pallas_call(rope_kernel, out_shape=[jax.ShapeDtypeStruct((3, BLK, WIDE...  4.62 us
  transfers between devices with their start and end apart: 17, of which 4 were waited for; matrix products, arithmetic and copies ran while one was open for 0% of the time, Pallas kernels for 9%

profile of v5, /device:TPU:32, one launch (start us, length us, event | category | flops | bytes accessed | tf_op | source)
XLA Modules:
  0.0 180.7 jit_solution(16318803969629208738)
XLA Ops:
  7.4 4.6 %rope.1 = (bf16[3,128,1024]{2,1,0:T(8,128)(2,1)S(1)}, bf16[3,128,1024]{2,1,0:T(8,128)(2,1)S(1)}, bf16[3,128,1024]{2,1,0:T(8,128)(2,1)S(1)}, bf16[3,128,1024]{2,1,0:T(8,128)(2,1)S(1)}) custom-call(s32[4]{0:T(128)S(1)} %pad_add_fusion.scal_ref, s32[16,2]{1,0:T(8,128)S(1)} %copy.12.grid_ref, bf16[128,4096]{1,0:T(8,128)(2,1)} %q_ref.1, bf16[128,4096]{1,0:T(8,128)(2,1)} %k_ref.1, ...), custom_call_target="tpu_custom_call" | custom-call | flops 6899999744 | bytes 21000000 | tf_op jit(solution)/shard_map/rope/pallas_call | solution.py:130
  12.0 26.6 %all-gather = bf16[1024,128]{1,0:T(8,128)(2,1)} all-gather(bf16[256,128]{1,0:T(8,128)(2,1)S(1)} %copy-done.3), channel_id=2, replica_groups=mesh['grp'=16,'zq'=4,'zr'=4,'core'=2] {'zq'}, dimensions={0}, use_global_device_ids=true | all-gather | bytes 327680 | tf_op jit(solution)/shard_map/all_gather | solution.py:327
  40.6 3.0 %collective-permute-start.1 = (bf16[3,128,1024]{2,1,0:T(8,128)(2,1)S(1)}, bf16[3,128,1024]{2,1,0:T(8,128)(2,1)}, u32[]{:S(2)}, u32[]{:S(2)}) collective-permute-start(bf16[3,128,1024]{2,1,0:T(8,128)(2,1)S(1)} %get-tuple-element.62.a_ref), channel_id=1, source_target_pairs={{0,30},{2,0},{4,2},{6,4},{8,6},{10,8},{12,10},{14,12},{16,14},{18,... | collective-permute-start | bytes 2359304 | tf_op jit(solution)/shard_map/ppermute | solution.py:323
  43.6 2.7 %collective-permute-start.2 = (bf16[3,128,1024]{2,1,0:T(8,128)(2,1)S(1)}, bf16[3,128,1024]{2,1,0:T(8,128)(2,1)}, u32[]{:S(2)}, u32[]{:S(2)}) collective-permute-start(bf16[3,128,1024]{2,1,0:T(8,128)(2,1)S(1)} %get-tuple-element.57), channel_id=1, source_target_pairs={{1,30},{3,0},{5,2},{7,4},{9,6},{11,8},{13,10},{15,12},{17,14},{19,... | collective-permute-start | bytes 2359304 | tf_op jit(solution)/shard_map/ppermute | solution.py:323
  47.0 8.5 %all-to-all-start = ((bf16[32,1,128]{2,1,0:T(2,128)(2,1)}), bf16[32,1,128]{2,1,0:T(2,128)(2,1)S(1)}, u32[]{:S(2)}, u32[]{:S(2)}) async-start(bf16[32,1,128]{2,1,0:T(2,128)(2,1)} %copy.14), calls=%async_computation | async-start | bytes 32768 | tf_op jit(solution)/shard_map/all_to_all | solution.py:349
  55.5 2.1 %collective-permute-start.4 = (bf16[3,128,1024]{2,1,0:T(8,128)(2,1)S(1)}, bf16[3,128,1024]{2,1,0:T(8,128)(2,1)}, u32[]{:S(2)}, u32[]{:S(2)}) collective-permute-start(bf16[3,128,1024]{2,1,0:T(8,128)(2,1)S(1)} %get-tuple-element.58), channel_id=1, source_target_pairs={{0,1},{1,0},{2,3},{3,2},{4,5},{5,4},{6,7},{7,6},{8,9},{9,8},{10,11... | collective-permute-start | bytes 2359304 | tf_op jit(solution)/shard_map/ppermute | solution.py:323
  57.6 2.3 %collective-permute-start.5 = (bf16[3,128,1024]{2,1,0:T(8,128)(2,1)S(1)}, bf16[3,128,1024]{2,1,0:T(8,128)(2,1)}, u32[]{:S(2)}, u32[]{:S(2)}) collective-permute-start(bf16[3,128,1024]{2,1,0:T(8,128)(2,1)S(1)} %get-tuple-element.68.a_ref), channel_id=1, source_target_pairs={{0,30},{2,0},{4,2},{6,4},{8,6},{10,8},{12,10},{14,12},{16,14},{18,... | collective-permute-start | bytes 2359304 | tf_op jit(solution)/shard_map/ppermute | solution.py:323
  63.0 2.2 %index.1 = (s32[1,1024]{1,0:T(1,128)S(1)}, s32[1,2048]{1,0:T(1,128)S(1)}) custom-call(s32[4]{0:T(128)S(1)} %pad_add_fusion.scal_ref, s32[16,1024]{1,0:T(8,128)S(1)} %reshape.25.pos_ref), custom_call_target="tpu_custom_call" | custom-call | tf_op jit(solution)/shard_map/index/pallas_call | solution.py:340
  65.2 4.2 %collective-permute-start.6 = (bf16[3,128,1024]{2,1,0:T(8,128)(2,1)S(1)}, bf16[3,128,1024]{2,1,0:T(8,128)(2,1)}, u32[]{:S(2)}, u32[]{:S(2)}) collective-permute-start(bf16[3,128,1024]{2,1,0:T(8,128)(2,1)S(1)} %get-tuple-element.58), channel_id=1, source_target_pairs={{1,30},{3,0},{5,2},{7,4},{9,6},{11,8},{13,10},{15,12},{17,14},{19,... | collective-permute-start | bytes 2359304 | tf_op jit(solution)/shard_map/ppermute | solution.py:323
  69.4 6.2 %attend.2 = (bf16[64,1024]{1,0:T(8,128)(2,1)S(1)}, bf16[64,1024]{1,0:T(8,128)(2,1)S(1)}) custom-call(bf16[3,128,1024]{2,1,0:T(8,128)(2,1)S(1)} %get-tuple-element.62.a_ref, bf16[3,128,1024]{2,1,0:T(8,128)(2,1)} %collective-permute-done.b_ref, bf16[3,128,1024]{2,1,0:T(8,128)(2,1)} %collective-permute-done.1.c_ref, ...), custom_call_target="tpu_custom_call" | custom-call | flops 6899999744 | bytes 21000000 | tf_op jit(solution)/shard_map/attend/pallas_call | solution.py:219
  75.7 4.6 %collective-permute-start.3 = (bf16[64,1024]{1,0:T(8,128)(2,1)S(1)}, bf16[64,1024]{1,0:T(8,128)(2,1)S(1)}, u32[]{:S(2)}, u32[]{:S(2)}) collective-permute-start(bf16[64,1024]{1,0:T(8,128)(2,1)S(1)} %get-tuple-element.67), channel_id=1, source_target_pairs={{0,2},{2,4},{4,6},{6,8},{8,10},{10,12},{12,14},{14,16},{16,18},{18... | collective-permute-start | bytes 393224 | tf_op jit(solution)/shard_map/ppermute | solution.py:323
  80.2 2.5 %collective-permute-done.3 = bf16[64,1024]{1,0:T(8,128)(2,1)S(1)} collective-permute-done((bf16[64,1024]{1,0:T(8,128)(2,1)S(1)}, bf16[64,1024]{1,0:T(8,128)(2,1)S(1)}, u32[]{:S(2)}, u32[]{:S(2)}) %collective-permute-start.3) | collective-permute-done | bytes 131104 | tf_op jit(solution)/shard_map/ppermute | solution.py:323
  82.8 6.2 %attend.3 = (bf16[64,1024]{1,0:T(8,128)(2,1)S(1)}, bf16[64,1024]{1,0:T(8,128)(2,1)S(1)}) custom-call(bf16[3,128,1024]{2,1,0:T(8,128)(2,1)S(1)} %get-tuple-element.68.a_ref, bf16[3,128,1024]{2,1,0:T(8,128)(2,1)} %collective-permute-done.4.b_ref, bf16[3,128,1024]{2,1,0:T(8,128)(2,1)} %collective-permute-done.5.c_ref, ...), custom_call_target="tpu_custom_call" | custom-call | flops 6899999744 | bytes 21000000 | tf_op jit(solution)/shard_map/attend/pallas_call | solution.py:219
  89.0 4.4 %collective-permute-start.7 = (bf16[64,1024]{1,0:T(8,128)(2,1)S(1)}, bf16[64,1024]{1,0:T(8,128)(2,1)S(1)}, u32[]{:S(2)}, u32[]{:S(2)}) collective-permute-start(bf16[64,1024]{1,0:T(8,128)(2,1)S(1)} %get-tuple-element.73), channel_id=1, source_target_pairs={{0,2},{2,4},{4,6},{6,8},{8,10},{10,12},{12,14},{14,16},{16,18},{18... | collective-permute-start | bytes 393224 | tf_op jit(solution)/shard_map/ppermute | solution.py:323
  93.4 2.5 %collective-permute-done.7 = bf16[64,1024]{1,0:T(8,128)(2,1)S(1)} collective-permute-done((bf16[64,1024]{1,0:T(8,128)(2,1)S(1)}, bf16[64,1024]{1,0:T(8,128)(2,1)S(1)}, u32[]{:S(2)}, u32[]{:S(2)}) %collective-permute-start.7) | collective-permute-done | bytes 131104 | tf_op jit(solution)/shard_map/ppermute | solution.py:323
  95.9 4.4 %collective-permute-start.8 = (bf16[64,2048]{1,0:T(8,128)(2,1)S(1)}, bf16[64,2048]{1,0:T(8,128)(2,1)S(1)}, u32[]{:S(2)}, u32[]{:S(2)}) collective-permute-start(bf16[64,2048]{1,0:T(8,128)(2,1)S(1)} %multiply_convert_fusion.refs_1_), channel_id=1, source_target_pairs={{0,2},{1,3},{2,4},{3,5},{4,6},{5,7},{6,8},{7,9},{8,10},{9,11},{10,... | collective-permute-start | bytes 786440 | tf_op jit(solution)/shard_map/ppermute | solution.py:323
  100.3 2.4 %collective-permute-start.9 = (bf16[64,2048]{1,0:T(8,128)(2,1)S(1)}, bf16[64,2048]{1,0:T(8,128)(2,1)S(1)}, u32[]{:S(2)}, u32[]{:S(2)}) collective-permute-start(bf16[64,2048]{1,0:T(8,128)(2,1)S(1)} %multiply_convert_fusion.refs_1_), channel_id=1, source_target_pairs={{0,30},{1,31},{2,0},{3,1},{4,2},{5,3},{6,4},{7,5},{8,6},{9,7},{10,... | collective-permute-start | bytes 786440 | tf_op jit(solution)/shard_map/ppermute | solution.py:323
  102.7 2.4 %collective-permute-done.8.refs_0_ = bf16[64,2048]{1,0:T(8,128)(2,1)S(1)} collective-permute-done((bf16[64,2048]{1,0:T(8,128)(2,1)S(1)}, bf16[64,2048]{1,0:T(8,128)(2,1)S(1)}, u32[]{:S(2)}, u32[]{:S(2)}) %collective-permute-start.8) | collective-permute-done | bytes 262176 | tf_op jit(solution)/shard_map/ppermute | solution.py:323
  105.1 3.7 %collective-permute-start.10 = (bf16[64,2048]{1,0:T(8,128)(2,1)S(1)}, bf16[64,2048]{1,0:T(8,128)(2,1)S(1)}, u32[]{:S(2)}, u32[]{:S(2)}) collective-permute-start(bf16[64,2048]{1,0:T(8,128)(2,1)S(1)} %collective-permute-done.8.refs_0_), channel_id=1, source_target_pairs={{0,2},{1,3},{2,4},{3,5},{4,6},{5,7},{6,8},{7,9},{8,10},{9,11},{10,... | collective-permute-start | bytes 786440 | tf_op jit(solution)/shard_map/ppermute | solution.py:323
  110.8 2.4 %collective-permute-start.11 = (bf16[64,2048]{1,0:T(8,128)(2,1)S(1)}, bf16[64,2048]{1,0:T(8,128)(2,1)S(1)}, u32[]{:S(2)}, u32[]{:S(2)}) collective-permute-start(bf16[64,2048]{1,0:T(8,128)(2,1)S(1)} %collective-permute-done.8.refs_0_), channel_id=1, source_target_pairs={{0,1},{1,0},{2,3},{3,2},{4,5},{5,4},{6,7},{7,6},{8,9},{9,8},{10,11... | collective-permute-start | bytes 786440 | tf_op jit(solution)/shard_map/ppermute | solution.py:323
  115.1 2.4 %collective-permute-start.14 = (bf16[64,2048]{1,0:T(8,128)(2,1)S(1)}, bf16[64,2048]{1,0:T(8,128)(2,1)S(1)}, u32[]{:S(2)}, u32[]{:S(2)}) collective-permute-start(bf16[64,2048]{1,0:T(8,128)(2,1)S(1)} %collective-permute-done.10.refs_3_), channel_id=1, source_target_pairs={{0,1},{1,0},{2,3},{3,2},{4,5},{5,4},{6,7},{7,6},{8,9},{9,8},{10,11... | collective-permute-start | bytes 786440 | tf_op jit(solution)/shard_map/ppermute | solution.py:323
  118.7 3.6 %project.1 = bf16[4,256,128]{2,1,0:T(8,128)(2,1)S(1)} custom-call(s32[4]{0:T(128)S(1)} %pad_add_fusion.scal_ref, bf16[64,2048]{1,0:T(8,128)(2,1)S(1)} %collective-permute-done.8.refs_0_, bf16[64,2048]{1,0:T(8,128)(2,1)S(1)} %multiply_convert_fusion.refs_1_, bf16[64,2048]{1,0:T(8,128)(2,1)S(1)} %collective-permute-done.9.refs_2_, ...), custom_call_target="tpu_custom_call" | custom-call | flops 4600000000 | bytes 14000000 | tf_op jit(solution)/shard_map/project/pallas_call | solution.py:249
  122.3 30.7 %all_to_all.25.got_ref = bf16[4,256,128]{2,1,0:T(8,128)(2,1)S(1)} all-to-all(bf16[4,256,128]{2,1,0:T(8,128)(2,1)S(1)} %project.1), channel_id=1, replica_groups=mesh['grp'=16,'zq'=4,'zr'=4,'core'=2] {'zq'}, dimensions={0} | all-to-all | bytes 524288 | tf_op jit(solution)/shard_map/all_to_all | solution.py:367
  154.8 17.1 %all_to_all.26 = bf16[16,128,128]{2,1,0:T(8,128)(2,1)S(1)} all-to-all(bf16[16,128,128]{2,1,0:T(8,128)(2,1)S(1)} %bitcast.12), channel_id=1, replica_groups=mesh['grp'=16,'zq'=4,'zr'=4,'core'=2] {'grp'}, dimensions={0} | all-to-all | bytes 1048576 | tf_op jit(solution)/shard_map/all_to_all | solution.py:378
  (43 shorter events, 15.5 us)
Async XLA Ops:
  6.5 111.0 %all-gather.4.cloned.1.call-start = ((), (), s32[]{:S(2)}) async-start(), calls=%async_computation.3 | async-start | bytes 4456448 | tf_op jit(solution)/shard_map/all_gather | solution.py:329
  7.4 4.6 %copy-start.3 = (bf16[256,128]{1,0:T(8,128)(2,1)S(1)}, bf16[256,128]{1,0:T(8,128)(2,1)}, u32[]{:S(2)}) copy-start(bf16[256,128]{1,0:T(8,128)(2,1)} %param.11) | copy-start | bytes 196612
  7.4 39.0 %copy-start.5 = (bf16[128]{0:T(256)(128)(2,1)S(1)}, bf16[128]{0:T(256)(128)(2,1)}, u32[]{:S(2)}) copy-start(bf16[128]{0:T(256)(128)(2,1)} %param.10) | copy-start | bytes 772
  7.4 55.6 %copy-start.4 = (s32[16384]{0:T(1024)S(1)}, s32[16384]{0:T(1024)}, u32[]{:S(2)}) copy-start(s32[16384]{0:T(1024)} %param.13) | copy-start | bytes 196612
  38.7 26.5 %collective-permute-start = (bf16[3,128,1024]{2,1,0:T(8,128)(2,1)S(1)}, bf16[3,128,1024]{2,1,0:T(8,128)(2,1)}, u32[]{:S(2)}, u32[]{:S(2)}) collective-permute-start(bf16[3,128,1024]{2,1,0:T(8,128)(2,1)S(1)} %get-tuple-element.57), channel_id=1, source_target_pairs={{0,1},{1,0},{2,3},{3,2},{4,5},{5,4},{6,7},{7,6},{8,9},{9,8},{10,11... | collective-permute-start | bytes 2359304 | tf_op jit(solution)/shard_map/ppermute | solution.py:323
  40.6 28.8 %collective-permute-start.1 = (bf16[3,128,1024]{2,1,0:T(8,128)(2,1)S(1)}, bf16[3,128,1024]{2,1,0:T(8,128)(2,1)}, u32[]{:S(2)}, u32[]{:S(2)}) collective-permute-start(bf16[3,128,1024]{2,1,0:T(8,128)(2,1)S(1)} %get-tuple-element.62.a_ref), channel_id=1, source_target_pairs={{0,30},{2,0},{4,2},{6,4},{8,6},{10,8},{12,10},{14,12},{16,14},{18,... | collective-permute-start | bytes 2359304 | tf_op jit(solution)/shard_map/ppermute | solution.py:323
  43.6 25.8 %collective-permute-start.2 = (bf16[3,128,1024]{2,1,0:T(8,128)(2,1)S(1)}, bf16[3,128,1024]{2,1,0:T(8,128)(2,1)}, u32[]{:S(2)}, u32[]{:S(2)}) collective-permute-start(bf16[3,128,1024]{2,1,0:T(8,128)(2,1)S(1)} %get-tuple-element.57), channel_id=1, source_target_pairs={{1,30},{3,0},{5,2},{7,4},{9,6},{11,8},{13,10},{15,12},{17,14},{19,... | collective-permute-start | bytes 2359304 | tf_op jit(solution)/shard_map/ppermute | solution.py:323
  47.0 22.4 %all-to-all-start = ((bf16[32,1,128]{2,1,0:T(2,128)(2,1)}), bf16[32,1,128]{2,1,0:T(2,128)(2,1)S(1)}, u32[]{:S(2)}, u32[]{:S(2)}) async-start(bf16[32,1,128]{2,1,0:T(2,128)(2,1)} %copy.14), calls=%async_computation | async-start | bytes 32768 | tf_op jit(solution)/shard_map/all_to_all | solution.py:349
  55.5 27.2 %collective-permute-start.4 = (bf16[3,128,1024]{2,1,0:T(8,128)(2,1)S(1)}, bf16[3,128,1024]{2,1,0:T(8,128)(2,1)}, u32[]{:S(2)}, u32[]{:S(2)}) collective-permute-start(bf16[3,128,1024]{2,1,0:T(8,128)(2,1)S(1)} %get-tuple-element.58), channel_id=1, source_target_pairs={{0,1},{1,0},{2,3},{3,2},{4,5},{5,4},{6,7},{7,6},{8,9},{9,8},{10,11... | collective-permute-start | bytes 2359304 | tf_op jit(solution)/shard_map/ppermute | solution.py:323
  57.6 25.2 %collective-permute-start.5 = (bf16[3,128,1024]{2,1,0:T(8,128)(2,1)S(1)}, bf16[3,128,1024]{2,1,0:T(8,128)(2,1)}, u32[]{:S(2)}, u32[]{:S(2)}) collective-permute-start(bf16[3,128,1024]{2,1,0:T(8,128)(2,1)S(1)} %get-tuple-element.68.a_ref), channel_id=1, source_target_pairs={{0,30},{2,0},{4,2},{6,4},{8,6},{10,8},{12,10},{14,12},{16,14},{18,... | collective-permute-start | bytes 2359304 | tf_op jit(solution)/shard_map/ppermute | solution.py:323
  61.0 0.7 copy-start
  61.7 0.6 copy-start.1
  62.3 0.7 copy-start.2
  65.2 17.5 %collective-permute-start.6 = (bf16[3,128,1024]{2,1,0:T(8,128)(2,1)S(1)}, bf16[3,128,1024]{2,1,0:T(8,128)(2,1)}, u32[]{:S(2)}, u32[]{:S(2)}) collective-permute-start(bf16[3,128,1024]{2,1,0:T(8,128)(2,1)S(1)} %get-tuple-element.58), channel_id=1, source_target_pairs={{1,30},{3,0},{5,2},{7,4},{9,6},{11,8},{13,10},{15,12},{17,14},{19,... | collective-permute-start | bytes 2359304 | tf_op jit(solution)/shard_map/ppermute | solution.py:323
  75.7 7.1 %collective-permute-start.3 = (bf16[64,1024]{1,0:T(8,128)(2,1)S(1)}, bf16[64,1024]{1,0:T(8,128)(2,1)S(1)}, u32[]{:S(2)}, u32[]{:S(2)}) collective-permute-start(bf16[64,1024]{1,0:T(8,128)(2,1)S(1)} %get-tuple-element.67), channel_id=1, source_target_pairs={{0,2},{2,4},{4,6},{6,8},{8,10},{10,12},{12,14},{14,16},{16,18},{18... | collective-permute-start | bytes 393224 | tf_op jit(solution)/shard_map/ppermute | solution.py:323
  89.0 6.9 %collective-permute-start.7 = (bf16[64,1024]{1,0:T(8,128)(2,1)S(1)}, bf16[64,1024]{1,0:T(8,128)(2,1)S(1)}, u32[]{:S(2)}, u32[]{:S(2)}) collective-permute-start(bf16[64,1024]{1,0:T(8,128)(2,1)S(1)} %get-tuple-element.73), channel_id=1, source_target_pairs={{0,2},{2,4},{4,6},{6,8},{8,10},{10,12},{12,14},{14,16},{16,18},{18... | collective-permute-start | bytes 393224 | tf_op jit(solution)/shard_map/ppermute | solution.py:323
  95.9 9.2 %collective-permute-start.8 = (bf16[64,2048]{1,0:T(8,128)(2,1)S(1)}, bf16[64,2048]{1,0:T(8,128)(2,1)S(1)}, u32[]{:S(2)}, u32[]{:S(2)}) collective-permute-start(bf16[64,2048]{1,0:T(8,128)(2,1)S(1)} %multiply_convert_fusion.refs_1_), channel_id=1, source_target_pairs={{0,2},{1,3},{2,4},{3,5},{4,6},{5,7},{6,8},{7,9},{8,10},{9,11},{10,... | collective-permute-start | bytes 786440 | tf_op jit(solution)/shard_map/ppermute | solution.py:323
  100.3 12.9 %collective-permute-start.9 = (bf16[64,2048]{1,0:T(8,128)(2,1)S(1)}, bf16[64,2048]{1,0:T(8,128)(2,1)S(1)}, u32[]{:S(2)}, u32[]{:S(2)}) collective-permute-start(bf16[64,2048]{1,0:T(8,128)(2,1)S(1)} %multiply_convert_fusion.refs_1_), channel_id=1, source_target_pairs={{0,30},{1,31},{2,0},{3,1},{4,2},{5,3},{6,4},{7,5},{8,6},{9,7},{10,... | collective-permute-start | bytes 786440 | tf_op jit(solution)/shard_map/ppermute | solution.py:323
  105.1 10.0 %collective-permute-start.10 = (bf16[64,2048]{1,0:T(8,128)(2,1)S(1)}, bf16[64,2048]{1,0:T(8,128)(2,1)S(1)}, u32[]{:S(2)}, u32[]{:S(2)}) collective-permute-start(bf16[64,2048]{1,0:T(8,128)(2,1)S(1)} %collective-permute-done.8.refs_0_), channel_id=1, source_target_pairs={{0,2},{1,3},{2,4},{3,5},{4,6},{5,7},{6,8},{7,9},{8,10},{9,11},{10,... | collective-permute-start | bytes 786440 | tf_op jit(solution)/shard_map/ppermute | solution.py:323
  108.8 8.7 %collective-permute-start.12 = (bf16[64,2048]{1,0:T(8,128)(2,1)S(1)}, bf16[64,2048]{1,0:T(8,128)(2,1)S(1)}, u32[]{:S(2)}, u32[]{:S(2)}) collective-permute-start(bf16[64,2048]{1,0:T(8,128)(2,1)S(1)} %multiply_convert_fusion.refs_1_), channel_id=1, source_target_pairs={{0,1},{1,0},{2,3},{3,2},{4,5},{5,4},{6,7},{7,6},{8,9},{9,8},{10,11... | collective-permute-start | bytes 786440 | tf_op jit(solution)/shard_map/ppermute | solution.py:323
  110.8 6.8 %collective-permute-start.11 = (bf16[64,2048]{1,0:T(8,128)(2,1)S(1)}, bf16[64,2048]{1,0:T(8,128)(2,1)S(1)}, u32[]{:S(2)}, u32[]{:S(2)}) collective-permute-start(bf16[64,2048]{1,0:T(8,128)(2,1)S(1)} %collective-permute-done.8.refs_0_), channel_id=1, source_target_pairs={{0,1},{1,0},{2,3},{3,2},{4,5},{5,4},{6,7},{7,6},{8,9},{9,8},{10,11... | collective-permute-start | bytes 786440 | tf_op jit(solution)/shard_map/ppermute | solution.py:323
  113.2 4.4 %collective-permute-start.13 = (bf16[64,2048]{1,0:T(8,128)(2,1)S(1)}, bf16[64,2048]{1,0:T(8,128)(2,1)S(1)}, u32[]{:S(2)}, u32[]{:S(2)}) collective-permute-start(bf16[64,2048]{1,0:T(8,128)(2,1)S(1)} %collective-permute-done.9.refs_2_), channel_id=1, source_target_pairs={{0,1},{1,0},{2,3},{3,2},{4,5},{5,4},{6,7},{7,6},{8,9},{9,8},{10,11... | collective-permute-start | bytes 786440 | tf_op jit(solution)/shard_map/ppermute | solution.py:323
  115.1 3.6 %collective-permute-start.14 = (bf16[64,2048]{1,0:T(8,128)(2,1)S(1)}, bf16[64,2048]{1,0:T(8,128)(2,1)S(1)}, u32[]{:S(2)}, u32[]{:S(2)}) collective-permute-start(bf16[64,2048]{1,0:T(8,128)(2,1)S(1)} %collective-permute-done.10.refs_3_), channel_id=1, source_target_pairs={{0,1},{1,0},{2,3},{3,2},{4,5},{5,4},{6,7},{7,6},{8,9},{9,8},{10,11... | collective-permute-start | bytes 786440 | tf_op jit(solution)/shard_map/ppermute | solution.py:323
Sparse Core Ops, SparseCore 0:
  38.8 63.5 all-gather.3

commit v6 on v5

--- a/solution.py
+++ b/solution.py
@@ -331,30 +331,32 @@
 
     tables = pl.pallas_call(
         layout_kernel,
-        out_shape=[shape((NB * BLK, HD), BF16)] * 2 + [shape((2 * ROWS, NB * BLK), BF16)],
+        out_shape=[pltpu.HBM((NB * BLK, HD), BF16)] * 2 + [pltpu.HBM((2 * ROWS, NB * BLK), BF16)],
         in_specs=[smem(), smem()],
         out_specs=[vmem()] * 3,
         compiler_params=params(16),
         name="layout",
     )(scal, grids)
-    to, frm = pl.pallas_call(
-        index_kernel,
-        out_shape=[shape((1, GPOOL), I32), shape((1, GROUPS * CAP), I32)],
-        in_specs=[smem(), vmem()],
-        out_specs=[vmem(), vmem()],
-        compiler_params=params(24),
-        name="index",
-    )(scal, positions.reshape(GROUPS, GPOOL))
-    gains, _ = lax.optimization_barrier((jnp.broadcast_to(gamma[None, :], (2 * CHIPS, HD)), halves))
+    gains, parts[-1][1] = lax.optimization_barrier((jnp.broadcast_to(gamma[None, :], (2 * CHIPS, HD)), parts[-1][1]))
     gains = lax.all_to_all(gains, MLP, split_axis=0, concat_axis=0, tiled=True)
     gains = lax.dynamic_slice_in_dim(gains, core * CHIPS, CHIPS, 0).reshape(1, HALF).astype(F32)
-    owns, tables, to, frm, gains = lax.optimization_barrier(([p[0] for p in parts], tables, to, frm, gains))
+    owns, tables, gains = lax.optimization_barrier(([p[0] for p in parts], tables, gains))
     pooled = []
     for chunk in range(CHUNKS):
         mid, edge = attend([owns[chunk]] + parts[chunk][1:], tables)
         edge = move(edge, RING)
         pooled.append((mid, edge))
-        tables, _ = lax.optimization_barrier((tables, edge))
+        if chunk == 0:
+            positions, _ = lax.optimization_barrier((positions, mid))
+            to, frm = pl.pallas_call(
+                index_kernel,
+                out_shape=[shape((1, GPOOL), I32), shape((1, GROUPS * CAP), I32)],
+                in_specs=[smem(), vmem()],
+                out_specs=[vmem(), vmem()],
+                compiler_params=params(24),
+                name="index",
+            )(scal, positions.reshape(GROUPS, GPOOL))
+            tables, to, frm, _ = lax.optimization_barrier((tables, to, frm, edge))
     rows = jnp.concatenate([mid + edge for mid, edge in pooled], axis=1)
     rows = (rows.astype(F32) * gains).astype(BF16)
     below = move(rows, UP)

time: 181 us -> 183 us (1.011)
  waiting for transfers between devices: 8.51 us -> 17.4 us
  starting transfers between devices: 52.7 us -> 47.3 us
    ppermute x15, starting transfers between devices: 44.2 us -> 38.3 us  [move(): return lax.ppermute(x, MLP, perm)]
    all_to_all x1, waiting for transfers between devices: 0.01 us -> 5.82 us  [body(): gains = lax.all_to_all(gains, MLP, split_axis=0, concat_axis=0, tiled=True)]
    ppermute x15, waiting for transfers between devices: 8.47 us -> 11.5 us  [move(): return lax.ppermute(x, MLP, perm)]
  transfers between devices with their start and end apart: 17 -> 17, of which waited for: 4 -> 6; matrix products, arithmetic and copies ran while one was open for 0% -> 0% of each run, Pallas kernels for 9% -> 9%
where the time goes in v6:
time: 183 us; the launch traced here: 182 us
  blocking collectives  72.7 us (40%)
  starting transfers between devices  47.3 us (26%)
  Pallas kernels  28.3 us (15%)
  waiting for transfers between devices  17.4 us (10%)
  between operations  13.7 us (7%)
  local copies, waits for them, and re-layouts  2.28 us (1%)
    ppermute x15, starting transfers between devices, move(): return lax.ppermute(x, MLP, perm)  38.3 us
    all_to_all x1, blocking collectives, body(): out = lax.all_to_all(out, 'zq', split_axis=0, concat_axis=0, tiled=True)  29.1 us
    all_gather x1, blocking collectives, body(): cols = lax.all_gather(w_merge, 'zq', axis=0)  26.6 us
    all_to_all x1, blocking collectives, body(): out = lax.all_to_all(out, 'grp', split_axis=0, concat_axis=0, tiled=True)  17 us
    pallas_call x2, Pallas kernels, attend(): pl.pallas_call(attend_kernel, grid=(HEADS // STEP,), out_shape=[jax.Shape...  12.3 us
    ppermute x15, waiting for transfers between devices, move(): return lax.ppermute(x, MLP, perm)  11.5 us
    all_to_all x1, starting transfers between devices, body(): gains = lax.all_to_all(gains, MLP, split_axis=0, concat_axis=0, tiled=True)  8.98 us
    all_to_all x1, waiting for transfers between devices, body(): gains = lax.all_to_all(gains, MLP, split_axis=0, concat_axis=0, tiled=True)  5.82 us
  transfers between devices with their start and end apart: 17, of which 6 were waited for; matrix products, arithmetic and copies ran while one was open for 0% of the time, Pallas kernels for 9%

profile of v6, /device:TPU:32, one launch (start us, length us, event | category | flops | bytes accessed | tf_op | source)
XLA Modules:
  0.0 181.9 jit_solution(13948064310216221935)
XLA Ops:
  7.4 4.6 %rope.1 = (bf16[3,128,1024]{2,1,0:T(8,128)(2,1)S(1)}, bf16[3,128,1024]{2,1,0:T(8,128)(2,1)S(1)}, bf16[3,128,1024]{2,1,0:T(8,128)(2,1)S(1)}, bf16[3,128,1024]{2,1,0:T(8,128)(2,1)S(1)}) custom-call(s32[4]{0:T(128)S(1)} %pad_add_fusion.scal_ref, s32[16,2]{1,0:T(8,128)S(1)} %copy.12.grid_ref, bf16[128,4096]{1,0:T(8,128)(2,1)} %q_ref.1, bf16[128,4096]{1,0:T(8,128)(2,1)} %k_ref.1, ...), custom_call_target="tpu_custom_call" | custom-call | flops 6899999744 | bytes 21000000 | tf_op jit(solution)/shard_map/rope/pallas_call | solution.py:130
  12.9 26.6 %all-gather = bf16[1024,128]{1,0:T(8,128)(2,1)} all-gather(bf16[256,128]{1,0:T(8,128)(2,1)S(1)} %copy-done.1), channel_id=2, replica_groups=mesh['grp'=16,'zq'=4,'zr'=4,'core'=2] {'zq'}, dimensions={0}, use_global_device_ids=true | all-gather | bytes 327680 | tf_op jit(solution)/shard_map/all_gather | solution.py:327
  41.5 2.4 %collective-permute-start.1 = (bf16[3,128,1024]{2,1,0:T(8,128)(2,1)}, bf16[3,128,1024]{2,1,0:T(8,128)(2,1)}, u32[]{:S(2)}, u32[]{:S(2)}) collective-permute-start(bf16[3,128,1024]{2,1,0:T(8,128)(2,1)} %copy-done), channel_id=1, source_target_pairs={{0,1},{1,0},{2,3},{3,2},{4,5},{5,4},{6,7},{7,6},{8,9},{9,8},{10,11... | collective-permute-start | bytes 2359304 | tf_op jit(solution)/shard_map/ppermute | solution.py:323
  43.9 3.0 %collective-permute-start.2 = (bf16[3,128,1024]{2,1,0:T(8,128)(2,1)S(1)}, bf16[3,128,1024]{2,1,0:T(8,128)(2,1)}, u32[]{:S(2)}, u32[]{:S(2)}) collective-permute-start(bf16[3,128,1024]{2,1,0:T(8,128)(2,1)S(1)} %get-tuple-element.62.a_ref), channel_id=1, source_target_pairs={{0,30},{2,0},{4,2},{6,4},{8,6},{10,8},{12,10},{14,12},{16,14},{18,... | collective-permute-start | bytes 2359304 | tf_op jit(solution)/shard_map/ppermute | solution.py:323
  46.9 2.2 %collective-permute-start.3 = (bf16[3,128,1024]{2,1,0:T(8,128)(2,1)}, bf16[3,128,1024]{2,1,0:T(8,128)(2,1)}, u32[]{:S(2)}, u32[]{:S(2)}) collective-permute-start(bf16[3,128,1024]{2,1,0:T(8,128)(2,1)} %copy-done), channel_id=1, source_target_pairs={{1,30},{3,0},{5,2},{7,4},{9,6},{11,8},{13,10},{15,12},{17,14},{19,... | collective-permute-start | bytes 2359304 | tf_op jit(solution)/shard_map/ppermute | solution.py:323
  49.8 9.0 %all-to-all-start = ((bf16[32,1,128]{2,1,0:T(2,128)(2,1)}), bf16[32,1,128]{2,1,0:T(2,128)(2,1)S(1)}, u32[]{:S(2)}, u32[]{:S(2)}) async-start(bf16[32,1,128]{2,1,0:T(2,128)(2,1)} %copy.14), calls=%async_computation | async-start | bytes 32768 | tf_op jit(solution)/shard_map/all_to_all | solution.py:341
  58.8 3.1 %collective-permute-start.6 = (bf16[3,128,1024]{2,1,0:T(8,128)(2,1)S(1)}, bf16[3,128,1024]{2,1,0:T(8,128)(2,1)}, u32[]{:S(2)}, u32[]{:S(2)}) collective-permute-start(bf16[3,128,1024]{2,1,0:T(8,128)(2,1)S(1)} %get-tuple-element.57), channel_id=1, source_target_pairs={{1,30},{3,0},{5,2},{7,4},{9,6},{11,8},{13,10},{15,12},{17,14},{19,... | collective-permute-start | bytes 2359304 | tf_op jit(solution)/shard_map/ppermute | solution.py:323
  61.9 2.5 %collective-permute-start.5 = (bf16[3,128,1024]{2,1,0:T(8,128)(2,1)S(1)}, bf16[3,128,1024]{2,1,0:T(8,128)(2,1)}, u32[]{:S(2)}, u32[]{:S(2)}) collective-permute-start(bf16[3,128,1024]{2,1,0:T(8,128)(2,1)S(1)} %get-tuple-element.71.a_ref), channel_id=1, source_target_pairs={{0,30},{2,0},{4,2},{6,4},{8,6},{10,8},{12,10},{14,12},{16,14},{18,... | collective-permute-start | bytes 2359304 | tf_op jit(solution)/shard_map/ppermute | solution.py:323
  66.2 5.8 %all-to-all-done = bf16[32,1,128]{2,1,0:T(2,128)(2,1)S(1)} async-done(((bf16[32,1,128]{2,1,0:T(2,128)(2,1)}), bf16[32,1,128]{2,1,0:T(2,128)(2,1)S(1)}, u32[]{:S(2)}, u32[]{:S(2)}) %all-to-all-start) | async-done | bytes 8224 | tf_op jit(solution)/shard_map/all_to_all | solution.py:341
  72.1 6.2 %attend.2 = (bf16[64,1024]{1,0:T(8,128)(2,1)S(1)}, bf16[64,1024]{1,0:T(8,128)(2,1)S(1)}) custom-call(bf16[3,128,1024]{2,1,0:T(8,128)(2,1)S(1)} %get-tuple-element.62.a_ref, bf16[3,128,1024]{2,1,0:T(8,128)(2,1)} %collective-permute-done.1.b_ref, bf16[3,128,1024]{2,1,0:T(8,128)(2,1)} %collective-permute-done.2.c_ref, ...), custom_call_target="tpu_custom_call" | custom-call | flops 6899999744 | bytes 21000000 | tf_op jit(solution)/shard_map/attend/pallas_call | solution.py:219
  78.3 2.4 %collective-permute-start.4 = (bf16[64,1024]{1,0:T(8,128)(2,1)S(1)}, bf16[64,1024]{1,0:T(8,128)(2,1)S(1)}, u32[]{:S(2)}, u32[]{:S(2)}) collective-permute-start(bf16[64,1024]{1,0:T(8,128)(2,1)S(1)} %get-tuple-element.68), channel_id=1, source_target_pairs={{0,2},{2,4},{4,6},{6,8},{8,10},{10,12},{12,14},{14,16},{16,18},{18... | collective-permute-start | bytes 393224 | tf_op jit(solution)/shard_map/ppermute | solution.py:323
  80.7 2.2 %index.1 = (s32[1,1024]{1,0:T(1,128)S(1)}, s32[1,2048]{1,0:T(1,128)S(1)}) custom-call(s32[4]{0:T(128)S(1)} %pad_add_fusion.scal_ref, s32[16,1024]{1,0:T(8,128)S(1)} %reshape.25.pos_ref), custom_call_target="tpu_custom_call" | custom-call | tf_op jit(solution)/shard_map/index/pallas_call | solution.py:351
  82.9 2.3 %collective-permute-done.4 = bf16[64,1024]{1,0:T(8,128)(2,1)S(1)} collective-permute-done((bf16[64,1024]{1,0:T(8,128)(2,1)S(1)}, bf16[64,1024]{1,0:T(8,128)(2,1)S(1)}, u32[]{:S(2)}, u32[]{:S(2)}) %collective-permute-start.4) | collective-permute-done | bytes 131104 | tf_op jit(solution)/shard_map/ppermute | solution.py:323
  85.2 6.1 %attend.3 = (bf16[64,1024]{1,0:T(8,128)(2,1)S(1)}, bf16[64,1024]{1,0:T(8,128)(2,1)S(1)}) custom-call(bf16[3,128,1024]{2,1,0:T(8,128)(2,1)S(1)} %get-tuple-element.71.a_ref, bf16[3,128,1024]{2,1,0:T(8,128)(2,1)S(1)} %collective-permute-done.b_ref, bf16[3,128,1024]{2,1,0:T(8,128)(2,1)} %collective-permute-done.5.c_ref, ...), custom_call_target="tpu_custom_call" | custom-call | flops 6899999744 | bytes 21000000 | tf_op jit(solution)/shard_map/attend/pallas_call | solution.py:219
  91.3 3.0 %collective-permute-start.7 = (bf16[64,1024]{1,0:T(8,128)(2,1)S(1)}, bf16[64,1024]{1,0:T(8,128)(2,1)S(1)}, u32[]{:S(2)}, u32[]{:S(2)}) collective-permute-start(bf16[64,1024]{1,0:T(8,128)(2,1)S(1)} %get-tuple-element.77), channel_id=1, source_target_pairs={{0,2},{2,4},{4,6},{6,8},{8,10},{10,12},{12,14},{14,16},{16,18},{18... | collective-permute-start | bytes 393224 | tf_op jit(solution)/shard_map/ppermute | solution.py:323
  94.4 3.8 %collective-permute-done.7 = bf16[64,1024]{1,0:T(8,128)(2,1)S(1)} collective-permute-done((bf16[64,1024]{1,0:T(8,128)(2,1)S(1)}, bf16[64,1024]{1,0:T(8,128)(2,1)S(1)}, u32[]{:S(2)}, u32[]{:S(2)}) %collective-permute-start.7) | collective-permute-done | bytes 131104 | tf_op jit(solution)/shard_map/ppermute | solution.py:323
  98.3 3.0 %collective-permute-start.8 = (bf16[64,2048]{1,0:T(8,128)(2,1)S(1)}, bf16[64,2048]{1,0:T(8,128)(2,1)S(1)}, u32[]{:S(2)}, u32[]{:S(2)}) collective-permute-start(bf16[64,2048]{1,0:T(8,128)(2,1)S(1)} %multiply_convert_fusion.refs_1_), channel_id=1, source_target_pairs={{0,2},{1,3},{2,4},{3,5},{4,6},{5,7},{6,8},{7,9},{8,10},{9,11},{10,... | collective-permute-start | bytes 786440 | tf_op jit(solution)/shard_map/ppermute | solution.py:323
  101.3 3.4 %collective-permute-start.9 = (bf16[64,2048]{1,0:T(8,128)(2,1)S(1)}, bf16[64,2048]{1,0:T(8,128)(2,1)S(1)}, u32[]{:S(2)}, u32[]{:S(2)}) collective-permute-start(bf16[64,2048]{1,0:T(8,128)(2,1)S(1)} %multiply_convert_fusion.refs_1_), channel_id=1, source_target_pairs={{0,30},{1,31},{2,0},{3,1},{4,2},{5,3},{6,4},{7,5},{8,6},{9,7},{10,... | collective-permute-start | bytes 786440 | tf_op jit(solution)/shard_map/ppermute | solution.py:323
  104.6 3.2 %collective-permute-done.8.refs_0_ = bf16[64,2048]{1,0:T(8,128)(2,1)S(1)} collective-permute-done((bf16[64,2048]{1,0:T(8,128)(2,1)S(1)}, bf16[64,2048]{1,0:T(8,128)(2,1)S(1)}, u32[]{:S(2)}, u32[]{:S(2)}) %collective-permute-start.8) | collective-permute-done | bytes 262176 | tf_op jit(solution)/shard_map/ppermute | solution.py:323
  107.8 3.3 %collective-permute-start.10 = (bf16[64,2048]{1,0:T(8,128)(2,1)S(1)}, bf16[64,2048]{1,0:T(8,128)(2,1)S(1)}, u32[]{:S(2)}, u32[]{:S(2)}) collective-permute-start(bf16[64,2048]{1,0:T(8,128)(2,1)S(1)} %collective-permute-done.8.refs_0_), channel_id=1, source_target_pairs={{0,2},{1,3},{2,4},{3,5},{4,6},{5,7},{6,8},{7,9},{8,10},{9,11},{10,... | collective-permute-start | bytes 786440 | tf_op jit(solution)/shard_map/ppermute | solution.py:323
  113.1 2.4 %collective-permute-start.11 = (bf16[64,2048]{1,0:T(8,128)(2,1)S(1)}, bf16[64,2048]{1,0:T(8,128)(2,1)S(1)}, u32[]{:S(2)}, u32[]{:S(2)}) collective-permute-start(bf16[64,2048]{1,0:T(8,128)(2,1)S(1)} %collective-permute-done.8.refs_0_), channel_id=1, source_target_pairs={{0,1},{1,0},{2,3},{3,2},{4,5},{5,4},{6,7},{7,6},{8,9},{9,8},{10,11... | collective-permute-start | bytes 786440 | tf_op jit(solution)/shard_map/ppermute | solution.py:323
  121.6 3.6 %project.1 = bf16[4,256,128]{2,1,0:T(8,128)(2,1)S(1)} custom-call(s32[4]{0:T(128)S(1)} %pad_add_fusion.scal_ref, bf16[64,2048]{1,0:T(8,128)(2,1)S(1)} %collective-permute-done.8.refs_0_, bf16[64,2048]{1,0:T(8,128)(2,1)S(1)} %multiply_convert_fusion.refs_1_, bf16[64,2048]{1,0:T(8,128)(2,1)S(1)} %collective-permute-done.9.refs_2_, ...), custom_call_target="tpu_custom_call" | custom-call | flops 4600000000 | bytes 14000000 | tf_op jit(solution)/shard_map/project/pallas_call | solution.py:249
  125.2 29.1 %all_to_all.25.got_ref = bf16[4,256,128]{2,1,0:T(8,128)(2,1)S(1)} all-to-all(bf16[4,256,128]{2,1,0:T(8,128)(2,1)S(1)} %project.1), channel_id=1, replica_groups=mesh['grp'=16,'zq'=4,'zr'=4,'core'=2] {'zq'}, dimensions={0} | all-to-all | bytes 524288 | tf_op jit(solution)/shard_map/all_to_all | solution.py:369
  156.1 17.0 %all_to_all.26 = bf16[16,128,128]{2,1,0:T(8,128)(2,1)S(1)} all-to-all(bf16[16,128,128]{2,1,0:T(8,128)(2,1)S(1)} %bitcast.12), channel_id=1, replica_groups=mesh['grp'=16,'zq'=4,'zr'=4,'core'=2] {'grp'}, dimensions={0} | all-to-all | bytes 1048576 | tf_op jit(solution)/shard_map/all_to_all | solution.py:380
  (39 shorter events, 18.1 us)
Async XLA Ops:
  6.5 113.6 %all-gather.4.cloned.1.call-start = ((), (), s32[]{:S(2)}) async-start(), calls=%async_computation.3 | async-start | bytes 4456448 | tf_op jit(solution)/shard_map/all_gather | solution.py:329
  7.4 5.5 %copy-start.1 = (bf16[256,128]{1,0:T(8,128)(2,1)S(1)}, bf16[256,128]{1,0:T(8,128)(2,1)}, u32[]{:S(2)}) copy-start(bf16[256,128]{1,0:T(8,128)(2,1)} %param.11) | copy-start | bytes 196612
  7.4 41.8 %copy-start.3 = (bf16[128]{0:T(256)(128)(2,1)S(1)}, bf16[128]{0:T(256)(128)(2,1)}, u32[]{:S(2)}) copy-start(bf16[128]{0:T(256)(128)(2,1)} %param.10) | copy-start | bytes 772
  12.0 0.9 copy-start
  39.5 9.6 %collective-permute-start = (bf16[3,128,1024]{2,1,0:T(8,128)(2,1)S(1)}, bf16[3,128,1024]{2,1,0:T(8,128)(2,1)S(1)}, u32[]{:S(2)}, u32[]{:S(2)}) collective-permute-start(bf16[3,128,1024]{2,1,0:T(8,128)(2,1)S(1)} %get-tuple-element.57), channel_id=1, source_target_pairs={{0,1},{1,0},{2,3},{3,2},{4,5},{5,4},{6,7},{7,6},{8,9},{9,8},{10,11... | collective-permute-start | bytes 2359304 | tf_op jit(solution)/shard_map/ppermute | solution.py:323
  41.5 30.6 %collective-permute-start.1 = (bf16[3,128,1024]{2,1,0:T(8,128)(2,1)}, bf16[3,128,1024]{2,1,0:T(8,128)(2,1)}, u32[]{:S(2)}, u32[]{:S(2)}) collective-permute-start(bf16[3,128,1024]{2,1,0:T(8,128)(2,1)} %copy-done), channel_id=1, source_target_pairs={{0,1},{1,0},{2,3},{3,2},{4,5},{5,4},{6,7},{7,6},{8,9},{9,8},{10,11... | collective-permute-start | bytes 2359304 | tf_op jit(solution)/shard_map/ppermute | solution.py:323
  43.9 28.2 %collective-permute-start.2 = (bf16[3,128,1024]{2,1,0:T(8,128)(2,1)S(1)}, bf16[3,128,1024]{2,1,0:T(8,128)(2,1)}, u32[]{:S(2)}, u32[]{:S(2)}) collective-permute-start(bf16[3,128,1024]{2,1,0:T(8,128)(2,1)S(1)} %get-tuple-element.62.a_ref), channel_id=1, source_target_pairs={{0,30},{2,0},{4,2},{6,4},{8,6},{10,8},{12,10},{14,12},{16,14},{18,... | collective-permute-start | bytes 2359304 | tf_op jit(solution)/shard_map/ppermute | solution.py:323
  46.9 25.2 %collective-permute-start.3 = (bf16[3,128,1024]{2,1,0:T(8,128)(2,1)}, bf16[3,128,1024]{2,1,0:T(8,128)(2,1)}, u32[]{:S(2)}, u32[]{:S(2)}) collective-permute-start(bf16[3,128,1024]{2,1,0:T(8,128)(2,1)} %copy-done), channel_id=1, source_target_pairs={{1,30},{3,0},{5,2},{7,4},{9,6},{11,8},{13,10},{15,12},{17,14},{19,... | collective-permute-start | bytes 2359304 | tf_op jit(solution)/shard_map/ppermute | solution.py:323
  49.8 22.3 %all-to-all-start = ((bf16[32,1,128]{2,1,0:T(2,128)(2,1)}), bf16[32,1,128]{2,1,0:T(2,128)(2,1)S(1)}, u32[]{:S(2)}, u32[]{:S(2)}) async-start(bf16[32,1,128]{2,1,0:T(2,128)(2,1)} %copy.14), calls=%async_computation | async-start | bytes 32768 | tf_op jit(solution)/shard_map/all_to_all | solution.py:341
  58.8 26.4 %collective-permute-start.6 = (bf16[3,128,1024]{2,1,0:T(8,128)(2,1)S(1)}, bf16[3,128,1024]{2,1,0:T(8,128)(2,1)}, u32[]{:S(2)}, u32[]{:S(2)}) collective-permute-start(bf16[3,128,1024]{2,1,0:T(8,128)(2,1)S(1)} %get-tuple-element.57), channel_id=1, source_target_pairs={{1,30},{3,0},{5,2},{7,4},{9,6},{11,8},{13,10},{15,12},{17,14},{19,... | collective-permute-start | bytes 2359304 | tf_op jit(solution)/shard_map/ppermute | solution.py:323
  61.9 23.3 %collective-permute-start.5 = (bf16[3,128,1024]{2,1,0:T(8,128)(2,1)S(1)}, bf16[3,128,1024]{2,1,0:T(8,128)(2,1)}, u32[]{:S(2)}, u32[]{:S(2)}) collective-permute-start(bf16[3,128,1024]{2,1,0:T(8,128)(2,1)S(1)} %get-tuple-element.71.a_ref), channel_id=1, source_target_pairs={{0,30},{2,0},{4,2},{6,4},{8,6},{10,8},{12,10},{14,12},{16,14},{18,... | collective-permute-start | bytes 2359304 | tf_op jit(solution)/shard_map/ppermute | solution.py:323
  72.1 8.6 %copy-start.2 = (s32[16384]{0:T(1024)S(1)}, s32[16384]{0:T(1024)}, u32[]{:S(2)}) copy-start(s32[16384]{0:T(1024)} %param.13) | copy-start | bytes 196612
  78.3 6.9 %collective-permute-start.4 = (bf16[64,1024]{1,0:T(8,128)(2,1)S(1)}, bf16[64,1024]{1,0:T(8,128)(2,1)S(1)}, u32[]{:S(2)}, u32[]{:S(2)}) collective-permute-start(bf16[64,1024]{1,0:T(8,128)(2,1)S(1)} %get-tuple-element.68), channel_id=1, source_target_pairs={{0,2},{2,4},{4,6},{6,8},{8,10},{10,12},{12,14},{14,16},{16,18},{18... | collective-permute-start | bytes 393224 | tf_op jit(solution)/shard_map/ppermute | solution.py:323
  91.3 6.9 %collective-permute-start.7 = (bf16[64,1024]{1,0:T(8,128)(2,1)S(1)}, bf16[64,1024]{1,0:T(8,128)(2,1)S(1)}, u32[]{:S(2)}, u32[]{:S(2)}) collective-permute-start(bf16[64,1024]{1,0:T(8,128)(2,1)S(1)} %get-tuple-element.77), channel_id=1, source_target_pairs={{0,2},{2,4},{4,6},{6,8},{8,10},{10,12},{12,14},{14,16},{16,18},{18... | collective-permute-start | bytes 393224 | tf_op jit(solution)/shard_map/ppermute | solution.py:323
  98.3 9.5 %collective-permute-start.8 = (bf16[64,2048]{1,0:T(8,128)(2,1)S(1)}, bf16[64,2048]{1,0:T(8,128)(2,1)S(1)}, u32[]{:S(2)}, u32[]{:S(2)}) collective-permute-start(bf16[64,2048]{1,0:T(8,128)(2,1)S(1)} %multiply_convert_fusion.refs_1_), channel_id=1, source_target_pairs={{0,2},{1,3},{2,4},{3,5},{4,6},{5,7},{6,8},{7,9},{8,10},{9,11},{10,... | collective-permute-start | bytes 786440 | tf_op jit(solution)/shard_map/ppermute | solution.py:323
  101.3 14.2 %collective-permute-start.9 = (bf16[64,2048]{1,0:T(8,128)(2,1)S(1)}, bf16[64,2048]{1,0:T(8,128)(2,1)S(1)}, u32[]{:S(2)}, u32[]{:S(2)}) collective-permute-start(bf16[64,2048]{1,0:T(8,128)(2,1)S(1)} %multiply_convert_fusion.refs_1_), channel_id=1, source_target_pairs={{0,30},{1,31},{2,0},{3,1},{4,2},{5,3},{6,4},{7,5},{8,6},{9,7},{10,... | collective-permute-start | bytes 786440 | tf_op jit(solution)/shard_map/ppermute | solution.py:323
  107.8 10.4 %collective-permute-start.10 = (bf16[64,2048]{1,0:T(8,128)(2,1)S(1)}, bf16[64,2048]{1,0:T(8,128)(2,1)S(1)}, u32[]{:S(2)}, u32[]{:S(2)}) collective-permute-start(bf16[64,2048]{1,0:T(8,128)(2,1)S(1)} %collective-permute-done.8.refs_0_), channel_id=1, source_target_pairs={{0,2},{1,3},{2,4},{3,5},{4,6},{5,7},{6,8},{7,9},{8,10},{9,11},{10,... | collective-permute-start | bytes 786440 | tf_op jit(solution)/shard_map/ppermute | solution.py:323
  111.1 9.0 %collective-permute-start.12 = (bf16[64,2048]{1,0:T(8,128)(2,1)S(1)}, bf16[64,2048]{1,0:T(8,128)(2,1)S(1)}, u32[]{:S(2)}, u32[]{:S(2)}) collective-permute-start(bf16[64,2048]{1,0:T(8,128)(2,1)S(1)} %multiply_convert_fusion.refs_1_), channel_id=1, source_target_pairs={{0,1},{1,0},{2,3},{3,2},{4,5},{5,4},{6,7},{7,6},{8,9},{9,8},{10,11... | collective-permute-start | bytes 786440 | tf_op jit(solution)/shard_map/ppermute | solution.py:323
  113.1 7.1 %collective-permute-start.11 = (bf16[64,2048]{1,0:T(8,128)(2,1)S(1)}, bf16[64,2048]{1,0:T(8,128)(2,1)S(1)}, u32[]{:S(2)}, u32[]{:S(2)}) collective-permute-start(bf16[64,2048]{1,0:T(8,128)(2,1)S(1)} %collective-permute-done.8.refs_0_), channel_id=1, source_target_pairs={{0,1},{1,0},{2,3},{3,2},{4,5},{5,4},{6,7},{7,6},{8,9},{9,8},{10,11... | collective-permute-start | bytes 786440 | tf_op jit(solution)/shard_map/ppermute | solution.py:323
  115.5 4.7 %collective-permute-start.13 = (bf16[64,2048]{1,0:T(8,128)(2,1)S(1)}, bf16[64,2048]{1,0:T(8,128)(2,1)S(1)}, u32[]{:S(2)}, u32[]{:S(2)}) collective-permute-start(bf16[64,2048]{1,0:T(8,128)(2,1)S(1)} %collective-permute-done.9.refs_2_), channel_id=1, source_target_pairs={{0,1},{1,0},{2,3},{3,2},{4,5},{5,4},{6,7},{7,6},{8,9},{9,8},{10,11... | collective-permute-start | bytes 786440 | tf_op jit(solution)/shard_map/ppermute | solution.py:323
  118.2 3.4 %collective-permute-start.14 = (bf16[64,2048]{1,0:T(8,128)(2,1)S(1)}, bf16[64,2048]{1,0:T(8,128)(2,1)S(1)}, u32[]{:S(2)}, u32[]{:S(2)}) collective-permute-start(bf16[64,2048]{1,0:T(8,128)(2,1)S(1)} %collective-permute-done.10.refs_3_), channel_id=1, source_target_pairs={{0,1},{1,0},{2,3},{3,2},{4,5},{5,4},{6,7},{7,6},{8,9},{9,8},{10,11... | collective-permute-start | bytes 786440 | tf_op jit(solution)/shard_map/ppermute | solution.py:323
Sparse Core Ops, SparseCore 0:
  39.7 63.6 all-gather.3

commit v7 on v6

--- a/solution.py
+++ b/solution.py
@@ -62,17 +62,17 @@
 def images_of(tok, grid_ref):
     image = jnp.where(tok < 0, -1, 0)
     first = jnp.zeros_like(tok)
-    width = jnp.full_like(tok, grid_ref[0, 1])
-    end = jnp.full_like(tok, grid_ref[0, 0] * grid_ref[0, 1])
+    width = jnp.full_like(tok, grid_ref[1, 0])
+    end = jnp.full_like(tok, grid_ref[0, 0] * grid_ref[1, 0])
     upto = jnp.int32(0)
     for n in range(IMGS):
-        upto = upto + grid_ref[n, 0] * grid_ref[n, 1]
+        upto = upto + grid_ref[0, n] * grid_ref[1, n]
         past = tok >= upto
         image = jnp.where(past, n + 1, image)
         first = jnp.where(past, upto, first)
         if n + 1 < IMGS:
-            width = jnp.where(past, grid_ref[n + 1, 1], width)
-            end = jnp.where(past, upto + grid_ref[n + 1, 0] * grid_ref[n + 1, 1], end)
+            width = jnp.where(past, grid_ref[1, n + 1], width)
+            end = jnp.where(past, upto + grid_ref[0, n + 1] * grid_ref[1, n + 1], end)
         else:
             width = jnp.where(past, 2, width)
     return image, first, width, end
@@ -129,7 +129,7 @@
 
     outs = pl.pallas_call(
         rope_kernel,
-        out_shape=[jax.ShapeDtypeStruct((3, BLK, WIDE), BF16)] * (2 * CHUNKS),
+        out_shape=[pltpu.HBM((3, BLK, WIDE), BF16)] * (2 * CHUNKS),
         grid_spec=pltpu.PrefetchScalarGridSpec(
             num_scalar_prefetch=1,
             grid=(2 * CHUNKS,),
@@ -173,7 +173,7 @@
     pool_ref[...] = jnp.where((target == mine) & (target >= 0), 1.0, 0.0).astype(BF16)
 
 
-def attend_kernel(a_ref, b_ref, c_ref, d_ref, qhot_ref, khot_ref, pool_ref, mid_ref, edge_ref):
+def attend_kernel(a_ref, c_ref, d_ref, b_ref, qhot_ref, khot_ref, pool_ref, mid_ref, edge_ref):
     refs = (a_ref, b_ref, c_ref, d_ref)
     pairs = NB // 2
     ones = jnp.ones((16, NB * BLK), BF16)
@@ -214,7 +214,7 @@
 
 def attend(parts, tables):
     part = pl.BlockSpec((3, BLK, STEP * HD), lambda h: (0, 0, h))
-    tables = [pltpu.with_memory_space_constraint(t, pltpu.HBM) for t in tables]
+    own, tables = ([pltpu.with_memory_space_constraint(t, pltpu.HBM) for t in x] for x in (parts[:1], tables))
     whole = [pl.BlockSpec(t.shape, lambda h: (0, 0)) for t in tables]
     return pl.pallas_call(
         attend_kernel,
@@ -225,7 +225,7 @@
         compiler_params=params(32),
         cost_estimate=cost(6),
         name="attend",
-    )(*parts, *tables)
+    )(*own, *parts[1:], *tables)
 
 
 def project_kernel(scal_ref, *refs):
@@ -322,12 +322,17 @@
     def move(x, perm):
         return lax.ppermute(x, MLP, perm)
 
+    grids = grids.T
     halves = rope(scal, grids, queries, keys, values)
     w_merge, halves = lax.optimization_barrier((w_merge, halves))
     cols = lax.all_gather(w_merge, "zq", axis=0)
     halves, cols = lax.optimization_barrier((halves, cols))
     cols = lax.all_gather(cols, "grp", axis=0)
-    parts = [[own, move(oth, PART), move(own, SAME), move(oth, OPP)] for own, oth in halves]
+    parts = []
+    for own, oth in halves:
+        up = move(own, SAME)
+        across = move(oth, OPP)
+        parts.append([own, up, across, move(oth, PART)])
 
     tables = pl.pallas_call(
         layout_kernel,
@@ -337,14 +342,13 @@
         compiler_params=params(16),
         name="layout",
     )(scal, grids)
-    gains, parts[-1][1] = lax.optimization_barrier((jnp.broadcast_to(gamma[None, :], (2 * CHIPS, HD)), parts[-1][1]))
+    gains, _ = lax.optimization_barrier((jnp.broadcast_to(gamma[None, :], (2 * CHIPS, HD)), halves))
     gains = lax.all_to_all(gains, MLP, split_axis=0, concat_axis=0, tiled=True)
     gains = lax.dynamic_slice_in_dim(gains, core * CHIPS, CHIPS, 0).reshape(1, HALF).astype(F32)
-    owns, tables, gains = lax.optimization_barrier(([p[0] for p in parts], tables, gains))
+    owns, tables = lax.optimization_barrier(([p[0] for p in parts], tables))
     pooled = []
     for chunk in range(CHUNKS):
         mid, edge = attend([owns[chunk]] + parts[chunk][1:], tables)
-        edge = move(edge, RING)
         pooled.append((mid, edge))
         if chunk == 0:
             positions, _ = lax.optimization_barrier((positions, mid))
@@ -356,8 +360,9 @@
                 compiler_params=params(24),
                 name="index",
             )(scal, positions.reshape(GROUPS, GPOOL))
-            tables, to, frm, _ = lax.optimization_barrier((tables, to, frm, edge))
-    rows = jnp.concatenate([mid + edge for mid, edge in pooled], axis=1)
+            tables, to, frm, gains = lax.optimization_barrier((tables, to, frm, gains))
+    mid, edge = (jnp.concatenate(half, axis=1) for half in zip(*pooled))
+    rows = mid + move(edge, RING)
     rows = (rows.astype(F32) * gains).astype(BF16)
     below = move(rows, UP)
     above = move(rows, DOWN)

time: 183 us -> 181 us (0.989)
  the two profiles are of different devices: /device:TPU:32 before, /device:TPU:1 now
where the time goes in v7:
time: 181 us; the launch traced here: 178 us
  blocking collectives  68.4 us (38%)
  starting transfers between devices  53.5 us (30%)
  Pallas kernels  29.6 us (16%)
  between operations  13.7 us (8%)
  waiting for transfers between devices  10.4 us (6%)
    ppermute x14, starting transfers between devices, move(): return lax.ppermute(x, MLP, perm)  46 us
    all_to_all x1, blocking collectives, body(): out = lax.all_to_all(out, 'zq', split_axis=0, concat_axis=0, tiled=True)  26.8 us
    all_gather x1, blocking collectives, body(): cols = lax.all_gather(w_merge, 'zq', axis=0)  25.6 us
    all_to_all x1, blocking collectives, body(): out = lax.all_to_all(out, 'grp', split_axis=0, concat_axis=0, tiled=True)  16 us
    pallas_call x2, Pallas kernels, attend(): pl.pallas_call(attend_kernel, grid=(HEADS // STEP,), out_shape=[jax.Shape...  12.1 us
    ppermute x14, waiting for transfers between devices, move(): return lax.ppermute(x, MLP, perm)  10.3 us
    all_to_all x1, starting transfers between devices, body(): gains = lax.all_to_all(gains, MLP, split_axis=0, concat_axis=0, tiled=True)  7.47 us
    pallas_call x1, Pallas kernels, rope(): pl.pallas_call(rope_kernel, out_shape=[pltpu.HBM((3, BLK, WIDE), BF16)] *...  6.24 us
  transfers between devices with their start and end apart: 16, of which 4 were waited for; matrix products, arithmetic and copies ran while one was open for 1% of the time, Pallas kernels for 9%

profile of v7, /device:TPU:1, one launch (start us, length us, event | category | flops | bytes accessed | tf_op | source)
XLA Modules:
  0.0 177.7 jit_solution(13031569877288173829)
XLA Ops:
  7.3 6.2 %rope.1 = (bf16[3,128,1024]{2,1,0:T(8,128)(2,1)}, bf16[3,128,1024]{2,1,0:T(8,128)(2,1)}, bf16[3,128,1024]{2,1,0:T(8,128)(2,1)}, bf16[3,128,1024]{2,1,0:T(8,128)(2,1)}) custom-call(s32[4]{0:T(128)S(1)} %pad_add_fusion.scal_ref, s32[2,16]{1,0:T(2,128)S(1)} %bitcast.15, bf16[128,4096]{1,0:T(8,128)(2,1)} %q_ref.1, bf16[128,4096]{1,0:T(8,128)(2,1)} %k_ref.1, ...), custom_call_target="tpu_custom_call" | custom-call | flops 6899999744 | bytes 21000000 | tf_op jit(solution)/shard_map/rope/pallas_call | solution.py:130
  13.5 25.6 %all-gather = bf16[1024,128]{1,0:T(8,128)(2,1)} all-gather(bf16[256,128]{1,0:T(8,128)(2,1)S(1)} %copy-done.2), channel_id=2, replica_groups=mesh['grp'=16,'zq'=4,'zr'=4,'core'=2] {'zq'}, dimensions={0}, use_global_device_ids=true | all-gather | bytes 327680 | tf_op jit(solution)/shard_map/all_gather | solution.py:328
  39.1 2.8 %collective-permute-start = (bf16[3,128,1024]{2,1,0:T(8,128)(2,1)}, bf16[3,128,1024]{2,1,0:T(8,128)(2,1)S(1)}, u32[]{:S(2)}, u32[]{:S(2)}) collective-permute-start(bf16[3,128,1024]{2,1,0:T(8,128)(2,1)} %get-tuple-element.59.a_ref), channel_id=1, source_target_pairs={{0,30},{2,0},{4,2},{6,4},{8,6},{10,8},{12,10},{14,12},{16,14},{18,... | collective-permute-start | bytes 2359304 | tf_op jit(solution)/shard_map/ppermute | solution.py:323
  42.0 6.4 %collective-permute-start.1 = (bf16[3,128,1024]{2,1,0:T(8,128)(2,1)}, bf16[3,128,1024]{2,1,0:T(8,128)(2,1)S(1)}, u32[]{:S(2)}, u32[]{:S(2)}) collective-permute-start(bf16[3,128,1024]{2,1,0:T(8,128)(2,1)} %get-tuple-element.60), channel_id=1, source_target_pairs={{1,30},{3,0},{5,2},{7,4},{9,6},{11,8},{13,10},{15,12},{17,14},{19,... | collective-permute-start | bytes 2359304 | tf_op jit(solution)/shard_map/ppermute | solution.py:323
  48.4 2.3 %collective-permute-start.2 = (bf16[3,128,1024]{2,1,0:T(8,128)(2,1)}, bf16[3,128,1024]{2,1,0:T(8,128)(2,1)}, u32[]{:S(2)}, u32[]{:S(2)}) collective-permute-start(bf16[3,128,1024]{2,1,0:T(8,128)(2,1)} %get-tuple-element.60), channel_id=1, source_target_pairs={{0,1},{1,0},{2,3},{3,2},{4,5},{5,4},{6,7},{7,6},{8,9},{9,8},{10,11... | collective-permute-start | bytes 2359304 | tf_op jit(solution)/shard_map/ppermute | solution.py:323
  51.3 7.5 %all-to-all-start = ((bf16[32,1,128]{2,1,0:T(2,128)(2,1)}), bf16[32,1,128]{2,1,0:T(2,128)(2,1)S(1)}, u32[]{:S(2)}, u32[]{:S(2)}) async-start(bf16[32,1,128]{2,1,0:T(2,128)(2,1)} %copy.8), calls=%async_computation | async-start | bytes 32768 | tf_op jit(solution)/shard_map/all_to_all | solution.py:346
  58.8 3.3 %collective-permute-start.3 = (bf16[3,128,1024]{2,1,0:T(8,128)(2,1)}, bf16[3,128,1024]{2,1,0:T(8,128)(2,1)S(1)}, u32[]{:S(2)}, u32[]{:S(2)}) collective-permute-start(bf16[3,128,1024]{2,1,0:T(8,128)(2,1)} %get-tuple-element.69.a_ref), channel_id=1, source_target_pairs={{0,30},{2,0},{4,2},{6,4},{8,6},{10,8},{12,10},{14,12},{16,14},{18,... | collective-permute-start | bytes 2359304 | tf_op jit(solution)/shard_map/ppermute | solution.py:323
  62.1 4.9 %collective-permute-start.4 = (bf16[3,128,1024]{2,1,0:T(8,128)(2,1)}, bf16[3,128,1024]{2,1,0:T(8,128)(2,1)S(1)}, u32[]{:S(2)}, u32[]{:S(2)}) collective-permute-start(bf16[3,128,1024]{2,1,0:T(8,128)(2,1)} %get-tuple-element.65), channel_id=1, source_target_pairs={{1,30},{3,0},{5,2},{7,4},{9,6},{11,8},{13,10},{15,12},{17,14},{19,... | collective-permute-start | bytes 2359304 | tf_op jit(solution)/shard_map/ppermute | solution.py:323
  71.3 6.1 %attend.2 = (bf16[64,1024]{1,0:T(8,128)(2,1)S(1)}, bf16[64,1024]{1,0:T(8,128)(2,1)S(1)}) custom-call(bf16[3,128,1024]{2,1,0:T(8,128)(2,1)} %get-tuple-element.59.a_ref, bf16[3,128,1024]{2,1,0:T(8,128)(2,1)S(1)} %collective-permute-done.c_ref, bf16[3,128,1024]{2,1,0:T(8,128)(2,1)S(1)} %collective-permute-done.1.d_ref, ...), custom_call_target="tpu_custom_call" | custom-call | flops 6899999744 | bytes 21000000 | tf_op jit(solution)/shard_map/attend/pallas_call | solution.py:219
  77.4 2.2 %index.1 = (s32[1,1024]{1,0:T(1,128)S(1)}, s32[1,2048]{1,0:T(1,128)S(1)}) custom-call(s32[4]{0:T(128)S(1)} %pad_add_fusion.scal_ref, s32[16,1024]{1,0:T(8,128)S(1)} %reshape.25.pos_ref), custom_call_target="tpu_custom_call" | custom-call | tf_op jit(solution)/shard_map/index/pallas_call | solution.py:355
  79.6 2.6 %collective-permute-done.4.d_ref = bf16[3,128,1024]{2,1,0:T(8,128)(2,1)S(1)} collective-permute-done((bf16[3,128,1024]{2,1,0:T(8,128)(2,1)}, bf16[3,128,1024]{2,1,0:T(8,128)(2,1)S(1)}, u32[]{:S(2)}, u32[]{:S(2)}) %collective-permute-start.4) | collective-permute-done | bytes 786464 | tf_op jit(solution)/shard_map/ppermute | solution.py:323
  82.2 6.1 %attend.3 = (bf16[64,1024]{1,0:T(8,128)(2,1)S(1)}, bf16[64,1024]{1,0:T(8,128)(2,1)S(1)}) custom-call(bf16[3,128,1024]{2,1,0:T(8,128)(2,1)} %get-tuple-element.69.a_ref, bf16[3,128,1024]{2,1,0:T(8,128)(2,1)S(1)} %collective-permute-done.3.c_ref, bf16[3,128,1024]{2,1,0:T(8,128)(2,1)S(1)} %collective-permute-done.4.d_ref, ...), custom_call_target="tpu_custom_call" | custom-call | flops 6899999744 | bytes 21000000 | tf_op jit(solution)/shard_map/attend/pallas_call | solution.py:219
  88.3 3.1 %collective-permute-start.6 = (bf16[64,2048]{1,0:T(8,128)(2,1)S(1)}, bf16[64,2048]{1,0:T(8,128)(2,1)S(1)}, u32[]{:S(2)}, u32[]{:S(2)}) collective-permute-start(bf16[64,2048]{1,0:T(8,128)(2,1)S(1)} %pad_maximum_fusion), channel_id=1, source_target_pairs={{0,2},{2,4},{4,6},{6,8},{8,10},{10,12},{12,14},{14,16},{16,18},{18... | collective-permute-start | bytes 786440 | tf_op jit(solution)/shard_map/ppermute | solution.py:323
  91.5 4.4 %collective-permute-done.6 = bf16[64,2048]{1,0:T(8,128)(2,1)S(1)} collective-permute-done((bf16[64,2048]{1,0:T(8,128)(2,1)S(1)}, bf16[64,2048]{1,0:T(8,128)(2,1)S(1)}, u32[]{:S(2)}, u32[]{:S(2)}) %collective-permute-start.6) | collective-permute-done | bytes 262176 | tf_op jit(solution)/shard_map/ppermute | solution.py:323
  95.9 1.9 %collective-permute-start.7 = (bf16[64,2048]{1,0:T(8,128)(2,1)S(1)}, bf16[64,2048]{1,0:T(8,128)(2,1)S(1)}, u32[]{:S(2)}, u32[]{:S(2)}) collective-permute-start(bf16[64,2048]{1,0:T(8,128)(2,1)S(1)} %multiply_convert_fusion.refs_1_), channel_id=1, source_target_pairs={{0,2},{1,3},{2,4},{3,5},{4,6},{5,7},{6,8},{7,9},{8,10},{9,11},{10,... | collective-permute-start | bytes 786440 | tf_op jit(solution)/shard_map/ppermute | solution.py:323
  97.9 4.6 %collective-permute-start.8 = (bf16[64,2048]{1,0:T(8,128)(2,1)S(1)}, bf16[64,2048]{1,0:T(8,128)(2,1)S(1)}, u32[]{:S(2)}, u32[]{:S(2)}) collective-permute-start(bf16[64,2048]{1,0:T(8,128)(2,1)S(1)} %multiply_convert_fusion.refs_1_), channel_id=1, source_target_pairs={{0,30},{1,31},{2,0},{3,1},{4,2},{5,3},{6,4},{7,5},{8,6},{9,7},{10,... | collective-permute-start | bytes 786440 | tf_op jit(solution)/shard_map/ppermute | solution.py:323
  102.4 2.2 %collective-permute-done.7.refs_0_ = bf16[64,2048]{1,0:T(8,128)(2,1)S(1)} collective-permute-done((bf16[64,2048]{1,0:T(8,128)(2,1)S(1)}, bf16[64,2048]{1,0:T(8,128)(2,1)S(1)}, u32[]{:S(2)}, u32[]{:S(2)}) %collective-permute-start.7) | collective-permute-done | bytes 262176 | tf_op jit(solution)/shard_map/ppermute | solution.py:323
  106.6 5.4 %collective-permute-start.11 = (bf16[64,2048]{1,0:T(8,128)(2,1)S(1)}, bf16[64,2048]{1,0:T(8,128)(2,1)S(1)}, u32[]{:S(2)}, u32[]{:S(2)}) collective-permute-start(bf16[64,2048]{1,0:T(8,128)(2,1)S(1)} %multiply_convert_fusion.refs_1_), channel_id=1, source_target_pairs={{0,1},{1,0},{2,3},{3,2},{4,5},{5,4},{6,7},{7,6},{8,9},{9,8},{10,11... | collective-permute-start | bytes 786440 | tf_op jit(solution)/shard_map/ppermute | solution.py:323
  113.9 2.4 %collective-permute-start.12 = (bf16[64,2048]{1,0:T(8,128)(2,1)S(1)}, bf16[64,2048]{1,0:T(8,128)(2,1)S(1)}, u32[]{:S(2)}, u32[]{:S(2)}) collective-permute-start(bf16[64,2048]{1,0:T(8,128)(2,1)S(1)} %collective-permute-done.8.refs_2_), channel_id=1, source_target_pairs={{0,1},{1,0},{2,3},{3,2},{4,5},{5,4},{6,7},{7,6},{8,9},{9,8},{10,11... | collective-permute-start | bytes 786440 | tf_op jit(solution)/shard_map/ppermute | solution.py:323
  116.3 3.2 %collective-permute-start.13 = (bf16[64,2048]{1,0:T(8,128)(2,1)S(1)}, bf16[64,2048]{1,0:T(8,128)(2,1)S(1)}, u32[]{:S(2)}, u32[]{:S(2)}) collective-permute-start(bf16[64,2048]{1,0:T(8,128)(2,1)S(1)} %collective-permute-done.9.refs_3_), channel_id=1, source_target_pairs={{0,1},{1,0},{2,3},{3,2},{4,5},{5,4},{6,7},{7,6},{8,9},{9,8},{10,11... | collective-permute-start | bytes 786440 | tf_op jit(solution)/shard_map/ppermute | solution.py:323
  120.6 3.6 %project.1 = bf16[4,256,128]{2,1,0:T(8,128)(2,1)S(1)} custom-call(s32[4]{0:T(128)S(1)} %pad_add_fusion.scal_ref, bf16[64,2048]{1,0:T(8,128)(2,1)S(1)} %collective-permute-done.7.refs_0_, bf16[64,2048]{1,0:T(8,128)(2,1)S(1)} %multiply_convert_fusion.refs_1_, bf16[64,2048]{1,0:T(8,128)(2,1)S(1)} %collective-permute-done.8.refs_2_, ...), custom_call_target="tpu_custom_call" | custom-call | flops 4600000000 | bytes 14000000 | tf_op jit(solution)/shard_map/project/pallas_call | solution.py:249
  124.2 26.8 %all_to_all.25.got_ref = bf16[4,256,128]{2,1,0:T(8,128)(2,1)S(1)} all-to-all(bf16[4,256,128]{2,1,0:T(8,128)(2,1)S(1)} %project.1), channel_id=1, replica_groups=mesh['grp'=16,'zq'=4,'zr'=4,'core'=2] {'zq'}, dimensions={0} | all-to-all | bytes 524288 | tf_op jit(solution)/shard_map/all_to_all | solution.py:374
  152.8 16.0 %all_to_all.26 = bf16[16,128,128]{2,1,0:T(8,128)(2,1)S(1)} all-to-all(bf16[16,128,128]{2,1,0:T(8,128)(2,1)S(1)} %bitcast.13), channel_id=1, replica_groups=mesh['grp'=16,'zq'=4,'zr'=4,'core'=2] {'grp'}, dimensions={0} | all-to-all | bytes 1048576 | tf_op jit(solution)/shard_map/all_to_all | solution.py:385
  168.9 1.9 %place.1 = bf16[1024,128]{1,0:T(8,128)(2,1)} custom-call(s32[1,2048]{1,0:T(1,128)S(1)} %get-tuple-element.67.from_ref, bf16[2048,128]{1,0:T(8,128)(2,1)S(1)} %bitcast.14), custom_call_target="tpu_custom_call" | custom-call | tf_op jit(solution)/shard_map/place/pallas_call | solution.py:386
  (39 shorter events, 12.6 us)
Async XLA Ops:
  6.5 113.0 %all-gather.4.cloned.1.call-start = ((), (), s32[]{:S(2)}) async-start(), calls=%async_computation.3 | async-start | bytes 4456448 | tf_op jit(solution)/shard_map/all_gather | solution.py:330
  6.6 0.7 copy-start
  7.3 6.2 %copy-start.2 = (bf16[256,128]{1,0:T(8,128)(2,1)S(1)}, bf16[256,128]{1,0:T(8,128)(2,1)}, u32[]{:S(2)}) copy-start(bf16[256,128]{1,0:T(8,128)(2,1)} %param.11) | copy-start | bytes 196612
  7.3 43.4 %copy-start.5 = (bf16[128]{0:T(256)(128)(2,1)S(1)}, bf16[128]{0:T(256)(128)(2,1)}, u32[]{:S(2)}) copy-start(bf16[128]{0:T(256)(128)(2,1)} %param.10) | copy-start | bytes 772
  7.3 59.7 %copy-start.1 = (s32[16,2]{0,1:T(2,128)S(1)}, s32[16,2]{0,1:T(2,128)}, u32[]{:S(2)}) copy-start(s32[16,2]{0,1:T(2,128)} %param.12) | copy-start | bytes 388
  39.1 29.6 %collective-permute-start = (bf16[3,128,1024]{2,1,0:T(8,128)(2,1)}, bf16[3,128,1024]{2,1,0:T(8,128)(2,1)S(1)}, u32[]{:S(2)}, u32[]{:S(2)}) collective-permute-start(bf16[3,128,1024]{2,1,0:T(8,128)(2,1)} %get-tuple-element.59.a_ref), channel_id=1, source_target_pairs={{0,30},{2,0},{4,2},{6,4},{8,6},{10,8},{12,10},{14,12},{16,14},{18,... | collective-permute-start | bytes 2359304 | tf_op jit(solution)/shard_map/ppermute | solution.py:323
  42.0 29.3 %collective-permute-start.1 = (bf16[3,128,1024]{2,1,0:T(8,128)(2,1)}, bf16[3,128,1024]{2,1,0:T(8,128)(2,1)S(1)}, u32[]{:S(2)}, u32[]{:S(2)}) collective-permute-start(bf16[3,128,1024]{2,1,0:T(8,128)(2,1)} %get-tuple-element.60), channel_id=1, source_target_pairs={{1,30},{3,0},{5,2},{7,4},{9,6},{11,8},{13,10},{15,12},{17,14},{19,... | collective-permute-start | bytes 2359304 | tf_op jit(solution)/shard_map/ppermute | solution.py:323
  48.4 22.9 %collective-permute-start.2 = (bf16[3,128,1024]{2,1,0:T(8,128)(2,1)}, bf16[3,128,1024]{2,1,0:T(8,128)(2,1)}, u32[]{:S(2)}, u32[]{:S(2)}) collective-permute-start(bf16[3,128,1024]{2,1,0:T(8,128)(2,1)} %get-tuple-element.60), channel_id=1, source_target_pairs={{0,1},{1,0},{2,3},{3,2},{4,5},{5,4},{6,7},{7,6},{8,9},{9,8},{10,11... | collective-permute-start | bytes 2359304 | tf_op jit(solution)/shard_map/ppermute | solution.py:323
  51.3 19.3 %all-to-all-start = ((bf16[32,1,128]{2,1,0:T(2,128)(2,1)}), bf16[32,1,128]{2,1,0:T(2,128)(2,1)S(1)}, u32[]{:S(2)}, u32[]{:S(2)}) async-start(bf16[32,1,128]{2,1,0:T(2,128)(2,1)} %copy.8), calls=%async_computation | async-start | bytes 32768 | tf_op jit(solution)/shard_map/all_to_all | solution.py:346
  58.8 20.8 %collective-permute-start.3 = (bf16[3,128,1024]{2,1,0:T(8,128)(2,1)}, bf16[3,128,1024]{2,1,0:T(8,128)(2,1)S(1)}, u32[]{:S(2)}, u32[]{:S(2)}) collective-permute-start(bf16[3,128,1024]{2,1,0:T(8,128)(2,1)} %get-tuple-element.69.a_ref), channel_id=1, source_target_pairs={{0,30},{2,0},{4,2},{6,4},{8,6},{10,8},{12,10},{14,12},{16,14},{18,... | collective-permute-start | bytes 2359304 | tf_op jit(solution)/shard_map/ppermute | solution.py:323
  62.1 20.1 %collective-permute-start.4 = (bf16[3,128,1024]{2,1,0:T(8,128)(2,1)}, bf16[3,128,1024]{2,1,0:T(8,128)(2,1)S(1)}, u32[]{:S(2)}, u32[]{:S(2)}) collective-permute-start(bf16[3,128,1024]{2,1,0:T(8,128)(2,1)} %get-tuple-element.65), channel_id=1, source_target_pairs={{1,30},{3,0},{5,2},{7,4},{9,6},{11,8},{13,10},{15,12},{17,14},{19,... | collective-permute-start | bytes 2359304 | tf_op jit(solution)/shard_map/ppermute | solution.py:323
  68.7 13.5 %collective-permute-start.5 = (bf16[3,128,1024]{2,1,0:T(8,128)(2,1)}, bf16[3,128,1024]{2,1,0:T(8,128)(2,1)}, u32[]{:S(2)}, u32[]{:S(2)}) collective-permute-start(bf16[3,128,1024]{2,1,0:T(8,128)(2,1)} %get-tuple-element.65), channel_id=1, source_target_pairs={{0,1},{1,0},{2,3},{3,2},{4,5},{5,4},{6,7},{7,6},{8,9},{9,8},{10,11... | collective-permute-start | bytes 2359304 | tf_op jit(solution)/shard_map/ppermute | solution.py:323
  71.3 6.1 %copy-start.3 = (s32[16384]{0:T(1024)S(1)}, s32[16384]{0:T(1024)}, u32[]{:S(2)}) copy-start(s32[16384]{0:T(1024)} %param.13) | copy-start | bytes 196612
  79.6 16.3 %copy-start.4 = (f32[1,2048]{1,0:T(1,128)S(1)}, f32[1,2048]{1,0:T(1,128)}, u32[]{:S(2)}) copy-start(f32[1,2048]{1,0:T(1,128)} %bitcast_convert_fusion) | copy-start | bytes 24580
  88.3 7.5 %collective-permute-start.6 = (bf16[64,2048]{1,0:T(8,128)(2,1)S(1)}, bf16[64,2048]{1,0:T(8,128)(2,1)S(1)}, u32[]{:S(2)}, u32[]{:S(2)}) collective-permute-start(bf16[64,2048]{1,0:T(8,128)(2,1)S(1)} %pad_maximum_fusion), channel_id=1, source_target_pairs={{0,2},{2,4},{4,6},{6,8},{8,10},{10,12},{12,14},{14,16},{16,18},{18... | collective-permute-start | bytes 786440 | tf_op jit(solution)/shard_map/ppermute | solution.py:323
  95.9 8.7 %collective-permute-start.7 = (bf16[64,2048]{1,0:T(8,128)(2,1)S(1)}, bf16[64,2048]{1,0:T(8,128)(2,1)S(1)}, u32[]{:S(2)}, u32[]{:S(2)}) collective-permute-start(bf16[64,2048]{1,0:T(8,128)(2,1)S(1)} %multiply_convert_fusion.refs_1_), channel_id=1, source_target_pairs={{0,2},{1,3},{2,4},{3,5},{4,6},{5,7},{6,8},{7,9},{8,10},{9,11},{10,... | collective-permute-start | bytes 786440 | tf_op jit(solution)/shard_map/ppermute | solution.py:323
  97.9 16.0 %collective-permute-start.8 = (bf16[64,2048]{1,0:T(8,128)(2,1)S(1)}, bf16[64,2048]{1,0:T(8,128)(2,1)S(1)}, u32[]{:S(2)}, u32[]{:S(2)}) collective-permute-start(bf16[64,2048]{1,0:T(8,128)(2,1)S(1)} %multiply_convert_fusion.refs_1_), channel_id=1, source_target_pairs={{0,30},{1,31},{2,0},{3,1},{4,2},{5,3},{6,4},{7,5},{8,6},{9,7},{10,... | collective-permute-start | bytes 786440 | tf_op jit(solution)/shard_map/ppermute | solution.py:323
  104.6 11.7 %collective-permute-start.9 = (bf16[64,2048]{1,0:T(8,128)(2,1)S(1)}, bf16[64,2048]{1,0:T(8,128)(2,1)S(1)}, u32[]{:S(2)}, u32[]{:S(2)}) collective-permute-start(bf16[64,2048]{1,0:T(8,128)(2,1)S(1)} %collective-permute-done.7.refs_0_), channel_id=1, source_target_pairs={{0,2},{1,3},{2,4},{3,5},{4,6},{5,7},{6,8},{7,9},{8,10},{9,11},{10,... | collective-permute-start | bytes 786440 | tf_op jit(solution)/shard_map/ppermute | solution.py:323
  106.6 12.9 %collective-permute-start.11 = (bf16[64,2048]{1,0:T(8,128)(2,1)S(1)}, bf16[64,2048]{1,0:T(8,128)(2,1)S(1)}, u32[]{:S(2)}, u32[]{:S(2)}) collective-permute-start(bf16[64,2048]{1,0:T(8,128)(2,1)S(1)} %multiply_convert_fusion.refs_1_), channel_id=1, source_target_pairs={{0,1},{1,0},{2,3},{3,2},{4,5},{5,4},{6,7},{7,6},{8,9},{9,8},{10,11... | collective-permute-start | bytes 786440 | tf_op jit(solution)/shard_map/ppermute | solution.py:323
  111.9 7.6 %collective-permute-start.10 = (bf16[64,2048]{1,0:T(8,128)(2,1)S(1)}, bf16[64,2048]{1,0:T(8,128)(2,1)S(1)}, u32[]{:S(2)}, u32[]{:S(2)}) collective-permute-start(bf16[64,2048]{1,0:T(8,128)(2,1)S(1)} %collective-permute-done.7.refs_0_), channel_id=1, source_target_pairs={{0,1},{1,0},{2,3},{3,2},{4,5},{5,4},{6,7},{7,6},{8,9},{9,8},{10,11... | collective-permute-start | bytes 786440 | tf_op jit(solution)/shard_map/ppermute | solution.py:323
  113.9 5.7 %collective-permute-start.12 = (bf16[64,2048]{1,0:T(8,128)(2,1)S(1)}, bf16[64,2048]{1,0:T(8,128)(2,1)S(1)}, u32[]{:S(2)}, u32[]{:S(2)}) collective-permute-start(bf16[64,2048]{1,0:T(8,128)(2,1)S(1)} %collective-permute-done.8.refs_2_), channel_id=1, source_target_pairs={{0,1},{1,0},{2,3},{3,2},{4,5},{5,4},{6,7},{7,6},{8,9},{9,8},{10,11... | collective-permute-start | bytes 786440 | tf_op jit(solution)/shard_map/ppermute | solution.py:323
  116.3 4.3 %collective-permute-start.13 = (bf16[64,2048]{1,0:T(8,128)(2,1)S(1)}, bf16[64,2048]{1,0:T(8,128)(2,1)S(1)}, u32[]{:S(2)}, u32[]{:S(2)}) collective-permute-start(bf16[64,2048]{1,0:T(8,128)(2,1)S(1)} %collective-permute-done.9.refs_3_), channel_id=1, source_target_pairs={{0,1},{1,0},{2,3},{3,2},{4,5},{5,4},{6,7},{7,6},{8,9},{9,8},{10,11... | collective-permute-start | bytes 786440 | tf_op jit(solution)/shard_map/ppermute | solution.py:323
Sparse Core Ops, SparseCore 0:
  39.3 65.7 all-gather.3

commit v8 on v7

--- a/solution.py
+++ b/solution.py
@@ -129,7 +129,7 @@
 
     outs = pl.pallas_call(
         rope_kernel,
-        out_shape=[pltpu.HBM((3, BLK, WIDE), BF16)] * (2 * CHUNKS),
+        out_shape=[jax.ShapeDtypeStruct((3, BLK, WIDE), BF16)] * (2 * CHUNKS),
         grid_spec=pltpu.PrefetchScalarGridSpec(
             num_scalar_prefetch=1,
             grid=(2 * CHUNKS,),
@@ -214,7 +214,7 @@
 
 def attend(parts, tables):
     part = pl.BlockSpec((3, BLK, STEP * HD), lambda h: (0, 0, h))
-    own, tables = ([pltpu.with_memory_space_constraint(t, pltpu.HBM) for t in x] for x in (parts[:1], tables))
+    tables = [pltpu.with_memory_space_constraint(t, pltpu.HBM) for t in tables]
     whole = [pl.BlockSpec(t.shape, lambda h: (0, 0)) for t in tables]
     return pl.pallas_call(
         attend_kernel,
@@ -225,7 +225,7 @@
         compiler_params=params(32),
         cost_estimate=cost(6),
         name="attend",
-    )(*own, *parts[1:], *tables)
+    )(*parts, *tables)
 
 
 def project_kernel(scal_ref, *refs):

time: 181 us -> 179 us (0.989)
    all_to_all x1, blocking collectives: 16 us -> 18.1 us  [body(): out = lax.all_to_all(out, 'grp', split_axis=0, concat_axis=0, tiled=True)]
    all_to_all x1, blocking collectives: 26.8 us -> 24.8 us  [body(): out = lax.all_to_all(out, 'zq', split_axis=0, concat_axis=0, tiled=True)]
where the time goes in v8:
time: 179 us; the launch traced here: 176 us
  blocking collectives  68.4 us (38%)
  starting transfers between devices  53.9 us (30%)
  Pallas kernels  28.3 us (16%)
  between operations  13.7 us (8%)
  waiting for transfers between devices  9.7 us (5%)
    ppermute x14, starting transfers between devices, move(): return lax.ppermute(x, MLP, perm)  46.4 us
    all_gather x1, blocking collectives, body(): cols = lax.all_gather(w_merge, 'zq', axis=0)  25.6 us
    all_to_all x1, blocking collectives, body(): out = lax.all_to_all(out, 'zq', split_axis=0, concat_axis=0, tiled=True)  24.8 us
    all_to_all x1, blocking collectives, body(): out = lax.all_to_all(out, 'grp', split_axis=0, concat_axis=0, tiled=True)  18.1 us
    pallas_call x2, Pallas kernels, attend(): pl.pallas_call(attend_kernel, grid=(HEADS // STEP,), out_shape=[jax.Shape...  12.4 us
    ppermute x14, waiting for transfers between devices, move(): return lax.ppermute(x, MLP, perm)  9.66 us
    all_to_all x1, starting transfers between devices, body(): gains = lax.all_to_all(gains, MLP, split_axis=0, concat_axis=0, tiled=True)  7.47 us
    pallas_call x1, Pallas kernels, rope(): pl.pallas_call(rope_kernel, out_shape=[jax.ShapeDtypeStruct((3, BLK, WIDE...  4.61 us
  transfers between devices with their start and end apart: 16, of which 4 were waited for; matrix products, arithmetic and copies ran while one was open for 1% of the time, Pallas kernels for 9%

profile of v8, /device:TPU:1, one launch (start us, length us, event | category | flops | bytes accessed | tf_op | source)
XLA Modules:
  0.0 176.1 jit_solution(15853858506723886656)
XLA Ops:
  7.3 4.6 %rope.1 = (bf16[3,128,1024]{2,1,0:T(8,128)(2,1)S(1)}, bf16[3,128,1024]{2,1,0:T(8,128)(2,1)S(1)}, bf16[3,128,1024]{2,1,0:T(8,128)(2,1)S(1)}, bf16[3,128,1024]{2,1,0:T(8,128)(2,1)S(1)}) custom-call(s32[4]{0:T(128)S(1)} %pad_add_fusion.scal_ref, s32[2,16]{1,0:T(2,128)S(1)} %bitcast.15, bf16[128,4096]{1,0:T(8,128)(2,1)} %q_ref.1, bf16[128,4096]{1,0:T(8,128)(2,1)} %k_ref.1, ...), custom_call_target="tpu_custom_call" | custom-call | flops 6899999744 | bytes 21000000 | tf_op jit(solution)/shard_map/rope/pallas_call | solution.py:130
  11.9 25.6 %all-gather = bf16[1024,128]{1,0:T(8,128)(2,1)} all-gather(bf16[256,128]{1,0:T(8,128)(2,1)S(1)} %copy-done.1), channel_id=2, replica_groups=mesh['grp'=16,'zq'=4,'zr'=4,'core'=2] {'zq'}, dimensions={0}, use_global_device_ids=true | all-gather | bytes 327680 | tf_op jit(solution)/shard_map/all_gather | solution.py:328
  37.5 2.8 %collective-permute-start = (bf16[3,128,1024]{2,1,0:T(8,128)(2,1)S(1)}, bf16[3,128,1024]{2,1,0:T(8,128)(2,1)}, u32[]{:S(2)}, u32[]{:S(2)}) collective-permute-start(bf16[3,128,1024]{2,1,0:T(8,128)(2,1)S(1)} %get-tuple-element.59.a_ref), channel_id=1, source_target_pairs={{0,30},{2,0},{4,2},{6,4},{8,6},{10,8},{12,10},{14,12},{16,14},{18,... | collective-permute-start | bytes 2359304 | tf_op jit(solution)/shard_map/ppermute | solution.py:323
  40.4 6.4 %collective-permute-start.1 = (bf16[3,128,1024]{2,1,0:T(8,128)(2,1)S(1)}, bf16[3,128,1024]{2,1,0:T(8,128)(2,1)}, u32[]{:S(2)}, u32[]{:S(2)}) collective-permute-start(bf16[3,128,1024]{2,1,0:T(8,128)(2,1)S(1)} %get-tuple-element.60), channel_id=1, source_target_pairs={{1,30},{3,0},{5,2},{7,4},{9,6},{11,8},{13,10},{15,12},{17,14},{19,... | collective-permute-start | bytes 2359304 | tf_op jit(solution)/shard_map/ppermute | solution.py:323
  46.8 2.3 %collective-permute-start.2 = (bf16[3,128,1024]{2,1,0:T(8,128)(2,1)S(1)}, bf16[3,128,1024]{2,1,0:T(8,128)(2,1)}, u32[]{:S(2)}, u32[]{:S(2)}) collective-permute-start(bf16[3,128,1024]{2,1,0:T(8,128)(2,1)S(1)} %get-tuple-element.60), channel_id=1, source_target_pairs={{0,1},{1,0},{2,3},{3,2},{4,5},{5,4},{6,7},{7,6},{8,9},{9,8},{10,11... | collective-permute-start | bytes 2359304 | tf_op jit(solution)/shard_map/ppermute | solution.py:323
  49.7 7.5 %all-to-all-start = ((bf16[32,1,128]{2,1,0:T(2,128)(2,1)}), bf16[32,1,128]{2,1,0:T(2,128)(2,1)S(1)}, u32[]{:S(2)}, u32[]{:S(2)}) async-start(bf16[32,1,128]{2,1,0:T(2,128)(2,1)} %copy.8), calls=%async_computation | async-start | bytes 32768 | tf_op jit(solution)/shard_map/all_to_all | solution.py:346
  57.2 3.3 %collective-permute-start.3 = (bf16[3,128,1024]{2,1,0:T(8,128)(2,1)S(1)}, bf16[3,128,1024]{2,1,0:T(8,128)(2,1)}, u32[]{:S(2)}, u32[]{:S(2)}) collective-permute-start(bf16[3,128,1024]{2,1,0:T(8,128)(2,1)S(1)} %get-tuple-element.69.a_ref), channel_id=1, source_target_pairs={{0,30},{2,0},{4,2},{6,4},{8,6},{10,8},{12,10},{14,12},{16,14},{18,... | collective-permute-start | bytes 2359304 | tf_op jit(solution)/shard_map/ppermute | solution.py:323
  60.5 4.9 %collective-permute-start.4 = (bf16[3,128,1024]{2,1,0:T(8,128)(2,1)S(1)}, bf16[3,128,1024]{2,1,0:T(8,128)(2,1)}, u32[]{:S(2)}, u32[]{:S(2)}) collective-permute-start(bf16[3,128,1024]{2,1,0:T(8,128)(2,1)S(1)} %get-tuple-element.65), channel_id=1, source_target_pairs={{1,30},{3,0},{5,2},{7,4},{9,6},{11,8},{13,10},{15,12},{17,14},{19,... | collective-permute-start | bytes 2359304 | tf_op jit(solution)/shard_map/ppermute | solution.py:323
  69.7 6.2 %attend.2 = (bf16[64,1024]{1,0:T(8,128)(2,1)S(1)}, bf16[64,1024]{1,0:T(8,128)(2,1)S(1)}) custom-call(bf16[3,128,1024]{2,1,0:T(8,128)(2,1)S(1)} %get-tuple-element.59.a_ref, bf16[3,128,1024]{2,1,0:T(8,128)(2,1)} %collective-permute-done.c_ref, bf16[3,128,1024]{2,1,0:T(8,128)(2,1)} %collective-permute-done.1.d_ref, ...), custom_call_target="tpu_custom_call" | custom-call | flops 6899999744 | bytes 21000000 | tf_op jit(solution)/shard_map/attend/pallas_call | solution.py:219
  75.9 2.2 %index.1 = (s32[1,1024]{1,0:T(1,128)S(1)}, s32[1,2048]{1,0:T(1,128)S(1)}) custom-call(s32[4]{0:T(128)S(1)} %pad_add_fusion.scal_ref, s32[16,1024]{1,0:T(8,128)S(1)} %reshape.25.pos_ref), custom_call_target="tpu_custom_call" | custom-call | tf_op jit(solution)/shard_map/index/pallas_call | solution.py:355
  78.1 2.2 %collective-permute-done.4.d_ref = bf16[3,128,1024]{2,1,0:T(8,128)(2,1)} collective-permute-done((bf16[3,128,1024]{2,1,0:T(8,128)(2,1)S(1)}, bf16[3,128,1024]{2,1,0:T(8,128)(2,1)}, u32[]{:S(2)}, u32[]{:S(2)}) %collective-permute-start.4) | collective-permute-done | bytes 786464 | tf_op jit(solution)/shard_map/ppermute | solution.py:323
  80.3 6.2 %attend.3 = (bf16[64,1024]{1,0:T(8,128)(2,1)S(1)}, bf16[64,1024]{1,0:T(8,128)(2,1)S(1)}) custom-call(bf16[3,128,1024]{2,1,0:T(8,128)(2,1)S(1)} %get-tuple-element.69.a_ref, bf16[3,128,1024]{2,1,0:T(8,128)(2,1)} %collective-permute-done.3.c_ref, bf16[3,128,1024]{2,1,0:T(8,128)(2,1)} %collective-permute-done.4.d_ref, ...), custom_call_target="tpu_custom_call" | custom-call | flops 6899999744 | bytes 21000000 | tf_op jit(solution)/shard_map/attend/pallas_call | solution.py:219
  86.5 3.4 %collective-permute-start.6 = (bf16[64,2048]{1,0:T(8,128)(2,1)S(1)}, bf16[64,2048]{1,0:T(8,128)(2,1)S(1)}, u32[]{:S(2)}, u32[]{:S(2)}) collective-permute-start(bf16[64,2048]{1,0:T(8,128)(2,1)S(1)} %pad_maximum_fusion), channel_id=1, source_target_pairs={{0,2},{2,4},{4,6},{6,8},{8,10},{10,12},{12,14},{14,16},{16,18},{18... | collective-permute-start | bytes 786440 | tf_op jit(solution)/shard_map/ppermute | solution.py:323
  89.9 4.2 %collective-permute-done.6 = bf16[64,2048]{1,0:T(8,128)(2,1)S(1)} collective-permute-done((bf16[64,2048]{1,0:T(8,128)(2,1)S(1)}, bf16[64,2048]{1,0:T(8,128)(2,1)S(1)}, u32[]{:S(2)}, u32[]{:S(2)}) %collective-permute-start.6) | collective-permute-done | bytes 262176 | tf_op jit(solution)/shard_map/ppermute | solution.py:323
  94.1 2.1 %collective-permute-start.7 = (bf16[64,2048]{1,0:T(8,128)(2,1)S(1)}, bf16[64,2048]{1,0:T(8,128)(2,1)S(1)}, u32[]{:S(2)}, u32[]{:S(2)}) collective-permute-start(bf16[64,2048]{1,0:T(8,128)(2,1)S(1)} %multiply_convert_fusion.refs_1_), channel_id=1, source_target_pairs={{0,2},{1,3},{2,4},{3,5},{4,6},{5,7},{6,8},{7,9},{8,10},{9,11},{10,... | collective-permute-start | bytes 786440 | tf_op jit(solution)/shard_map/ppermute | solution.py:323
  96.3 4.4 %collective-permute-start.8 = (bf16[64,2048]{1,0:T(8,128)(2,1)S(1)}, bf16[64,2048]{1,0:T(8,128)(2,1)S(1)}, u32[]{:S(2)}, u32[]{:S(2)}) collective-permute-start(bf16[64,2048]{1,0:T(8,128)(2,1)S(1)} %multiply_convert_fusion.refs_1_), channel_id=1, source_target_pairs={{0,30},{1,31},{2,0},{3,1},{4,2},{5,3},{6,4},{7,5},{8,6},{9,7},{10,... | collective-permute-start | bytes 786440 | tf_op jit(solution)/shard_map/ppermute | solution.py:323
  100.6 2.2 %collective-permute-done.7.refs_0_ = bf16[64,2048]{1,0:T(8,128)(2,1)S(1)} collective-permute-done((bf16[64,2048]{1,0:T(8,128)(2,1)S(1)}, bf16[64,2048]{1,0:T(8,128)(2,1)S(1)}, u32[]{:S(2)}, u32[]{:S(2)}) %collective-permute-start.7) | collective-permute-done | bytes 262176 | tf_op jit(solution)/shard_map/ppermute | solution.py:323
  104.8 5.6 %collective-permute-start.11 = (bf16[64,2048]{1,0:T(8,128)(2,1)S(1)}, bf16[64,2048]{1,0:T(8,128)(2,1)S(1)}, u32[]{:S(2)}, u32[]{:S(2)}) collective-permute-start(bf16[64,2048]{1,0:T(8,128)(2,1)S(1)} %multiply_convert_fusion.refs_1_), channel_id=1, source_target_pairs={{0,1},{1,0},{2,3},{3,2},{4,5},{5,4},{6,7},{7,6},{8,9},{9,8},{10,11... | collective-permute-start | bytes 786440 | tf_op jit(solution)/shard_map/ppermute | solution.py:323
  112.3 2.4 %collective-permute-start.12 = (bf16[64,2048]{1,0:T(8,128)(2,1)S(1)}, bf16[64,2048]{1,0:T(8,128)(2,1)S(1)}, u32[]{:S(2)}, u32[]{:S(2)}) collective-permute-start(bf16[64,2048]{1,0:T(8,128)(2,1)S(1)} %collective-permute-done.8.refs_2_), channel_id=1, source_target_pairs={{0,1},{1,0},{2,3},{3,2},{4,5},{5,4},{6,7},{7,6},{8,9},{9,8},{10,11... | collective-permute-start | bytes 786440 | tf_op jit(solution)/shard_map/ppermute | solution.py:323
  114.7 3.2 %collective-permute-start.13 = (bf16[64,2048]{1,0:T(8,128)(2,1)S(1)}, bf16[64,2048]{1,0:T(8,128)(2,1)S(1)}, u32[]{:S(2)}, u32[]{:S(2)}) collective-permute-start(bf16[64,2048]{1,0:T(8,128)(2,1)S(1)} %collective-permute-done.9.refs_3_), channel_id=1, source_target_pairs={{0,1},{1,0},{2,3},{3,2},{4,5},{5,4},{6,7},{7,6},{8,9},{9,8},{10,11... | collective-permute-start | bytes 786440 | tf_op jit(solution)/shard_map/ppermute | solution.py:323
  119.0 3.6 %project.1 = bf16[4,256,128]{2,1,0:T(8,128)(2,1)S(1)} custom-call(s32[4]{0:T(128)S(1)} %pad_add_fusion.scal_ref, bf16[64,2048]{1,0:T(8,128)(2,1)S(1)} %collective-permute-done.7.refs_0_, bf16[64,2048]{1,0:T(8,128)(2,1)S(1)} %multiply_convert_fusion.refs_1_, bf16[64,2048]{1,0:T(8,128)(2,1)S(1)} %collective-permute-done.8.refs_2_, ...), custom_call_target="tpu_custom_call" | custom-call | flops 4600000000 | bytes 14000000 | tf_op jit(solution)/shard_map/project/pallas_call | solution.py:249
  122.6 24.8 %all_to_all.25.got_ref = bf16[4,256,128]{2,1,0:T(8,128)(2,1)S(1)} all-to-all(bf16[4,256,128]{2,1,0:T(8,128)(2,1)S(1)} %project.1), channel_id=1, replica_groups=mesh['grp'=16,'zq'=4,'zr'=4,'core'=2] {'zq'}, dimensions={0} | all-to-all | bytes 524288 | tf_op jit(solution)/shard_map/all_to_all | solution.py:374
  149.2 18.1 %all_to_all.26 = bf16[16,128,128]{2,1,0:T(8,128)(2,1)S(1)} all-to-all(bf16[16,128,128]{2,1,0:T(8,128)(2,1)S(1)} %bitcast.13), channel_id=1, replica_groups=mesh['grp'=16,'zq'=4,'zr'=4,'core'=2] {'grp'}, dimensions={0} | all-to-all | bytes 1048576 | tf_op jit(solution)/shard_map/all_to_all | solution.py:385
  167.3 2.0 %place.1 = bf16[1024,128]{1,0:T(8,128)(2,1)} custom-call(s32[1,2048]{1,0:T(1,128)S(1)} %get-tuple-element.67.from_ref, bf16[2048,128]{1,0:T(8,128)(2,1)S(1)} %bitcast.14), custom_call_target="tpu_custom_call" | custom-call | tf_op jit(solution)/shard_map/place/pallas_call | solution.py:386
  (37 shorter events, 12.6 us)
Async XLA Ops:
  6.5 111.4 %all-gather.4.cloned.1.call-start = ((), (), s32[]{:S(2)}) async-start(), calls=%async_computation.3 | async-start | bytes 4456448 | tf_op jit(solution)/shard_map/all_gather | solution.py:330
  6.6 0.7 copy-start
  7.3 4.6 %copy-start.1 = (bf16[256,128]{1,0:T(8,128)(2,1)S(1)}, bf16[256,128]{1,0:T(8,128)(2,1)}, u32[]{:S(2)}) copy-start(bf16[256,128]{1,0:T(8,128)(2,1)} %param.11) | copy-start | bytes 196612
  7.3 41.8 %copy-start.4 = (bf16[128]{0:T(256)(128)(2,1)S(1)}, bf16[128]{0:T(256)(128)(2,1)}, u32[]{:S(2)}) copy-start(bf16[128]{0:T(256)(128)(2,1)} %param.10) | copy-start | bytes 772
  37.5 29.6 %collective-permute-start = (bf16[3,128,1024]{2,1,0:T(8,128)(2,1)S(1)}, bf16[3,128,1024]{2,1,0:T(8,128)(2,1)}, u32[]{:S(2)}, u32[]{:S(2)}) collective-permute-start(bf16[3,128,1024]{2,1,0:T(8,128)(2,1)S(1)} %get-tuple-element.59.a_ref), channel_id=1, source_target_pairs={{0,30},{2,0},{4,2},{6,4},{8,6},{10,8},{12,10},{14,12},{16,14},{18,... | collective-permute-start | bytes 2359304 | tf_op jit(solution)/shard_map/ppermute | solution.py:323
  40.4 29.3 %collective-permute-start.1 = (bf16[3,128,1024]{2,1,0:T(8,128)(2,1)S(1)}, bf16[3,128,1024]{2,1,0:T(8,128)(2,1)}, u32[]{:S(2)}, u32[]{:S(2)}) collective-permute-start(bf16[3,128,1024]{2,1,0:T(8,128)(2,1)S(1)} %get-tuple-element.60), channel_id=1, source_target_pairs={{1,30},{3,0},{5,2},{7,4},{9,6},{11,8},{13,10},{15,12},{17,14},{19,... | collective-permute-start | bytes 2359304 | tf_op jit(solution)/shard_map/ppermute | solution.py:323
  46.8 22.9 %collective-permute-start.2 = (bf16[3,128,1024]{2,1,0:T(8,128)(2,1)S(1)}, bf16[3,128,1024]{2,1,0:T(8,128)(2,1)}, u32[]{:S(2)}, u32[]{:S(2)}) collective-permute-start(bf16[3,128,1024]{2,1,0:T(8,128)(2,1)S(1)} %get-tuple-element.60), channel_id=1, source_target_pairs={{0,1},{1,0},{2,3},{3,2},{4,5},{5,4},{6,7},{7,6},{8,9},{9,8},{10,11... | collective-permute-start | bytes 2359304 | tf_op jit(solution)/shard_map/ppermute | solution.py:323
  49.7 19.3 %all-to-all-start = ((bf16[32,1,128]{2,1,0:T(2,128)(2,1)}), bf16[32,1,128]{2,1,0:T(2,128)(2,1)S(1)}, u32[]{:S(2)}, u32[]{:S(2)}) async-start(bf16[32,1,128]{2,1,0:T(2,128)(2,1)} %copy.8), calls=%async_computation | async-start | bytes 32768 | tf_op jit(solution)/shard_map/all_to_all | solution.py:346
  57.2 20.9 %collective-permute-start.3 = (bf16[3,128,1024]{2,1,0:T(8,128)(2,1)S(1)}, bf16[3,128,1024]{2,1,0:T(8,128)(2,1)}, u32[]{:S(2)}, u32[]{:S(2)}) collective-permute-start(bf16[3,128,1024]{2,1,0:T(8,128)(2,1)S(1)} %get-tuple-element.69.a_ref), channel_id=1, source_target_pairs={{0,30},{2,0},{4,2},{6,4},{8,6},{10,8},{12,10},{14,12},{16,14},{18,... | collective-permute-start | bytes 2359304 | tf_op jit(solution)/shard_map/ppermute | solution.py:323
  60.5 19.8 %collective-permute-start.4 = (bf16[3,128,1024]{2,1,0:T(8,128)(2,1)S(1)}, bf16[3,128,1024]{2,1,0:T(8,128)(2,1)}, u32[]{:S(2)}, u32[]{:S(2)}) collective-permute-start(bf16[3,128,1024]{2,1,0:T(8,128)(2,1)S(1)} %get-tuple-element.65), channel_id=1, source_target_pairs={{1,30},{3,0},{5,2},{7,4},{9,6},{11,8},{13,10},{15,12},{17,14},{19,... | collective-permute-start | bytes 2359304 | tf_op jit(solution)/shard_map/ppermute | solution.py:323
  67.1 13.2 %collective-permute-start.5 = (bf16[3,128,1024]{2,1,0:T(8,128)(2,1)S(1)}, bf16[3,128,1024]{2,1,0:T(8,128)(2,1)}, u32[]{:S(2)}, u32[]{:S(2)}) collective-permute-start(bf16[3,128,1024]{2,1,0:T(8,128)(2,1)S(1)} %get-tuple-element.65), channel_id=1, source_target_pairs={{0,1},{1,0},{2,3},{3,2},{4,5},{5,4},{6,7},{7,6},{8,9},{9,8},{10,11... | collective-permute-start | bytes 2359304 | tf_op jit(solution)/shard_map/ppermute | solution.py:323
  69.7 6.2 %copy-start.2 = (s32[16384]{0:T(1024)S(1)}, s32[16384]{0:T(1024)}, u32[]{:S(2)}) copy-start(s32[16384]{0:T(1024)} %param.13) | copy-start | bytes 196612
  78.1 15.9 %copy-start.3 = (f32[1,2048]{1,0:T(1,128)S(1)}, f32[1,2048]{1,0:T(1,128)}, u32[]{:S(2)}) copy-start(f32[1,2048]{1,0:T(1,128)} %bitcast_convert_fusion) | copy-start | bytes 24580
  86.5 7.5 %collective-permute-start.6 = (bf16[64,2048]{1,0:T(8,128)(2,1)S(1)}, bf16[64,2048]{1,0:T(8,128)(2,1)S(1)}, u32[]{:S(2)}, u32[]{:S(2)}) collective-permute-start(bf16[64,2048]{1,0:T(8,128)(2,1)S(1)} %pad_maximum_fusion), channel_id=1, source_target_pairs={{0,2},{2,4},{4,6},{6,8},{8,10},{10,12},{12,14},{14,16},{16,18},{18... | collective-permute-start | bytes 786440 | tf_op jit(solution)/shard_map/ppermute | solution.py:323
  94.1 8.7 %collective-permute-start.7 = (bf16[64,2048]{1,0:T(8,128)(2,1)S(1)}, bf16[64,2048]{1,0:T(8,128)(2,1)S(1)}, u32[]{:S(2)}, u32[]{:S(2)}) collective-permute-start(bf16[64,2048]{1,0:T(8,128)(2,1)S(1)} %multiply_convert_fusion.refs_1_), channel_id=1, source_target_pairs={{0,2},{1,3},{2,4},{3,5},{4,6},{5,7},{6,8},{7,9},{8,10},{9,11},{10,... | collective-permute-start | bytes 786440 | tf_op jit(solution)/shard_map/ppermute | solution.py:323
  96.3 16.0 %collective-permute-start.8 = (bf16[64,2048]{1,0:T(8,128)(2,1)S(1)}, bf16[64,2048]{1,0:T(8,128)(2,1)S(1)}, u32[]{:S(2)}, u32[]{:S(2)}) collective-permute-start(bf16[64,2048]{1,0:T(8,128)(2,1)S(1)} %multiply_convert_fusion.refs_1_), channel_id=1, source_target_pairs={{0,30},{1,31},{2,0},{3,1},{4,2},{5,3},{6,4},{7,5},{8,6},{9,7},{10,... | collective-permute-start | bytes 786440 | tf_op jit(solution)/shard_map/ppermute | solution.py:323
  102.9 11.9 %collective-permute-start.9 = (bf16[64,2048]{1,0:T(8,128)(2,1)S(1)}, bf16[64,2048]{1,0:T(8,128)(2,1)S(1)}, u32[]{:S(2)}, u32[]{:S(2)}) collective-permute-start(bf16[64,2048]{1,0:T(8,128)(2,1)S(1)} %collective-permute-done.7.refs_0_), channel_id=1, source_target_pairs={{0,2},{1,3},{2,4},{3,5},{4,6},{5,7},{6,8},{7,9},{8,10},{9,11},{10,... | collective-permute-start | bytes 786440 | tf_op jit(solution)/shard_map/ppermute | solution.py:323
  104.8 13.2 %collective-permute-start.11 = (bf16[64,2048]{1,0:T(8,128)(2,1)S(1)}, bf16[64,2048]{1,0:T(8,128)(2,1)S(1)}, u32[]{:S(2)}, u32[]{:S(2)}) collective-permute-start(bf16[64,2048]{1,0:T(8,128)(2,1)S(1)} %multiply_convert_fusion.refs_1_), channel_id=1, source_target_pairs={{0,1},{1,0},{2,3},{3,2},{4,5},{5,4},{6,7},{7,6},{8,9},{9,8},{10,11... | collective-permute-start | bytes 786440 | tf_op jit(solution)/shard_map/ppermute | solution.py:323
  110.4 7.6 %collective-permute-start.10 = (bf16[64,2048]{1,0:T(8,128)(2,1)S(1)}, bf16[64,2048]{1,0:T(8,128)(2,1)S(1)}, u32[]{:S(2)}, u32[]{:S(2)}) collective-permute-start(bf16[64,2048]{1,0:T(8,128)(2,1)S(1)} %collective-permute-done.7.refs_0_), channel_id=1, source_target_pairs={{0,1},{1,0},{2,3},{3,2},{4,5},{5,4},{6,7},{7,6},{8,9},{9,8},{10,11... | collective-permute-start | bytes 786440 | tf_op jit(solution)/shard_map/ppermute | solution.py:323
  112.3 5.7 %collective-permute-start.12 = (bf16[64,2048]{1,0:T(8,128)(2,1)S(1)}, bf16[64,2048]{1,0:T(8,128)(2,1)S(1)}, u32[]{:S(2)}, u32[]{:S(2)}) collective-permute-start(bf16[64,2048]{1,0:T(8,128)(2,1)S(1)} %collective-permute-done.8.refs_2_), channel_id=1, source_target_pairs={{0,1},{1,0},{2,3},{3,2},{4,5},{5,4},{6,7},{7,6},{8,9},{9,8},{10,11... | collective-permute-start | bytes 786440 | tf_op jit(solution)/shard_map/ppermute | solution.py:323
  114.7 4.3 %collective-permute-start.13 = (bf16[64,2048]{1,0:T(8,128)(2,1)S(1)}, bf16[64,2048]{1,0:T(8,128)(2,1)S(1)}, u32[]{:S(2)}, u32[]{:S(2)}) collective-permute-start(bf16[64,2048]{1,0:T(8,128)(2,1)S(1)} %collective-permute-done.9.refs_3_), channel_id=1, source_target_pairs={{0,1},{1,0},{2,3},{3,2},{4,5},{5,4},{6,7},{7,6},{8,9},{9,8},{10,11... | collective-permute-start | bytes 786440 | tf_op jit(solution)/shard_map/ppermute | solution.py:323
Sparse Core Ops, SparseCore 0:
  37.7 65.7 all-gather.3
